TPU v7x, 32 devices: a whole 2x2x4 slice. The times are simulated.
32 devices in a mesh: slab: 8 (over y, x, core), coil: 4 (over z).
Axes of the slice: x: 2, y: 2, z: 4, core: 2. Of those that a mesh axis runs over, the one named last changes fastest.
Arguments:
- samples: bfloat16 [8, 65536, 128], P('coil', 'slab'), may hold values from -6 to 6
- sample_pos: bfloat16 [65536, 64], P('slab'), may hold values from 0 to 64
- block_count: int32 [65536], P('slab'), may hold values from 16 to 64
- grid_block: int32 [65536], P('slab'), may hold values from 0 to 32767
- block_slab: int32 [65536, 1], P('slab'), may hold values from 0 to 7, as said below
- sensitivity: bfloat16 [8, 256, 16, 512], P(None, 'slab', 'coil'), may hold values from -3 to 3
Outputs:
- image: float32 [256, 16, 512], P('slab', 'coil')
Inputs may be any that keep to these rules, and one draw needn't show every extreme that they name: `block_slab`: within the rows of one device no slab is named more than 2560 times; one slab, the same for every device, is named exactly 2560 times by every device.
All inputs are finite; a program needn't handle non-finite values.
Results may differ from a plain program's by a relative error of at most 0.02.
The roundings to bfloat16 on the way count: a program that leaves them out, or rounds other values in their place, can miss the bound.
Values may be sent and summed in bfloat16 or wider, within the bound.
A program may use at most 128 MiB of HBM per device.

v0:
```python
import functools
import math

import jax
import jax.numpy as jnp
from jax import lax
from jax.experimental import pallas as pl
from jax.experimental.pallas import tpu as pltpu
from jax.sharding import PartitionSpec as P

KX = 256
CELLS = 64
NT = (((1,), (1,)), ((), ()))


def twiddle(first, second, length):
    phase = (first * second % length).astype(jnp.float32) * (2.0 * math.pi / length)
    scale = 1.0 / math.sqrt(length)
    return (jnp.cos(phase) * scale, jnp.sin(phase) * scale)


def ints(count):
    return jnp.arange(count, dtype=jnp.int32)


def across_table(coils, rows_out, x_here):
    x0 = (KX - rows_out) // 2
    cosine, sine = twiddle(x0 + ints(rows_out)[:, None], ints(CELLS)[None, :], KX)
    upper = jnp.stack([cosine, -sine], axis=1)
    lower = jnp.stack([sine, cosine], axis=1)
    eye = jnp.eye(coils, dtype=jnp.float32)
    tables = []
    for one in (jnp.stack([upper, lower], axis=1), jnp.stack([-lower, upper], axis=1)):
        one = one.reshape(rows_out // x_here, 1, x_here, 2, 1, 2, CELLS)
        one = one * eye[None, :, None, None, :, None, None]
        tables.append(one.reshape(2 * coils * rows_out, 2 * coils * CELLS))
    return jnp.concatenate(tables, axis=0).astype(jnp.bfloat16)


def right_table(length):
    cosine, sine = twiddle(ints(length)[:, None], ints(length)[None, :], length)
    upper = jnp.concatenate([cosine, sine], axis=1)
    lower = jnp.concatenate([-sine, cosine], axis=1)
    return jnp.concatenate([upper, lower], axis=0).astype(jnp.bfloat16)


def left_table(length):
    cosine, sine = twiddle(ints(length)[:, None], ints(length)[None, :], length)
    upper = jnp.concatenate([cosine, -sine], axis=1)
    lower = jnp.concatenate([sine, cosine], axis=1)
    return jnp.concatenate([upper, lower], axis=0).astype(jnp.bfloat16)


def grid_kernel(coils, pos_ref, val_ref, seg_ref, x_ref, tab_ref, out_ref, wide, where):
    lanes = wide.shape[2]
    rows = out_ref.shape[0]
    mid = (lax.broadcasted_iota(jnp.int32, (CELLS, lanes), 0).astype(jnp.float32) + 0.5) * 0.4

    @pl.loop(0, pos_ref.shape[1] // lanes)
    def _(at):
        cut = pl.ds(pl.multiple_of(at * lanes, lanes), lanes)
        for c in range(coils):
            wide[c] = val_ref[c, cut, :].astype(jnp.float32).T
        where[...] = pos_ref[:, cut]

        def step(i, sums):
            offset = where[pl.ds(i, 1), :] - mid
            bump = jnp.maximum(1.0 - offset * offset, 0.0)
            weight = (bump * bump).astype(jnp.bfloat16).astype(jnp.float32)
            return tuple(
                sums[n] + weight * wide[n // 2, pl.ds(n % 2 * CELLS + i, 1), :]
                for n in range(2 * coils)
            )

        zero = jnp.zeros((CELLS, lanes), jnp.float32)
        sums = lax.fori_loop(0, CELLS, step, (zero,) * (2 * coils), unroll=16)
        turn = (x_ref[...] * seg_ref[:, cut]) & 3
        cells = jnp.concatenate([part.astype(jnp.bfloat16) for part in sums], axis=0)
        moved = jnp.dot(tab_ref[...], cells, preferred_element_type=jnp.float32)
        turned = jnp.where((turn & 1) == 0, moved[:rows], moved[rows:])
        out_ref[:, cut] = jnp.where(turn >= 2, -turned, turned).astype(jnp.bfloat16)


def sort_kernel(vals_ref, spot_ref, kz_ref, out_ref, spot_out_ref, before, rank):
    rows, group = vals_ref.shape
    depth = before.shape[0]
    piece = math.gcd(128, group)
    pieces = group // piece
    level = lax.broadcasted_iota(jnp.int32, (depth, piece), 0)
    src = lax.broadcasted_iota(jnp.int32, (piece, 2 * piece), 0)
    dst = lax.broadcasted_iota(jnp.int32, (piece, 2 * piece), 1)
    steps = jnp.where((src < dst) | (dst >= piece), 1.0, 0.0).astype(jnp.bfloat16)
    seen = jnp.zeros((depth, piece), jnp.float32)
    for at in range(pieces):
        cut = slice(at * piece, (at + 1) * piece)
        hot = jnp.where(level == kz_ref[:, cut], 1.0, 0.0)
        counts = jnp.dot(hot.astype(jnp.bfloat16), steps, preferred_element_type=jnp.float32)
        before[:, cut] = seen + counts[:, :piece]
        seen = seen + counts[:, piece:]
    high = jnp.floor(seen * (1.0 / 256.0))
    low = seen - 256.0 * high
    here = lax.broadcasted_iota(jnp.int32, (depth, depth), 0)
    under = lax.broadcasted_iota(jnp.int32, (depth, depth), 1)
    lower = jnp.where(under < here, 1.0, 0.0).astype(jnp.bfloat16)
    first = 256.0 * jnp.dot(lower, high.astype(jnp.bfloat16), preferred_element_type=jnp.float32)
    first = first + jnp.dot(lower, low.astype(jnp.bfloat16), preferred_element_type=jnp.float32)
    for at in range(pieces):
        cut = slice(at * piece, (at + 1) * piece)
        found = jnp.where(level == kz_ref[:, cut], before[:, cut] + first, 0.0)
        rank[:, cut] = jnp.sum(found, axis=0, keepdims=True).astype(jnp.int32)

    tile = math.gcd(256, group)
    slot = lax.broadcasted_iota(jnp.int32, (tile, group), 0)
    vals = jnp.concatenate([vals_ref[...], spot_ref[...]], axis=0)

    @pl.loop(0, group // tile)
    def _(at):
        start = pl.multiple_of(at * tile, tile)
        hot = jnp.where(slot == (rank[...] - start), 1.0, 0.0).astype(jnp.bfloat16)
        moved = lax.dot_general(vals, hot, NT, preferred_element_type=jnp.float32)
        moved = moved.astype(jnp.bfloat16)
        out_ref[:, pl.ds(start, tile)] = moved[:rows]
        spot_out_ref[:, pl.ds(start, tile)] = moved[rows:]


def add_kernel(
    chunk, span, lo_ref, more_ref, vals_ref, kz_ref, ky_ref, ytab_ref, ztab_ref, out_ref, total
):
    step = pl.program_id(0)
    rows = vals_ref.shape[1]
    width = vals_ref.shape[2]
    depth, freq = out_ref.shape[1], total.shape[2]
    parts = width // chunk
    spot = lax.broadcasted_iota(jnp.int32, (freq, chunk), 0)
    plane = lax.broadcasted_iota(jnp.int32, (span, chunk), 0)

    @pl.when(step == 0)
    def _():
        total[...] = jnp.zeros_like(total)

    def add(part, start):
        cut = slice(part * chunk, (part + 1) * chunk)
        hot = jnp.where(spot == ky_ref[0, :, cut], 1.0, 0.0).astype(jnp.bfloat16)
        mine = jnp.where(plane == (kz_ref[0, :, cut] - start), 1.0, 0.0).astype(jnp.bfloat16)
        left = []
        for v in range(rows):
            row = vals_ref[0, v : v + 1, cut].astype(jnp.float32)
            row = jnp.broadcast_to(row, (16, chunk)).astype(jnp.bfloat16)
            left.append(mine * jnp.concatenate([row] * (span // 16), axis=0))
        left = jnp.concatenate(left, axis=0)
        moved = lax.dot_general(left, hot, NT, preferred_element_type=jnp.float32)
        for v in range(rows):
            total[v, pl.ds(start, span), :] += moved[v * span : (v + 1) * span]

    for part in range(parts):
        add(part, pl.multiple_of(lo_ref[step * parts + part], 8))

    for part in range(parts):
        first = lo_ref[step * parts + part]

        def again(at, carry):
            add(part, pl.multiple_of(first + at * span, 8))
            return carry

        lax.fori_loop(1, more_ref[step * parts + part], again, 0)

    @pl.when(step == pl.num_programs(0) - 1)
    def _():
        pairs = rows // 2
        for pair in range(pairs):
            both = jnp.concatenate(
                [total[2 * pair, :depth, :], total[2 * pair + 1, :depth, :]], axis=1
            )
            planes = jnp.dot(
                both.astype(jnp.bfloat16), ytab_ref[...], preferred_element_type=jnp.float32
            ).astype(jnp.bfloat16)
            planes = jnp.concatenate([planes[:, :freq], planes[:, freq:]], axis=0)
            image = jnp.dot(ztab_ref[...], planes, preferred_element_type=jnp.float32)
            out_ref[pair, :, :freq] = image[:depth].astype(jnp.bfloat16)
            out_ref[pair, :, freq:] = image[depth:].astype(jnp.bfloat16)


def whole(memory=pltpu.VMEM):
    return pl.BlockSpec(memory_space=memory)


def per_device(samples, sample_pos, block_count, grid_block, block_slab, sensitivity):
    slab_total = lax.axis_size("slab")
    coil_total = lax.axis_size("coil")
    coils = samples.shape[0]
    blocks = samples.shape[1]
    planes = sensitivity.shape[1]
    rows_out = sensitivity.shape[2] * coil_total
    depth = planes * slab_total
    freq = sensitivity.shape[3] // 2
    x_here = rows_out // slab_total
    segments = KX // CELLS

    live = ints(CELLS)[:, None] < block_count[None, :]
    pos = jnp.where(live, sample_pos.T.astype(jnp.float32), 1.0e4) * 0.4
    seg = (grid_block % segments)[None, :]
    kz = block_slab[:, 0] * planes + grid_block // (segments * freq)
    ky = grid_block // segments % freq

    tile = math.gcd(blocks, 1024)
    lanes = math.gcd(tile, 128)
    count = 2 * coils * rows_out
    table = across_table(coils, rows_out, x_here)
    x_at = (ints(count) // (2 * coils * x_here)) * x_here + ints(count) // 2 % x_here
    x_at = jnp.broadcast_to((x_at + (KX - rows_out) // 2)[:, None], (count, lanes))
    lines = pl.pallas_call(
        functools.partial(grid_kernel, coils),
        grid=(blocks // tile,),
        in_specs=[
            pl.BlockSpec((CELLS, tile), lambda b: (0, b)),
            pl.BlockSpec((coils, tile, 2 * CELLS), lambda b: (0, b, 0)),
            pl.BlockSpec((1, tile), lambda b: (0, b)),
            pl.BlockSpec(x_at.shape, lambda b: (0, 0)),
            pl.BlockSpec(table.shape, lambda b: (0, 0)),
        ],
        out_specs=pl.BlockSpec((count, tile), lambda b: (0, b)),
        out_shape=jax.ShapeDtypeStruct((count, blocks), jnp.bfloat16),
        scratch_shapes=[
            pltpu.VMEM((coils, 2 * CELLS, lanes), jnp.float32),
            pltpu.VMEM((CELLS, lanes), jnp.float32),
        ],
        name="grid_x",
    )(pos, samples, seg, x_at, table)

    group = math.gcd(blocks, 2048)
    groups = blocks // group
    spots = jnp.pad(jnp.stack([kz, ky]).astype(jnp.bfloat16), ((0, 14), (0, 0)))
    ordered, spots = pl.pallas_call(
        sort_kernel,
        grid=(groups,),
        in_specs=[
            pl.BlockSpec((count, group), lambda b: (0, b)),
            pl.BlockSpec((16, group), lambda b: (0, b)),
            pl.BlockSpec((1, group), lambda b: (0, b)),
        ],
        out_specs=[
            pl.BlockSpec((count, group), lambda b: (0, b)),
            pl.BlockSpec((16, group), lambda b: (0, b)),
        ],
        out_shape=[
            jax.ShapeDtypeStruct((count, blocks), jnp.bfloat16),
            jax.ShapeDtypeStruct((16, blocks), jnp.bfloat16),
        ],
        scratch_shapes=[
            pltpu.VMEM((depth, group), jnp.float32),
            pltpu.VMEM((1, group), jnp.int32),
        ],
        name="order_kz",
    )(lines, spots, kz[None, :])
    each = 2 * coils * x_here
    tail = jnp.broadcast_to(spots[:2].reshape(1, each, -1), (slab_total, each, 2 * blocks // each))
    sent = lax.all_to_all(
        jnp.concatenate([ordered.reshape(slab_total, each, blocks), tail], axis=2),
        "slab",
        0,
        0,
        tiled=True,
    )
    spots = sent[:, :, blocks:].reshape(slab_total, 2, blocks).astype(jnp.int32)
    kz_all = spots[:, 0:1]
    ky_all = spots[:, 1:2]

    chunk = math.gcd(blocks, 256)
    span = 64
    width = math.gcd(blocks, 1024)
    per_row = blocks // width
    by_chunk = kz_all.reshape(slab_total * blocks // chunk, chunk)
    low = jnp.min(by_chunk, axis=1) // 8 * 8
    high = (jnp.max(by_chunk, axis=1) - low) // span + 1
    ytab, ztab = right_table(freq), left_table(depth)
    pairs = each // 2
    imaged = pl.pallas_call(
        functools.partial(add_kernel, chunk, span),
        grid_spec=pltpu.PrefetchScalarGridSpec(
            num_scalar_prefetch=2,
            grid=(slab_total * per_row,),
            in_specs=[
                pl.BlockSpec((1, each, width), lambda i, a, b: (i // per_row, 0, i % per_row)),
                pl.BlockSpec((1, 1, width), lambda i, a, b: (i // per_row, 0, i % per_row)),
                pl.BlockSpec((1, 1, width), lambda i, a, b: (i // per_row, 0, i % per_row)),
                pl.BlockSpec(ytab.shape, lambda i, a, b: (0, 0)),
                pl.BlockSpec(ztab.shape, lambda i, a, b: (0, 0)),
            ],
            out_specs=pl.BlockSpec((pairs, depth, 2 * freq), lambda i, a, b: (0, 0, 0)),
            scratch_shapes=[pltpu.VMEM((each, depth + span, freq), jnp.float32)],
        ),
        out_shape=jax.ShapeDtypeStruct((pairs, depth, 2 * freq), jnp.bfloat16),
        name="add_yz",
    )(low, high, sent, kz_all, ky_all, ytab, ztab)

    split = imaged.reshape(pairs, slab_total, planes, 2 * freq)
    split = lax.all_to_all(jnp.swapaxes(split, 0, 1), "slab", 0, 0, tiled=True)
    split = split.reshape(slab_total, coils, x_here, planes, 2 * freq)
    split = jnp.transpose(split, (0, 2, 1, 3, 4)).reshape(
        coil_total, rows_out // coil_total, coils, planes, 2 * freq
    )
    split = lax.all_to_all(split, "coil", 0, 0, tiled=True)
    mine = jnp.transpose(split, (0, 2, 3, 1, 4)).reshape(sensitivity.shape).astype(jnp.float32)
    maps = sensitivity.astype(jnp.float32)
    map_re, map_im = maps[..., :freq], maps[..., freq:]
    img_re, img_im = mine[..., :freq], mine[..., freq:]
    real_part = jnp.sum(map_re * img_re + map_im * img_im, axis=0)
    imag_part = jnp.sum(map_re * img_im - map_im * img_re, axis=0)
    return jnp.concatenate([real_part, imag_part], axis=-1)


def solution(mesh):
    return jax.shard_map(
        per_device,
        mesh=mesh,
        in_specs=(
            P("coil", "slab", None),
            P("slab", None),
            P("slab"),
            P("slab"),
            P("slab", None),
            P(None, "slab", "coil", None),
        ),
        out_specs=P("slab", "coil", None),
        check_vma=False,
    )
```

profile of v0, /device:TPU:0, one launch (start us, length us, event | category | flops | bytes accessed | tf_op | source)
XLA Modules:
  0.0 244.2 jit_solution(11712285020338861472)
XLA Ops:
  0.0 0.1 multiply_bitcast_fusion.1
  0.1 0.1 sine_multiply_fusion.1
  0.4 0.2 multiply_convert_fusion.2
  0.5 0.1 mul.385
  0.7 0.1 mul.396
  0.8 0.8 broadcast_multiply_fusion
  1.6 1.4 fusion.14
  3.0 0.0 copy-start.1
  3.0 0.6 pad_maximum_fusion.6.tab_ref
  3.7 2.8 %fusion.pos_ref = f32[64,8192]{1,0:T(8,128)} fusion(bf16[8192,64]{0,1:T(8,128)(2,1)} %param.7, s32[8192]{0:T(1024)} %param.8), kind=kLoop, calls=%fused_computation.1 | loop fusion | flops 2097152 | bytes 3178496 | tf_op jit(solution)/shard_map/mul | solution.py:200
  6.5 0.8 fusion.8.spot_ref
  7.3 0.7 broadcast_in_dim.14.x_ref
  8.0 86.2 %grid_x.1.vals_ref = bf16[64,8192]{1,0:T(8,128)(2,1)} custom-call(f32[64,8192]{1,0:T(8,128)} %fusion.pos_ref, bf16[2,8192,128]{2,1,0:T(8,128)(2,1)} %val_ref.1, s32[1,8192]{1,0:T(1,128)} %bitcast.36, s32[64,128]{1,0:T(8,128)} %broadcast_in_dim.14.x_ref, bf16[128,256]{1,0:T(8,128)(2,1)} %pad_maximum_fusion.6.tab_ref), custom_call_target="tpu_custom_call" | custom-call | tf_op jit(solution)/shard_map/grid_x/pallas_call | solution.py:211
  94.2 0.0 copy-done.1
  94.2 21.2 %order_kz.1 = (bf16[64,8192]{1,0:T(8,128)(2,1)}, bf16[16,8192]{1,0:T(8,128)(2,1)}) custom-call(bf16[64,8192]{1,0:T(8,128)(2,1)} %grid_x.1.vals_ref, bf16[16,8192]{1,0:T(8,128)(2,1)} %fusion.8.spot_ref, s32[1,8192]{1,0:T(1,128)} %bitcast.35), custom_call_target="tpu_custom_call" | custom-call | tf_op jit(solution)/shard_map/order_kz/pallas_call | solution.py:233
  115.4 0.9 slice.25
  116.4 2.4 pad_maximum_fusion
  118.8 5.2 %all-to-all-start = ((bf16[8,8,10240]{2,1,0:T(8,128)(2,1)}), bf16[8,8,10240]{2,1,0:T(8,128)(2,1)S(1)}, u32[]{:S(2)}, u32[]{:S(2)}) async-start(bf16[8,8,10240]{2,1,0:T(8,128)(2,1)} %pad_maximum_fusion), calls=%async_computation | async-start | bytes 2621440 | tf_op jit(solution)/shard_map/all_to_all | solution.py:257
  124.0 1.0 fusion.12
  125.0 1.1 negate_convert_fusion
  126.1 1.0 fusion.2
  127.1 15.0 %all-to-all-done.vals_ref = bf16[8,8,10240]{2,1,0:T(8,128)(2,1)S(1)} async-done(((bf16[8,8,10240]{2,1,0:T(8,128)(2,1)}), bf16[8,8,10240]{2,1,0:T(8,128)(2,1)S(1)}, u32[]{:S(2)}, u32[]{:S(2)}) %all-to-all-start) | async-done | bytes 1310752 | tf_op jit(solution)/shard_map/all_to_all | solution.py:257
  142.2 0.0 copy-start
  142.2 0.1 slice_convert_fusion
  142.2 0.4 reshape.301
  142.6 1.4 fusion.40
  144.1 0.1 fusion.38
  144.3 0.6 fusion.32
  144.9 0.0 copy-done
  144.9 47.4 %add_yz.1 = bf16[4,256,512]{2,1,0:T(8,128)(2,1)} custom-call(s32[256]{0:T(256)} %get-tuple-element.14.lo_ref, s32[256]{0:T(256)} %get-tuple-element.13.more_ref, bf16[8,8,10240]{2,1,0:T(8,128)(2,1)} %copy-done, s32[8,1,8192]{2,1,0:T(1,128)} %get-tuple-element.17.kz_ref, s32[8,1,8192]{2,1,0:T(1,128)} %get-tuple-element.15.ky_ref, ...), custom_call_target="tpu_custom_call" | custom-call | tf_op jit(solution)/shard_map/add_yz/pallas_call | solution.py:277
  192.3 1.3 copy.30
  193.6 17.8 %all_to_all.15 = bf16[8,4,32,512]{3,2,1,0:T(8,128)(2,1)S(1)} all-to-all(bf16[8,4,32,512]{3,2,1,0:T(8,128)(2,1)S(1)} %bitcast.31), channel_id=1, replica_groups=mesh['slab'=8,'coil'=4] {'slab'}, dimensions={0} | all-to-all | bytes 2097152 | tf_op jit(solution)/shard_map/all_to_all | solution.py:297
  211.4 1.0 copy.25
  212.4 4.9 %all-to-all-start.2 = ((bf16[4,4,2,32,512]{4,3,2,1,0:T(8,128)(2,1)}), bf16[4,4,2,32,512]{4,3,2,1,0:T(8,128)(2,1)S(1)}, u32[]{:S(2)}, u32[]{:S(2)}) async-start(bf16[4,4,2,32,512]{4,3,2,1,0:T(8,128)(2,1)} %bitcast.14), calls=%async_computation.2 | async-start | bytes 2097152 | tf_op jit(solution)/shard_map/all_to_all | solution.py:302
  217.3 1.5 copy_convert_fusion
  218.8 23.6 %all-to-all-done.2 = bf16[4,4,2,32,512]{4,3,2,1,0:T(8,128)(2,1)S(1)} async-done(((bf16[4,4,2,32,512]{4,3,2,1,0:T(8,128)(2,1)}), bf16[4,4,2,32,512]{4,3,2,1,0:T(8,128)(2,1)S(1)}, u32[]{:S(2)}, u32[]{:S(2)}) %all-to-all-start.2) | async-done | bytes 1048608 | tf_op jit(solution)/shard_map/all_to_all | solution.py:302
  242.5 0.3 convert_bitcast_fusion
  242.7 0.3 copy.26
  243.0 0.3 add_reduce_fusion
  243.4 0.9 copy.27
  (13 shorter events, 0.2 us)
Async XLA Ops:
  3.0 91.2 %copy-start.1 = (s32[8192]{0:T(1024)}, s32[8192]{0:T(1024)S(1)}, u32[]{:S(2)}) copy-start(s32[8192]{0:T(1024)S(1)} %get-tuple-element.20) | copy-start | bytes 98308
  118.8 23.4 %all-to-all-start = ((bf16[8,8,10240]{2,1,0:T(8,128)(2,1)}), bf16[8,8,10240]{2,1,0:T(8,128)(2,1)S(1)}, u32[]{:S(2)}, u32[]{:S(2)}) async-start(bf16[8,8,10240]{2,1,0:T(8,128)(2,1)} %pad_maximum_fusion), calls=%async_computation | async-start | bytes 2621440 | tf_op jit(solution)/shard_map/all_to_all | solution.py:257
  142.2 2.7 %copy-start = (bf16[8,8,10240]{2,1,0:T(8,128)(2,1)}, bf16[8,8,10240]{2,1,0:T(8,128)(2,1)S(1)}, u32[]{:S(2)}) copy-start(bf16[8,8,10240]{2,1,0:T(8,128)(2,1)S(1)} %all-to-all-done.vals_ref) | copy-start | bytes 3932164
  212.4 30.0 %all-to-all-start.2 = ((bf16[4,4,2,32,512]{4,3,2,1,0:T(8,128)(2,1)}), bf16[4,4,2,32,512]{4,3,2,1,0:T(8,128)(2,1)S(1)}, u32[]{:S(2)}, u32[]{:S(2)}) async-start(bf16[4,4,2,32,512]{4,3,2,1,0:T(8,128)(2,1)} %bitcast.14), calls=%async_computation.2 | async-start | bytes 2097152 | tf_op jit(solution)/shard_map/all_to_all | solution.py:302
where the time goes:
time: 248 us; the launch traced here: 244 us
  Pallas kernels  155 us (62%)
  waiting for transfers between devices  38.7 us (16%)
  blocking collectives  17.8 us (7%)
  other arithmetic  15.4 us (6%)
  starting transfers between devices  10.1 us (4%)
  local copies, waits for them, and re-layouts  7.29 us (3%)
    pallas_call x1, Pallas kernels, per_device(): pl.pallas_call(functools.partial(grid_kernel, coils), grid=(blocks // til...  86.2 us
    pallas_call x1, Pallas kernels, per_device(): pl.pallas_call(functools.partial(add_kernel, chunk, span), grid_spec=pltp...  47.4 us
    all_to_all x1, waiting for transfers between devices, per_device(): split = lax.all_to_all(split, 'coil', 0, 0, tiled=True)  23.6 us
    pallas_call x1, Pallas kernels, per_device(): pl.pallas_call(sort_kernel, grid=(groups,), in_specs=[pl.BlockSpec((count...  21.2 us
    all_to_all x1, blocking collectives, per_device(): split = lax.all_to_all(jnp.swapaxes(split, 0, 1), 'slab', 0, 0, tiled=True)  17.8 us
    all_to_all x1, waiting for transfers between devices, per_device(): lax.all_to_all(jnp.concatenate([ordered.reshape(slab_total, each, blocks)...  15 us
    all_to_all x1, starting transfers between devices, per_device(): lax.all_to_all(jnp.concatenate([ordered.reshape(slab_total, each, blocks)...  5.2 us
  transfers between devices with their start and end apart: 2, of which 2 were waited for; matrix products, arithmetic and copies ran while one was open for 2% of the time, Pallas kernels for 0%

commit v1 on v0

--- a/solution.py
+++ b/solution.py
@@ -10,6 +10,7 @@
 
 KX = 256
 CELLS = 64
+CLASSES = 8
 NT = (((1,), (1,)), ((), ()))
 
 
@@ -51,34 +52,77 @@
     return jnp.concatenate([upper, lower], axis=0).astype(jnp.bfloat16)
 
 
-def grid_kernel(coils, pos_ref, val_ref, seg_ref, x_ref, tab_ref, out_ref, wide, where):
-    lanes = wide.shape[2]
-    rows = out_ref.shape[0]
-    mid = (lax.broadcasted_iota(jnp.int32, (CELLS, lanes), 0).astype(jnp.float32) + 0.5) * 0.4
-
-    @pl.loop(0, pos_ref.shape[1] // lanes)
-    def _(at):
-        cut = pl.ds(pl.multiple_of(at * lanes, lanes), lanes)
+def spread_table(table, values):
+    at = ints(2 * CELLS) % CELLS
+    cell = CLASSES * (at % CLASSES) + at // CLASSES
+    table = table.reshape(table.shape[0], values, CELLS)[:, :, cell]
+    return table.reshape(table.shape[0], values * 2 * CELLS)
+
+
+def grid_kernel(
+    coils, unroll, pos_ref, val_ref, seg_ref, x_ref, tab_ref, out_ref, cells, near, bump
+):
+    rows, tile = out_ref.shape
+    block = lax.broadcasted_iota(jnp.int32, (16, 2 * CELLS), 0)
+    upper = lax.broadcasted_iota(jnp.int32, (16, 2 * CELLS), 1) >= CELLS
+    odd = block % 2 == 1
+    own = [block % 4 // 2 == half for half in range(2)]
+    mine = block // 4 % 2 == upper.astype(jnp.int32)
+    level = lax.broadcasted_iota(jnp.int32, (CLASSES, 2 * CELLS), 0).astype(jnp.float32)
+
+    def step(g, slot):
+        at = pl.ds(pl.multiple_of(g * 16, 16), 16)
+        left = []
         for c in range(coils):
-            wide[c] = val_ref[c, cut, :].astype(jnp.float32).T
-        where[...] = pos_ref[:, cut]
-
-        def step(i, sums):
-            offset = where[pl.ds(i, 1), :] - mid
-            bump = jnp.maximum(1.0 - offset * offset, 0.0)
-            weight = (bump * bump).astype(jnp.bfloat16).astype(jnp.float32)
-            return tuple(
-                sums[n] + weight * wide[n // 2, pl.ds(n % 2 * CELLS + i, 1), :]
-                for n in range(2 * coils)
-            )
-
-        zero = jnp.zeros((CELLS, lanes), jnp.float32)
-        sums = lax.fori_loop(0, CELLS, step, (zero,) * (2 * coils), unroll=16)
-        turn = (x_ref[...] * seg_ref[:, cut]) & 3
-        cells = jnp.concatenate([part.astype(jnp.bfloat16) for part in sums], axis=0)
-        moved = jnp.dot(tab_ref[...], cells, preferred_element_type=jnp.float32)
-        turned = jnp.where((turn & 1) == 0, moved[:rows], moved[rows:])
-        out_ref[:, cut] = jnp.where(turn >= 2, -turned, turned).astype(jnp.bfloat16)
+            straight = val_ref[c, at, :].astype(jnp.float32)
+            turned = pltpu.roll(straight, CELLS, 1)
+            for low, high in ((straight, turned), (turned, straight)):
+                placed = jnp.where(
+                    odd, jnp.where(upper, high, 0.0), jnp.where(upper, 0.0, low)
+                )
+                halves = [jnp.where(own[half], placed, 0.0) for half in range(2)]
+                left.append(jnp.concatenate(halves, axis=1).astype(jnp.bfloat16))
+        place = pos_ref[pl.ds(pl.multiple_of(g * 8, 8), 8), :].astype(jnp.float32) * 0.125
+        for r in range(CLASSES):
+            offset = place - ((r + 0.5) * 0.125 - 0.5)
+            seat = jnp.floor(offset)
+            offset = (offset - seat) * 3.2 - 1.6
+            rise = jnp.maximum(1.0 - offset * offset, 0.0)
+            near[slot, r] = seat
+            bump[slot, r] = rise * rise
+        right = []
+        for quad in range(4):
+            halves = []
+            for half in range(2):
+                row = pl.ds(2 * quad + half, 1)
+                parts = []
+                for r in range(CLASSES):
+                    seat = jnp.broadcast_to(near[slot, r, row, :], level.shape)
+                    high = jnp.broadcast_to(bump[slot, r, row, :], level.shape)
+                    parts.append(jnp.where(level == seat, high, 0.0))
+                halves.append(jnp.concatenate(parts, axis=0).astype(jnp.bfloat16))
+            right.append(jnp.concatenate(halves, axis=1))
+        done = lax.dot_general(
+            jnp.concatenate(left, axis=0),
+            jnp.concatenate(right, axis=0),
+            NT,
+            preferred_element_type=jnp.float32,
+        )
+        for v in range(2 * coils):
+            first = done[16 * v : 16 * v + 8, : 2 * CELLS]
+            second = done[16 * v + 8 : 16 * v + 16, 2 * CELLS :]
+            both = jnp.where(mine, jnp.concatenate([first, second], axis=0), 0.0)
+            cells[at, 2 * CELLS * v : 2 * CELLS * (v + 1)] = both.astype(jnp.bfloat16)
+
+    @pl.loop(0, tile // (16 * unroll))
+    def _(outer):
+        for slot in range(unroll):
+            step(outer * unroll + slot, slot)
+
+    moved = lax.dot_general(tab_ref[...], cells[...], NT, preferred_element_type=jnp.float32)
+    turn = (x_ref[...] * seg_ref[...]) & 3
+    turned = jnp.where((turn & 1) == 0, moved[:rows], moved[rows:])
+    out_ref[...] = jnp.where(turn >= 2, -turned, turned).astype(jnp.bfloat16)
 
 
 def sort_kernel(vals_ref, spot_ref, kz_ref, out_ref, spot_out_ref, before, rank):
@@ -196,23 +240,23 @@
     x_here = rows_out // slab_total
     segments = KX // CELLS
 
-    live = ints(CELLS)[:, None] < block_count[None, :]
-    pos = jnp.where(live, sample_pos.T.astype(jnp.float32), 1.0e4) * 0.4
+    live = ints(CELLS)[None, :] < block_count[:, None]
+    pos = jnp.where(live, sample_pos, 9984.0).reshape(blocks // 2, 2 * CELLS)
     seg = (grid_block % segments)[None, :]
     kz = block_slab[:, 0] * planes + grid_block // (segments * freq)
     ky = grid_block // segments % freq
 
     tile = math.gcd(blocks, 1024)
-    lanes = math.gcd(tile, 128)
+    unroll = math.gcd(tile // 16, 16)
     count = 2 * coils * rows_out
-    table = across_table(coils, rows_out, x_here)
+    table = spread_table(across_table(coils, rows_out, x_here), 2 * coils)
     x_at = (ints(count) // (2 * coils * x_here)) * x_here + ints(count) // 2 % x_here
-    x_at = jnp.broadcast_to((x_at + (KX - rows_out) // 2)[:, None], (count, lanes))
+    x_at = jnp.broadcast_to((x_at + (KX - rows_out) // 2)[:, None], (count, tile))
     lines = pl.pallas_call(
-        functools.partial(grid_kernel, coils),
+        functools.partial(grid_kernel, coils, unroll),
         grid=(blocks // tile,),
         in_specs=[
-            pl.BlockSpec((CELLS, tile), lambda b: (0, b)),
+            pl.BlockSpec((tile // 2, 2 * CELLS), lambda b: (b, 0)),
             pl.BlockSpec((coils, tile, 2 * CELLS), lambda b: (0, b, 0)),
             pl.BlockSpec((1, tile), lambda b: (0, b)),
             pl.BlockSpec(x_at.shape, lambda b: (0, 0)),
@@ -221,8 +265,9 @@
         out_specs=pl.BlockSpec((count, tile), lambda b: (0, b)),
         out_shape=jax.ShapeDtypeStruct((count, blocks), jnp.bfloat16),
         scratch_shapes=[
-            pltpu.VMEM((coils, 2 * CELLS, lanes), jnp.float32),
-            pltpu.VMEM((CELLS, lanes), jnp.float32),
+            pltpu.VMEM((tile, 4 * coils * CELLS), jnp.bfloat16),
+            pltpu.VMEM((unroll, CLASSES, 8, 2 * CELLS), jnp.float32),
+            pltpu.VMEM((unroll, CLASSES, 8, 2 * CELLS), jnp.float32),
         ],
         name="grid_x",
     )(pos, samples, seg, x_at, table)

time: 248 us -> 202 us (0.81); the launches traced: 244 us -> 201 us
  Pallas kernels: 155 us -> 112 us
  local copies, waits for them, and re-layouts: 7.29 us -> 12.1 us
  other arithmetic: 15.4 us -> 10.7 us
    pallas_call x1, Pallas kernels: 86.2 us -> 38.4 us  [per_device(): pl.pallas_call(functools.partial(grid_kernel, coils, unroll), grid=(block...]
    pallas_call x1, Pallas kernels: 47.4 us -> 52.2 us  [per_device(): pl.pallas_call(functools.partial(add_kernel, chunk, span), grid_spec=pltp...]
    mul x1 -> x0, other arithmetic: 2.84 us -> none  [per_device(): pos = jnp.where(live, sample_pos.T.astype(jnp.float32), 10000.0) * 0.4]
where the time goes in v1:
time: 202 us; the launch traced here: 201 us
  Pallas kernels  112 us (55%)
  waiting for transfers between devices  38.6 us (19%)
  blocking collectives  17.8 us (9%)
  local copies, waits for them, and re-layouts  12.1 us (6%)
  other arithmetic  10.7 us (5%)
  starting transfers between devices  10.1 us (5%)
    pallas_call x1, Pallas kernels, per_device(): pl.pallas_call(functools.partial(add_kernel, chunk, span), grid_spec=pltp...  52.2 us
    pallas_call x1, Pallas kernels, per_device(): pl.pallas_call(functools.partial(grid_kernel, coils, unroll), grid=(block...  38.4 us
    all_to_all x1, waiting for transfers between devices, per_device(): split = lax.all_to_all(split, 'coil', 0, 0, tiled=True)  23.6 us
    pallas_call x1, Pallas kernels, per_device(): pl.pallas_call(sort_kernel, grid=(groups,), in_specs=[pl.BlockSpec((count...  21.2 us
    all_to_all x1, blocking collectives, per_device(): split = lax.all_to_all(jnp.swapaxes(split, 0, 1), 'slab', 0, 0, tiled=True)  17.8 us
    all_to_all x1, waiting for transfers between devices, per_device(): lax.all_to_all(jnp.concatenate([ordered.reshape(slab_total, each, blocks)...  15 us
    all_to_all x1, starting transfers between devices, per_device(): lax.all_to_all(jnp.concatenate([ordered.reshape(slab_total, each, blocks)...  5.22 us
    all_to_all x1, starting transfers between devices, per_device(): split = lax.all_to_all(split, 'coil', 0, 0, tiled=True)  4.86 us
  transfers between devices with their start and end apart: 2, of which 2 were waited for; matrix products, arithmetic and copies ran while one was open for 2% of the time, Pallas kernels for 0%

profile of v1, /device:TPU:0, one launch (start us, length us, event | category | flops | bytes accessed | tf_op | source)
XLA Modules:
  0.0 201.4 jit_solution(7163786433205598746)
XLA Ops:
  0.0 0.0 copy-start.4
  0.0 0.0 copy-start.1
  0.0 0.0 copy-start.3
  0.0 0.1 multiply_bitcast_fusion.1
  0.1 0.1 sine_multiply_fusion.1
  0.4 0.1 copy.25
  0.6 0.1 copy.27
  0.7 0.1 mul.395
  0.8 0.1 mul.396
  1.0 0.1 pad_maximum_fusion.6
  1.1 0.7 gather_fusion
  1.9 0.1 copy.28
  2.0 0.7 copy.38
  2.7 0.0 copy-done.4
  2.7 0.0 copy-done.1
  2.7 0.0 copy-done.3
  2.7 0.2 fusion
  3.0 1.1 copy.23
  4.1 0.0 copy-start.5
  4.1 1.8 reshape.408.pos_ref
  5.9 0.0 copy-done.5
  5.9 0.7 fusion.14
  6.5 0.0 copy-start.2
  6.6 0.8 fusion.8.spot_ref
  7.4 0.8 broadcast_in_dim.14.x_ref
  8.2 38.4 %grid_x.1.vals_ref = bf16[64,8192]{1,0:T(8,128)(2,1)} custom-call(bf16[4096,128]{1,0:T(8,128)(2,1)} %reshape.408.pos_ref, bf16[2,8192,128]{2,1,0:T(8,128)(2,1)} %val_ref.1, s32[1,8192]{1,0:T(1,128)} %bitcast.46, s32[64,1024]{1,0:T(8,128)} %broadcast_in_dim.14.x_ref, bf16[128,512]{1,0:T(8,128)(2,1)} %bitcast.39), custom_call_target="tpu_custom_call" | custom-call | tf_op jit(solution)/shard_map/grid_x/pallas_call | solution.py:255
  46.6 0.0 copy-done.2
  46.6 21.2 %order_kz.1 = (bf16[64,8192]{1,0:T(8,128)(2,1)}, bf16[16,8192]{1,0:T(8,128)(2,1)}) custom-call(bf16[64,8192]{1,0:T(8,128)(2,1)} %grid_x.1.vals_ref, bf16[16,8192]{1,0:T(8,128)(2,1)} %fusion.8.spot_ref, s32[1,8192]{1,0:T(1,128)} %bitcast.45), custom_call_target="tpu_custom_call" | custom-call | tf_op jit(solution)/shard_map/order_kz/pallas_call | solution.py:278
  67.8 0.9 slice.25
  68.8 2.4 %pad_maximum_fusion = bf16[8,8,10240]{2,1,0:T(8,128)(2,1)} fusion(bf16[8,8,2048]{2,1,0:T(8,128)(2,1)S(1)} %broadcast_in_dim.16, bf16[8,8,8192]{2,1,0:T(8,128)(2,1)} %bitcast.38), kind=kLoop, calls=%fused_computation.4 | loop fusion | flops 2621440 | bytes 2621440 | tf_op jit(solution)/shard_map/concatenate | solution.py:303
  71.2 5.2 %all-to-all-start = ((bf16[8,8,10240]{2,1,0:T(8,128)(2,1)}), bf16[8,8,10240]{2,1,0:T(8,128)(2,1)S(1)}, u32[]{:S(2)}, u32[]{:S(2)}) async-start(bf16[8,8,10240]{2,1,0:T(8,128)(2,1)} %pad_maximum_fusion), calls=%async_computation | async-start | bytes 2621440 | tf_op jit(solution)/shard_map/all_to_all | solution.py:302
  76.4 1.0 fusion.12
  77.4 1.1 negate_convert_fusion
  78.5 1.1 fusion.2
  79.6 15.0 %all-to-all-done.vals_ref = bf16[8,8,10240]{2,1,0:T(8,128)(2,1)S(1)} async-done(((bf16[8,8,10240]{2,1,0:T(8,128)(2,1)}), bf16[8,8,10240]{2,1,0:T(8,128)(2,1)S(1)}, u32[]{:S(2)}, u32[]{:S(2)}) %all-to-all-start) | async-done | bytes 1310752 | tf_op jit(solution)/shard_map/all_to_all | solution.py:302
  94.6 0.0 copy-start
  94.6 0.1 slice_convert_fusion
  94.6 0.4 reshape.415
  95.1 1.4 fusion.43
  96.5 0.1 fusion.41
  96.7 0.6 fusion.32
  97.3 0.0 copy-done
  97.3 52.2 %add_yz.1 = bf16[4,256,512]{2,1,0:T(8,128)(2,1)} custom-call(s32[256]{0:T(256)} %get-tuple-element.14.lo_ref, s32[256]{0:T(256)} %get-tuple-element.13.more_ref, bf16[8,8,10240]{2,1,0:T(8,128)(2,1)} %copy-done, s32[8,1,8192]{2,1,0:T(1,128)} %get-tuple-element.17.kz_ref, s32[8,1,8192]{2,1,0:T(1,128)} %get-tuple-element.15.ky_ref, ...), custom_call_target="tpu_custom_call" | custom-call | tf_op jit(solution)/shard_map/add_yz/pallas_call | solution.py:322
  149.5 1.3 copy.37
  150.8 17.8 %all_to_all.15 = bf16[8,4,32,512]{3,2,1,0:T(8,128)(2,1)S(1)} all-to-all(bf16[8,4,32,512]{3,2,1,0:T(8,128)(2,1)S(1)} %bitcast.36), channel_id=1, replica_groups=mesh['slab'=8,'coil'=4] {'slab'}, dimensions={0} | all-to-all | bytes 2097152 | tf_op jit(solution)/shard_map/all_to_all | solution.py:342
  168.5 1.0 copy.30
  169.6 4.9 %all-to-all-start.2 = ((bf16[4,4,2,32,512]{4,3,2,1,0:T(8,128)(2,1)}), bf16[4,4,2,32,512]{4,3,2,1,0:T(8,128)(2,1)S(1)}, u32[]{:S(2)}, u32[]{:S(2)}) async-start(bf16[4,4,2,32,512]{4,3,2,1,0:T(8,128)(2,1)} %bitcast.16), calls=%async_computation.2 | async-start | bytes 2097152 | tf_op jit(solution)/shard_map/all_to_all | solution.py:347
  174.4 1.5 copy_convert_fusion
  176.0 23.6 %all-to-all-done.2 = bf16[4,4,2,32,512]{4,3,2,1,0:T(8,128)(2,1)S(1)} async-done(((bf16[4,4,2,32,512]{4,3,2,1,0:T(8,128)(2,1)}), bf16[4,4,2,32,512]{4,3,2,1,0:T(8,128)(2,1)S(1)}, u32[]{:S(2)}, u32[]{:S(2)}) %all-to-all-start.2) | async-done | bytes 1048608 | tf_op jit(solution)/shard_map/all_to_all | solution.py:347
  199.6 0.3 convert_bitcast_fusion
  199.9 0.3 copy.31
  200.2 0.3 add_reduce_fusion
  200.5 0.9 copy.32
  (19 shorter events, 0.4 us)
Async XLA Ops:
  0.0 2.7 %copy-start.4 = (s32[8192,1]{0,1:T(1,128)S(1)}, s32[8192,1]{0,1:T(1,128)}, u32[]{:S(2)}) copy-start(s32[8192,1]{0,1:T(1,128)} %param.10) | copy-start | bytes 98308
  0.0 2.7 %copy-start.1 = (bf16[8192,64]{0,1:T(8,128)(2,1)S(1)}, bf16[8192,64]{0,1:T(8,128)(2,1)}, u32[]{:S(2)}) copy-start(bf16[8192,64]{0,1:T(8,128)(2,1)} %param.7) | copy-start | bytes 3145732
  0.0 2.7 %copy-start.3 = (s32[8192]{0:T(1024)S(1)}, s32[8192]{0:T(1024)}, u32[]{:S(2)}) copy-start(s32[8192]{0:T(1024)} %param.8) | copy-start | bytes 98308
  4.1 1.8 copy-start.5
  6.5 40.1 %copy-start.2 = (s32[8192]{0:T(1024)}, s32[8192]{0:T(1024)S(1)}, u32[]{:S(2)}) copy-start(s32[8192]{0:T(1024)S(1)} %get-tuple-element.20) | copy-start | bytes 98308
  71.2 23.4 %all-to-all-start = ((bf16[8,8,10240]{2,1,0:T(8,128)(2,1)}), bf16[8,8,10240]{2,1,0:T(8,128)(2,1)S(1)}, u32[]{:S(2)}, u32[]{:S(2)}) async-start(bf16[8,8,10240]{2,1,0:T(8,128)(2,1)} %pad_maximum_fusion), calls=%async_computation | async-start | bytes 2621440 | tf_op jit(solution)/shard_map/all_to_all | solution.py:302
  94.6 2.7 %copy-start = (bf16[8,8,10240]{2,1,0:T(8,128)(2,1)}, bf16[8,8,10240]{2,1,0:T(8,128)(2,1)S(1)}, u32[]{:S(2)}) copy-start(bf16[8,8,10240]{2,1,0:T(8,128)(2,1)S(1)} %all-to-all-done.vals_ref) | copy-start | bytes 3932164
  169.6 30.0 %all-to-all-start.2 = ((bf16[4,4,2,32,512]{4,3,2,1,0:T(8,128)(2,1)}), bf16[4,4,2,32,512]{4,3,2,1,0:T(8,128)(2,1)S(1)}, u32[]{:S(2)}, u32[]{:S(2)}) async-start(bf16[4,4,2,32,512]{4,3,2,1,0:T(8,128)(2,1)} %bitcast.16), calls=%async_computation.2 | async-start | bytes 2097152 | tf_op jit(solution)/shard_map/all_to_all | solution.py:347

commit v2 on v1

v2 whole, which is shorter than its diff:
```python
import functools
import math

import jax
import jax.numpy as jnp
from jax import lax
from jax.experimental import pallas as pl
from jax.experimental.pallas import tpu as pltpu
from jax.sharding import PartitionSpec as P

KX = 256
CELLS = 64
CLASSES = 8
LANES = 128
RUNS = 4
NT = (((1,), (1,)), ((), ()))


def twiddle(first, second, length):
    phase = (first * second % length).astype(jnp.float32) * (2.0 * math.pi / length)
    scale = 1.0 / math.sqrt(length)
    return (jnp.cos(phase) * scale, jnp.sin(phase) * scale)


def ints(count):
    return jnp.arange(count, dtype=jnp.int32)


def across_table(coils, rows_out, x_here):
    x0 = (KX - rows_out) // 2
    cosine, sine = twiddle(x0 + ints(rows_out)[:, None], ints(CELLS)[None, :], KX)
    upper = jnp.stack([cosine, -sine], axis=1)
    lower = jnp.stack([sine, cosine], axis=1)
    eye = jnp.eye(coils, dtype=jnp.float32)
    tables = []
    for one in (jnp.stack([upper, lower], axis=1), jnp.stack([-lower, upper], axis=1)):
        one = one.reshape(rows_out // x_here, 1, x_here, 2, 1, 2, CELLS)
        one = one * eye[None, :, None, None, :, None, None]
        tables.append(one.reshape(2 * coils * rows_out, 2 * coils * CELLS))
    return jnp.concatenate(tables, axis=0).astype(jnp.bfloat16)


def right_table(length):
    cosine, sine = twiddle(ints(length)[:, None], ints(length)[None, :], length)
    upper = jnp.concatenate([cosine, sine], axis=1)
    lower = jnp.concatenate([-sine, cosine], axis=1)
    return jnp.concatenate([upper, lower], axis=0).astype(jnp.bfloat16)


def left_table(length):
    cosine, sine = twiddle(ints(length)[:, None], ints(length)[None, :], length)
    upper = jnp.concatenate([cosine, -sine], axis=1)
    lower = jnp.concatenate([sine, cosine], axis=1)
    return jnp.concatenate([upper, lower], axis=0).astype(jnp.bfloat16)


def spread_table(table, values):
    at = ints(2 * CELLS) % CELLS
    cell = CLASSES * (at % CLASSES) + at // CLASSES
    table = table.reshape(table.shape[0], values, CELLS)[:, :, cell]
    return table.reshape(table.shape[0], values * 2 * CELLS)


def hot_rows(spots, depth):
    level = lax.broadcasted_iota(jnp.int32, (16, spots.shape[1]), 0).astype(jnp.float32)
    spots = jnp.broadcast_to(spots, (16, spots.shape[1])).astype(jnp.bfloat16)
    one, none = jnp.bfloat16(1), jnp.bfloat16(0)
    return jnp.concatenate(
        [
            jnp.where((level + at).astype(jnp.bfloat16) == spots, one, none)
            for at in range(0, depth, 16)
        ],
        axis=0,
    )


def permute(values, spots):
    depth = spots.shape[1]
    level = lax.broadcasted_iota(jnp.int32, (depth, depth), 0).astype(jnp.float32)
    hot = jnp.where(level == spots, 1.0, 0.0).astype(jnp.bfloat16)
    return lax.dot_general(values, hot, NT, preferred_element_type=jnp.float32)


def regroup(runs):
    count = len(runs)
    rows, length = runs[0].shape
    wide = LANES // count
    place = lax.broadcasted_iota(jnp.int32, (rows, LANES), 1) // wide
    for at in range(length // wide):
        cut = slice(at // count * LANES, at // count * LANES + LANES)
        out = runs[0][:, cut]
        for run in range(1, count):
            out = jnp.where(place == (at + run) % count, runs[run][:, cut], out)
        yield at, out


def order_kernel(planes, freq, kz_ref, ky_ref, spot_ref, sorted_ref):
    tile = kz_ref.shape[1]
    length = tile // RUNS
    wide = LANES // RUNS
    pieces = length // LANES
    runs = []
    for run in range(RUNS):
        cut = slice(run * length, (run + 1) * length)
        kz, ky = kz_ref[:, cut], ky_ref[:, cut]
        lane = lax.broadcasted_iota(jnp.int32, (1, length), 1).astype(jnp.float32)
        key = kz * float(length) + lane
        rank = jnp.zeros((1, length), jnp.float32)
        for piece in range(pieces):
            part = key[:, piece * LANES : (piece + 1) * LANES]
            part = jnp.broadcast_to(part, (LANES, LANES)).T
            part = jnp.concatenate([part] * pieces, axis=1)
            rank = rank + jnp.sum(jnp.where(part < key, 1.0, 0.0), axis=0, keepdims=True)
        rank = rank.astype(jnp.int32)
        seat = rank // wide
        spot = (seat // RUNS) * LANES + (seat + run) % RUNS * wide + rank % wide
        spot = spot.astype(jnp.float32)
        spot_ref[:, cut] = spot
        both = jnp.concatenate([kz, ky, jnp.zeros((14, length), jnp.float32)], axis=0)
        runs.append(permute(both.astype(jnp.bfloat16), spot))
    for at, out in regroup(runs):
        sorted_ref[0, :, at * LANES : (at + 1) * LANES] = out[:2]


def grid_kernel(
    coils, unroll, pos_ref, val_ref, seg_ref, x_ref, tab_ref, spot_ref, out_ref,
    cells, near, bump, placed,
):
    slabs, _, each, tile = out_ref.shape
    rows = slabs * each
    length = tile // RUNS
    block = lax.broadcasted_iota(jnp.int32, (16, LANES), 0)
    upper = lax.broadcasted_iota(jnp.int32, (16, LANES), 1) >= CELLS
    odd = block % 2 == 1
    own = [block % 4 // 2 == half for half in range(2)]
    mine = block // 4 % 2 == upper.astype(jnp.int32)
    level = lax.broadcasted_iota(jnp.int32, (CLASSES, LANES), 0).astype(jnp.float32)

    def step(g, slot):
        at = pl.ds(pl.multiple_of(g * 16, 16), 16)
        left = []
        for c in range(coils):
            straight = val_ref[c, at, :].astype(jnp.float32)
            turned = pltpu.roll(straight, CELLS, 1)
            for low, high in ((straight, turned), (turned, straight)):
                placed_here = jnp.where(
                    odd, jnp.where(upper, high, 0.0), jnp.where(upper, 0.0, low)
                )
                halves = [jnp.where(own[half], placed_here, 0.0) for half in range(2)]
                left.append(jnp.concatenate(halves, axis=1).astype(jnp.bfloat16))
        place = pos_ref[pl.ds(pl.multiple_of(g * 8, 8), 8), :].astype(jnp.float32) * 0.125
        for r in range(CLASSES):
            offset = place - ((r + 0.5) * 0.125 - 0.5)
            seat = jnp.floor(offset)
            offset = (offset - seat) * 3.2 - 1.6
            rise = jnp.maximum(1.0 - offset * offset, 0.0)
            near[slot, r] = seat
            bump[slot, r] = rise * rise
        right = []
        for quad in range(4):
            halves = []
            for half in range(2):
                row = pl.ds(2 * quad + half, 1)
                parts = []
                for r in range(CLASSES):
                    seat = jnp.broadcast_to(near[slot, r, row, :], level.shape)
                    high = jnp.broadcast_to(bump[slot, r, row, :], level.shape)
                    parts.append(jnp.where(level == seat, high, 0.0))
                halves.append(jnp.concatenate(parts, axis=0).astype(jnp.bfloat16))
            right.append(jnp.concatenate(halves, axis=1))
        done = lax.dot_general(
            jnp.concatenate(left, axis=0),
            jnp.concatenate(right, axis=0),
            NT,
            preferred_element_type=jnp.float32,
        )
        for v in range(2 * coils):
            first = done[16 * v : 16 * v + 8, :LANES]
            second = done[16 * v + 8 : 16 * v + 16, LANES:]
            both = jnp.where(mine, jnp.concatenate([first, second], axis=0), 0.0)
            cells[at, LANES * v : LANES * (v + 1)] = both.astype(jnp.bfloat16)

    @pl.loop(0, tile // (16 * unroll))
    def _(outer):
        for slot in range(unroll):
            step(outer * unroll + slot, slot)

    for run in range(RUNS):
        cut = slice(run * length, (run + 1) * length)
        moved = lax.dot_general(
            tab_ref[...], cells[cut, :], NT, preferred_element_type=jnp.float32
        )
        turn = (x_ref[...] * seg_ref[:, cut]) & 3
        turned = jnp.where((turn & 1) == 0, moved[:rows], moved[rows:])
        turned = jnp.where(turn >= 2, -turned, turned).astype(jnp.bfloat16)
        placed[run] = permute(turned, spot_ref[:, cut]).astype(jnp.bfloat16)
    for at, out in regroup([placed.at[run] for run in range(RUNS)]):
        for slab in range(slabs):
            out_ref[slab, 0, :, at * LANES : (at + 1) * LANES] = out[
                slab * each : (slab + 1) * each
            ]


def add_kernel(
    span, per, lo_ref, more_ref, vals_ref, spot_ref, ytab_ref, ztab_ref, out_ref, total
):
    step = pl.program_id(0)
    tiles, rows = vals_ref.shape[1], vals_ref.shape[2]
    pairs, depth, freq = out_ref.shape[0], out_ref.shape[1], out_ref.shape[2] // 2
    deep = 16 // rows
    width = tiles * LANES
    inner = (lax.broadcasted_iota(jnp.int32, (16, width), 0) // rows).astype(jnp.float32)

    @pl.when(step == 0)
    def _():
        total[...] = jnp.zeros_like(total)

    def add(part, start):
        cut = slice(part * LANES, (part + 1) * LANES)
        across = [vals_ref[0, t, :, cut] for t in range(tiles)]
        vals = jnp.concatenate([jnp.concatenate(across, axis=1)] * deep, axis=0)
        kz = jnp.concatenate([spot_ref[0, t, 0:1, cut] for t in range(tiles)], axis=1)
        ky = jnp.concatenate([spot_ref[0, t, 1:2, cut] for t in range(tiles)], axis=1)
        base = jnp.full((16, width), start, jnp.int32).astype(jnp.float32)
        plane = (jnp.broadcast_to(kz, (16, width)) - base - inner).astype(jnp.bfloat16)
        left = [
            jnp.where(plane == jnp.bfloat16(at), vals, jnp.bfloat16(0))
            for at in range(0, span, deep)
        ]
        moved = lax.dot_general(
            jnp.concatenate(left, axis=0),
            hot_rows(ky, freq),
            NT,
            preferred_element_type=jnp.float32,
        )
        at = pl.ds(pl.multiple_of(start * rows, 8), span * rows)
        for half in range(freq // LANES):
            total[half, at, :] += moved[:, half * LANES : (half + 1) * LANES]

    for part in range(per):
        add(part, lo_ref[step * per + part])

    for part in range(per):
        first = lo_ref[step * per + part]

        def again(at, carry):
            add(part, first + at * span)
            return carry

        lax.fori_loop(1, more_ref[step * per + part], again, 0)

    @pl.when(step == pl.num_programs(0) - 1)
    def _():
        for pair in range(pairs):
            both = jnp.concatenate(
                [
                    total[half, pl.ds(2 * pair + part, depth, stride=rows), :]
                    for part in range(2)
                    for half in range(freq // LANES)
                ],
                axis=1,
            )
            planes = jnp.dot(
                both.astype(jnp.bfloat16), ytab_ref[...], preferred_element_type=jnp.float32
            ).astype(jnp.bfloat16)
            planes = jnp.concatenate([planes[:, :freq], planes[:, freq:]], axis=0)
            image = jnp.dot(ztab_ref[...], planes, preferred_element_type=jnp.float32)
            out_ref[pair, :, :freq] = image[:depth].astype(jnp.bfloat16)
            out_ref[pair, :, freq:] = image[depth:].astype(jnp.bfloat16)


def whole(memory=pltpu.VMEM):
    return pl.BlockSpec(memory_space=memory)


def per_device(samples, sample_pos, block_count, grid_block, block_slab, sensitivity):
    slab_total = lax.axis_size("slab")
    coil_total = lax.axis_size("coil")
    coils = samples.shape[0]
    blocks = samples.shape[1]
    planes = sensitivity.shape[1]
    rows_out = sensitivity.shape[2] * coil_total
    depth = planes * slab_total
    freq = sensitivity.shape[3] // 2
    x_here = rows_out // slab_total
    segments = KX // CELLS

    live = ints(CELLS)[None, :] < block_count[:, None]
    pos = jnp.where(live, sample_pos, 9984.0).reshape(blocks // 2, 2 * CELLS)
    seg = (grid_block % segments)[None, :]
    kz = block_slab[:, 0] * planes + grid_block // (segments * freq)
    ky = grid_block // segments % freq
    kz, ky = kz.astype(jnp.float32)[None, :], ky.astype(jnp.float32)[None, :]

    tile = math.gcd(blocks, 2048)
    tiles = blocks // tile
    chunks = tile // LANES
    unroll = math.gcd(tile // 16, 16)
    count = 2 * coils * rows_out
    each = 2 * coils * x_here

    row = pl.BlockSpec((1, tile), lambda b: (0, b))
    spot, spots = pl.pallas_call(
        functools.partial(order_kernel, planes, freq),
        grid=(tiles,),
        in_specs=[row, row],
        out_specs=[row, pl.BlockSpec((1, 2, tile), lambda b: (b, 0, 0))],
        out_shape=[
            jax.ShapeDtypeStruct((1, blocks), jnp.float32),
            jax.ShapeDtypeStruct((tiles, 2, tile), jnp.float32),
        ],
        name="order_kz",
    )(kz, ky)

    table = spread_table(across_table(coils, rows_out, x_here), 2 * coils)
    x_at = (ints(count) // (2 * coils * x_here)) * x_here + ints(count) // 2 % x_here
    x_at = jnp.broadcast_to((x_at + (KX - rows_out) // 2)[:, None], (count, tile // RUNS))
    lines = pl.pallas_call(
        functools.partial(grid_kernel, coils, unroll),
        grid=(tiles,),
        in_specs=[
            pl.BlockSpec((tile // 2, LANES), lambda b: (b, 0)),
            pl.BlockSpec((coils, tile, LANES), lambda b: (0, b, 0)),
            row,
            pl.BlockSpec(x_at.shape, lambda b: (0, 0)),
            pl.BlockSpec(table.shape, lambda b: (0, 0)),
            row,
        ],
        out_specs=pl.BlockSpec((slab_total, 1, each, tile), lambda b: (0, b, 0, 0)),
        out_shape=jax.ShapeDtypeStruct((slab_total, tiles, each, tile), jnp.bfloat16),
        scratch_shapes=[
            pltpu.VMEM((tile, 2 * coils * LANES), jnp.bfloat16),
            pltpu.VMEM((unroll, CLASSES, 8, LANES), jnp.float32),
            pltpu.VMEM((unroll, CLASSES, 8, LANES), jnp.float32),
            pltpu.VMEM((RUNS, count, tile // RUNS), jnp.bfloat16),
        ],
        name="grid_x",
    )(pos, samples, seg, x_at, table, spot)

    sent = lax.all_to_all(lines, "slab", 0, 0, tiled=True)
    spots = lax.all_gather(spots, "slab")

    span = 32
    per = math.gcd(chunks, 4)
    steps = chunks // per
    by_chunk = spots[:, :, 0].reshape(slab_total, tiles, chunks, LANES)
    step_down = max(8 // each, 1)
    low = jnp.min(by_chunk, axis=(1, 3)).astype(jnp.int32) // step_down * step_down
    high = (jnp.max(by_chunk, axis=(1, 3)).astype(jnp.int32) - low) // span + 1
    ytab, ztab = right_table(freq), left_table(depth)
    pairs = each // 2
    imaged = pl.pallas_call(
        functools.partial(add_kernel, span, per),
        grid_spec=pltpu.PrefetchScalarGridSpec(
            num_scalar_prefetch=2,
            grid=(slab_total * steps,),
            in_specs=[
                pl.BlockSpec(
                    (1, tiles, each, per * LANES), lambda i, a, b: (i // steps, 0, 0, i % steps)
                ),
                pl.BlockSpec(
                    (1, tiles, 2, per * LANES), lambda i, a, b: (i // steps, 0, 0, i % steps)
                ),
                pl.BlockSpec(ytab.shape, lambda i, a, b: (0, 0)),
                pl.BlockSpec(ztab.shape, lambda i, a, b: (0, 0)),
            ],
            out_specs=pl.BlockSpec((pairs, depth, 2 * freq), lambda i, a, b: (0, 0, 0)),
            scratch_shapes=[
                pltpu.VMEM((freq // LANES, (depth + span) * each, LANES), jnp.float32)
            ],
        ),
        out_shape=jax.ShapeDtypeStruct((pairs, depth, 2 * freq), jnp.bfloat16),
        name="add_yz",
    )(low.reshape(-1), high.reshape(-1), sent, spots, ytab, ztab)

    split = imaged.reshape(pairs, slab_total, planes, 2 * freq)
    split = lax.all_to_all(jnp.swapaxes(split, 0, 1), "slab", 0, 0, tiled=True)
    split = split.reshape(slab_total, coils, x_here, planes, 2 * freq)
    split = jnp.transpose(split, (0, 2, 1, 3, 4)).reshape(
        coil_total, rows_out // coil_total, coils, planes, 2 * freq
    )
    split = lax.all_to_all(split, "coil", 0, 0, tiled=True)
    mine = jnp.transpose(split, (0, 2, 3, 1, 4)).reshape(sensitivity.shape).astype(jnp.float32)
    maps = sensitivity.astype(jnp.float32)
    map_re, map_im = maps[..., :freq], maps[..., freq:]
    img_re, img_im = mine[..., :freq], mine[..., freq:]
    real_part = jnp.sum(map_re * img_re + map_im * img_im, axis=0)
    imag_part = jnp.sum(map_re * img_im - map_im * img_re, axis=0)
    return jnp.concatenate([real_part, imag_part], axis=-1)


def solution(mesh):
    return jax.shard_map(
        per_device,
        mesh=mesh,
        in_specs=(
            P("coil", "slab", None),
            P("slab", None),
            P("slab"),
            P("slab"),
            P("slab", None),
            P(None, "slab", "coil", None),
        ),
        out_specs=P("slab", "coil", None),
        check_vma=False,
    )
```

time: 202 us -> 178 us (0.88); the launches traced: 201 us -> 175 us
  Pallas kernels: 112 us -> 85.1 us
  blocking collectives: 17.8 us -> 37.6 us
  waiting for transfers between devices: 38.6 us -> 23.6 us
  other arithmetic: 10.7 us -> 7.82 us
    pallas_call x3, Pallas kernels: 112 us -> 85.1 us  [the longest x1 41.6 us: per_device(): pl.pallas_call(functools.partial(grid_kernel, coils, unroll), grid=(tiles...]
    all_gather x0 -> x1, blocking collectives: none -> 19.8 us  [per_device(): spots = lax.all_gather(spots, 'slab')]
    all_to_all x1, waiting for transfers between devices: 15 us -> 0.01 us  [per_device(): sent = lax.all_to_all(lines, 'slab', 0, 0, tiled=True)]
    concatenate x1 -> x0, other arithmetic: 2.38 us -> none  [per_device(): jnp.concatenate([ordered.reshape(slab_total, each, blocks), tail], axis=2)]
    slice x2 -> x0, local copies, waits for them, and re-layouts: 2.34 us -> none  [the longest x1 1.41 us: per_device(): ky_all = spots[:, 1:2]]
  transfers between devices with their start and end apart: 2 -> 2, of which waited for: 2 -> 1; matrix products, arithmetic and copies ran while one was open for 2% -> 3% of each run, Pallas kernels for 0% -> 0%
where the time goes in v2:
time: 178 us; the launch traced here: 175 us
  Pallas kernels  85.1 us (48%)
  blocking collectives  37.6 us (21%)
  waiting for transfers between devices  23.6 us (13%)
  local copies, waits for them, and re-layouts  10.5 us (6%)
  starting transfers between devices  10.2 us (6%)
  other arithmetic  7.82 us (4%)
    pallas_call x1, Pallas kernels, per_device(): pl.pallas_call(functools.partial(grid_kernel, coils, unroll), grid=(tiles...  41.6 us
    pallas_call x1, Pallas kernels, per_device(): pl.pallas_call(functools.partial(add_kernel, span, per), grid_spec=pltpu....  37.7 us
    all_to_all x1, waiting for transfers between devices, per_device(): split = lax.all_to_all(split, 'coil', 0, 0, tiled=True)  23.6 us
    all_gather x1, blocking collectives, per_device(): spots = lax.all_gather(spots, 'slab')  19.8 us
    all_to_all x1, blocking collectives, per_device(): split = lax.all_to_all(jnp.swapaxes(split, 0, 1), 'slab', 0, 0, tiled=True)  17.9 us
    pallas_call x1, Pallas kernels, per_device(): pl.pallas_call(functools.partial(order_kernel, planes, freq), grid=(tiles...  5.68 us
    all_to_all x1, starting transfers between devices, per_device(): sent = lax.all_to_all(lines, 'slab', 0, 0, tiled=True)  5.33 us
    all_to_all x1, starting transfers between devices, per_device(): split = lax.all_to_all(split, 'coil', 0, 0, tiled=True)  4.87 us
  transfers between devices with their start and end apart: 2, of which 1 were waited for; matrix products, arithmetic and copies ran while one was open for 3% of the time, Pallas kernels for 0%

profile of v2, /device:TPU:0, one launch (start us, length us, event | category | flops | bytes accessed | tf_op | source)
XLA Modules:
  0.0 175.1 jit_solution(2278805727285829331)
XLA Ops:
  0.0 0.0 copy-start.6
  0.0 0.0 copy-start.2
  0.0 0.0 copy-start.4
  0.0 0.1 multiply_bitcast_fusion.1
  0.1 0.1 sine_multiply_fusion.1
  0.4 0.1 copy.51
  0.6 0.1 copy.53
  0.7 0.1 mul.394
  0.8 0.1 mul.395
  1.0 0.1 pad_maximum_fusion.5
  1.1 0.7 gather_fusion
  1.9 0.1 copy.54
  2.0 0.7 copy.64
  2.7 0.0 copy-done.6
  2.7 0.0 copy-done.2
  2.7 0.0 copy-done.4
  2.8 0.2 fusion
  3.0 1.1 copy.49
  4.1 0.0 copy-start.5
  4.1 1.8 %reshape.406.pos_ref = bf16[4096,128]{1,0:T(8,128)(2,1)} reshape(bf16[8192,64]{1,0:T(8,128)(2,1)S(1)} %copy.49) | data formatting | bytes 2097152 | tf_op jit(solution)/shard_map/reshape | solution.py:289
  5.9 0.0 copy-done.5
  5.9 0.7 add_select_fusion.1
  6.5 5.7 %order_kz.1 = (f32[1,8192]{1,0:T(1,128)}, f32[4,2,2048]{2,1,0:T(2,128)}) custom-call(f32[1,8192]{1,0:T(1,128)} %bitcast.53, f32[1,8192]{1,0:T(1,128)} %bitcast.52), custom_call_target="tpu_custom_call" | custom-call | tf_op jit(solution)/shard_map/order_kz/pallas_call | solution.py:303
  12.2 0.7 broadcast_in_dim.16.x_ref
  13.0 41.6 %grid_x.1 = bf16[8,4,8,2048]{3,2,1,0:T(8,128)(2,1)} custom-call(bf16[4096,128]{1,0:T(8,128)(2,1)} %reshape.406.pos_ref, bf16[2,8192,128]{2,1,0:T(8,128)(2,1)} %val_ref.1, s32[1,8192]{1,0:T(1,128)} %bitcast.50, s32[64,512]{1,0:T(8,128)} %broadcast_in_dim.16.x_ref, bf16[128,512]{1,0:T(8,128)(2,1)} %bitcast.45, f32[1,8192]{1,0:T(1,128)} %get-tuple-element.8.spot_ref), custom_call_target="tpu_custom_call" | custom-call | tf_op jit(solution)/shard_map/grid_x/pallas_call | solution.py:318
  54.6 0.0 copy-start.3
  54.6 5.3 %all-to-all-start = ((bf16[8,4,8,2048]{3,2,1,0:T(8,128)(2,1)}), bf16[8,4,8,2048]{3,2,1,0:T(8,128)(2,1)S(1)}, u32[]{:S(2)}, u32[]{:S(2)}) async-start(bf16[8,4,8,2048]{3,2,1,0:T(8,128)(2,1)} %grid_x.1), calls=%async_computation | async-start | bytes 2097152 | tf_op jit(solution)/shard_map/all_to_all | solution.py:340
  59.9 0.0 copy-done.3
  59.9 19.8 %all-gather = f32[32,2,2048]{2,1,0:T(2,128)S(1)} all-gather(f32[4,2,2048]{2,1,0:T(2,128)S(1)} %copy-done.3), channel_id=2, replica_groups=mesh['slab'=8,'coil'=4] {'slab'}, dimensions={0}, use_global_device_ids=true | all-gather | bytes 589824 | tf_op jit(solution)/shard_map/all_gather | solution.py:341
  79.7 0.0 copy-start.1
  79.7 0.5 slice_reduce_fusion
  80.2 0.1 bitcast_reduce_fusion
  80.3 0.1 copy.47
  80.4 0.1 convert_element_type.120.lo_ref
  80.5 0.0 copy-start.7
  80.5 0.1 copy.48
  80.6 0.1 convert_element_type.122
  80.6 1.0 fusion.9
  81.7 1.1 negate_convert_fusion
  82.8 1.1 fusion.2
  83.8 0.5 fusion.37.more_ref
  84.3 0.0 all-to-all-done.vals_ref
  84.3 0.0 copy-start
  84.3 0.0 copy-done.1
  84.3 0.0 copy-done.7
  84.3 1.0 copy-done
  85.3 37.7 %add_yz.1 = bf16[4,256,512]{2,1,0:T(8,128)(2,1)} custom-call(s32[128]{0:T(128)} %copy-done.7, s32[128]{0:T(128)} %fusion.37.more_ref, bf16[8,4,8,2048]{3,2,1,0:T(8,128)(2,1)} %copy-done, f32[8,4,2,2048]{3,2,1,0:T(2,128)} %bitcast.44, bf16[512,512]{1,0:T(8,128)(2,1)} %get-tuple-element.14.ytab_ref, bf16[512,512]{1,0:T(8,128)(2,1)} %get-tuple-element.13.ztab_ref), custom_call_target="tpu_custom_call" | custom-call | tf_op jit(solution)/shard_map/add_yz/pallas_call | solution.py:352
  123.0 1.3 copy.63
  124.4 17.9 %all_to_all.15 = bf16[8,4,32,512]{3,2,1,0:T(8,128)(2,1)S(1)} all-to-all(bf16[8,4,32,512]{3,2,1,0:T(8,128)(2,1)S(1)} %bitcast.40), channel_id=1, replica_groups=mesh['slab'=8,'coil'=4] {'slab'}, dimensions={0} | all-to-all | bytes 2097152 | tf_op jit(solution)/shard_map/all_to_all | solution.py:377
  142.2 1.1 copy.56
  143.3 4.9 %all-to-all-start.2 = ((bf16[4,4,2,32,512]{4,3,2,1,0:T(8,128)(2,1)}), bf16[4,4,2,32,512]{4,3,2,1,0:T(8,128)(2,1)S(1)}, u32[]{:S(2)}, u32[]{:S(2)}) async-start(bf16[4,4,2,32,512]{4,3,2,1,0:T(8,128)(2,1)} %bitcast.19), calls=%async_computation.2 | async-start | bytes 2097152 | tf_op jit(solution)/shard_map/all_to_all | solution.py:382
  148.1 1.5 copy_convert_fusion
  149.7 23.6 %all-to-all-done.2 = bf16[4,4,2,32,512]{4,3,2,1,0:T(8,128)(2,1)S(1)} async-done(((bf16[4,4,2,32,512]{4,3,2,1,0:T(8,128)(2,1)}), bf16[4,4,2,32,512]{4,3,2,1,0:T(8,128)(2,1)S(1)}, u32[]{:S(2)}, u32[]{:S(2)}) %all-to-all-start.2) | async-done | bytes 1048608 | tf_op jit(solution)/shard_map/all_to_all | solution.py:382
  173.3 0.3 convert_bitcast_fusion
  173.6 0.3 copy.57
  173.9 0.3 add_reduce_fusion
  174.2 0.9 copy.58
  (16 shorter events, 0.3 us)
Async XLA Ops:
  0.0 2.7 %copy-start.6 = (s32[8192,1]{0,1:T(1,128)S(1)}, s32[8192,1]{0,1:T(1,128)}, u32[]{:S(2)}) copy-start(s32[8192,1]{0,1:T(1,128)} %param.10) | copy-start | bytes 98308
  0.0 2.7 %copy-start.2 = (bf16[8192,64]{0,1:T(8,128)(2,1)S(1)}, bf16[8192,64]{0,1:T(8,128)(2,1)}, u32[]{:S(2)}) copy-start(bf16[8192,64]{0,1:T(8,128)(2,1)} %param.7) | copy-start | bytes 3145732
  0.0 2.7 %copy-start.4 = (s32[8192]{0:T(1024)S(1)}, s32[8192]{0:T(1024)}, u32[]{:S(2)}) copy-start(s32[8192]{0:T(1024)} %param.8) | copy-start | bytes 98308
  4.1 1.8 %copy-start.5 = (s32[8192]{0:T(1024)S(1)}, s32[8192]{0:T(1024)}, u32[]{:S(2)}) copy-start(s32[8192]{0:T(1024)} %param.9) | copy-start | bytes 98308
  54.6 5.3 %copy-start.3 = (f32[4,2,2048]{2,1,0:T(2,128)S(1)}, f32[4,2,2048]{2,1,0:T(2,128)}, u32[]{:S(2)}) copy-start(f32[4,2,2048]{2,1,0:T(2,128)} %get-tuple-element.7) | copy-start | bytes 196612
  54.6 29.7 %all-to-all-start = ((bf16[8,4,8,2048]{3,2,1,0:T(8,128)(2,1)}), bf16[8,4,8,2048]{3,2,1,0:T(8,128)(2,1)S(1)}, u32[]{:S(2)}, u32[]{:S(2)}) async-start(bf16[8,4,8,2048]{3,2,1,0:T(8,128)(2,1)} %grid_x.1), calls=%async_computation | async-start | bytes 2097152 | tf_op jit(solution)/shard_map/all_to_all | solution.py:340
  79.7 4.6 %copy-start.1 = (f32[32,2,2048]{2,1,0:T(2,128)}, f32[32,2,2048]{2,1,0:T(2,128)S(1)}, u32[]{:S(2)}) copy-start(f32[32,2,2048]{2,1,0:T(2,128)S(1)} %all-gather) | copy-start | bytes 1572868
  80.5 3.9 %copy-start.7 = (s32[128]{0:T(128)}, s32[128]{0:T(128)S(1)}, u32[]{:S(2)}) copy-start(s32[128]{0:T(128)S(1)} %convert_element_type.120.lo_ref) | copy-start | bytes 1540
  84.3 1.0 copy-start
  143.3 30.0 %all-to-all-start.2 = ((bf16[4,4,2,32,512]{4,3,2,1,0:T(8,128)(2,1)}), bf16[4,4,2,32,512]{4,3,2,1,0:T(8,128)(2,1)S(1)}, u32[]{:S(2)}, u32[]{:S(2)}) async-start(bf16[4,4,2,32,512]{4,3,2,1,0:T(8,128)(2,1)} %bitcast.19), calls=%async_computation.2 | async-start | bytes 2097152 | tf_op jit(solution)/shard_map/all_to_all | solution.py:382

commit v3 on v2

--- a/solution.py
+++ b/solution.py
@@ -12,7 +12,10 @@
 CELLS = 64
 CLASSES = 8
 LANES = 128
+HALF = LANES // 2
 RUNS = 4
+STRETCH = HALF // RUNS
+SPAN = 40
 NT = (((1,), (1,)), ((), ()))
 
 
@@ -82,22 +85,19 @@
 
 
 def regroup(runs):
-    count = len(runs)
     rows, length = runs[0].shape
-    wide = LANES // count
-    place = lax.broadcasted_iota(jnp.int32, (rows, LANES), 1) // wide
-    for at in range(length // wide):
-        cut = slice(at // count * LANES, at // count * LANES + LANES)
+    place = lax.broadcasted_iota(jnp.int32, (rows, LANES), 1) % HALF // STRETCH
+    for at in range(length // (2 * STRETCH)):
+        cut = slice(at // RUNS * LANES, at // RUNS * LANES + LANES)
         out = runs[0][:, cut]
-        for run in range(1, count):
-            out = jnp.where(place == (at + run) % count, runs[run][:, cut], out)
+        for run in range(1, RUNS):
+            out = jnp.where(place == (at + run) % RUNS, runs[run][:, cut], out)
         yield at, out
 
 
 def order_kernel(planes, freq, kz_ref, ky_ref, spot_ref, sorted_ref):
     tile = kz_ref.shape[1]
     length = tile // RUNS
-    wide = LANES // RUNS
     pieces = length // LANES
     runs = []
     for run in range(RUNS):
@@ -112,8 +112,9 @@
             part = jnp.concatenate([part] * pieces, axis=1)
             rank = rank + jnp.sum(jnp.where(part < key, 1.0, 0.0), axis=0, keepdims=True)
         rank = rank.astype(jnp.int32)
-        seat = rank // wide
-        spot = (seat // RUNS) * LANES + (seat + run) % RUNS * wide + rank % wide
+        seat = rank // (2 * STRETCH)
+        spot = seat // RUNS * LANES + rank // STRETCH % 2 * HALF
+        spot = spot + (seat + run) % RUNS * STRETCH + rank % STRETCH
         spot = spot.astype(jnp.float32)
         spot_ref[:, cut] = spot
         both = jnp.concatenate([kz, ky, jnp.zeros((14, length), jnp.float32)], axis=0)
@@ -202,38 +203,50 @@
 
 
 def add_kernel(
-    span, per, lo_ref, more_ref, vals_ref, spot_ref, ytab_ref, ztab_ref, out_ref, total
+    per, lo_ref, more_ref, vals_ref, spot_ref, ytab_ref, ztab_ref, out_ref, total
 ):
     step = pl.program_id(0)
     tiles, rows = vals_ref.shape[1], vals_ref.shape[2]
     pairs, depth, freq = out_ref.shape[0], out_ref.shape[1], out_ref.shape[2] // 2
     deep = 16 // rows
-    width = tiles * LANES
+    width = tiles * HALF
     inner = (lax.broadcasted_iota(jnp.int32, (16, width), 0) // rows).astype(jnp.float32)
 
     @pl.when(step == 0)
     def _():
         total[...] = jnp.zeros_like(total)
 
+    def pick(part, read):
+        cut = slice(part // 2 * LANES, part // 2 * LANES + LANES)
+        out = []
+        for t in range(0, tiles, 2):
+            first, second = read(t, cut), read(t + 1, cut)
+            low = lax.broadcasted_iota(jnp.int32, first.shape, 1) < HALF
+            if part % 2 == 0:
+                second = pltpu.roll(second, HALF, 1)
+            else:
+                first = pltpu.roll(first, HALF, 1)
+            out.append(jnp.where(low, first, second))
+        return jnp.concatenate(out, axis=1)
+
     def add(part, start):
-        cut = slice(part * LANES, (part + 1) * LANES)
-        across = [vals_ref[0, t, :, cut] for t in range(tiles)]
-        vals = jnp.concatenate([jnp.concatenate(across, axis=1)] * deep, axis=0)
-        kz = jnp.concatenate([spot_ref[0, t, 0:1, cut] for t in range(tiles)], axis=1)
-        ky = jnp.concatenate([spot_ref[0, t, 1:2, cut] for t in range(tiles)], axis=1)
+        vals = pick(part, lambda t, cut: vals_ref[0, t, :, cut].astype(jnp.float32))
+        vals = jnp.concatenate([vals] * deep, axis=0).astype(jnp.bfloat16)
+        both = pick(part, lambda t, cut: spot_ref[0, t, :, cut])
         base = jnp.full((16, width), start, jnp.int32).astype(jnp.float32)
-        plane = (jnp.broadcast_to(kz, (16, width)) - base - inner).astype(jnp.bfloat16)
+        plane = jnp.broadcast_to(both[0:1], (16, width)) - base - inner
+        plane = plane.astype(jnp.bfloat16)
         left = [
             jnp.where(plane == jnp.bfloat16(at), vals, jnp.bfloat16(0))
-            for at in range(0, span, deep)
+            for at in range(0, SPAN, deep)
         ]
         moved = lax.dot_general(
             jnp.concatenate(left, axis=0),
-            hot_rows(ky, freq),
+            hot_rows(both[1:2], freq),
             NT,
             preferred_element_type=jnp.float32,
         )
-        at = pl.ds(pl.multiple_of(start * rows, 8), span * rows)
+        at = pl.ds(pl.multiple_of(start * rows, 8), SPAN * rows)
         for half in range(freq // LANES):
             total[half, at, :] += moved[:, half * LANES : (half + 1) * LANES]
 
@@ -244,7 +257,7 @@
         first = lo_ref[step * per + part]
 
         def again(at, carry):
-            add(part, first + at * span)
+            add(part, first + at * SPAN)
             return carry
 
         lax.fori_loop(1, more_ref[step * per + part], again, 0)
@@ -340,17 +353,16 @@
     sent = lax.all_to_all(lines, "slab", 0, 0, tiled=True)
     spots = lax.all_gather(spots, "slab")
 
-    span = 32
     per = math.gcd(chunks, 4)
     steps = chunks // per
-    by_chunk = spots[:, :, 0].reshape(slab_total, tiles, chunks, LANES)
+    by_chunk = spots[:, :, 0].reshape(slab_total, tiles, 2 * chunks, HALF)
     step_down = max(8 // each, 1)
     low = jnp.min(by_chunk, axis=(1, 3)).astype(jnp.int32) // step_down * step_down
-    high = (jnp.max(by_chunk, axis=(1, 3)).astype(jnp.int32) - low) // span + 1
+    high = (jnp.max(by_chunk, axis=(1, 3)).astype(jnp.int32) - low) // SPAN + 1
     ytab, ztab = right_table(freq), left_table(depth)
     pairs = each // 2
     imaged = pl.pallas_call(
-        functools.partial(add_kernel, span, per),
+        functools.partial(add_kernel, 2 * per),
         grid_spec=pltpu.PrefetchScalarGridSpec(
             num_scalar_prefetch=2,
             grid=(slab_total * steps,),
@@ -366,7 +378,7 @@
             ],
             out_specs=pl.BlockSpec((pairs, depth, 2 * freq), lambda i, a, b: (0, 0, 0)),
             scratch_shapes=[
-                pltpu.VMEM((freq // LANES, (depth + span) * each, LANES), jnp.float32)
+                pltpu.VMEM((freq // LANES, (depth + SPAN) * each, LANES), jnp.float32)
             ],
         ),
         out_shape=jax.ShapeDtypeStruct((pairs, depth, 2 * freq), jnp.bfloat16),

time: 178 us -> 176 us (0.989)
  transfers between devices with their start and end apart: 2 -> 2, of which waited for: 1 -> 1; matrix products, arithmetic and copies ran while one was open for 3% -> 4% of each run, Pallas kernels for 0% -> 0%
where the time goes in v3:
time: 176 us; the launch traced here: 174 us
  Pallas kernels  84.1 us (48%)
  blocking collectives  37.6 us (21%)
  waiting for transfers between devices  23.6 us (13%)
  local copies, waits for them, and re-layouts  10.5 us (6%)
  starting transfers between devices  10.2 us (6%)
  other arithmetic  8.02 us (5%)
    pallas_call x1, Pallas kernels, per_device(): pl.pallas_call(functools.partial(grid_kernel, coils, unroll), grid=(tiles...  41.7 us
    pallas_call x1, Pallas kernels, per_device(): pl.pallas_call(functools.partial(add_kernel, 2 * per), grid_spec=pltpu.Pr...  36.6 us
    all_to_all x1, waiting for transfers between devices, per_device(): split = lax.all_to_all(split, 'coil', 0, 0, tiled=True)  23.6 us
    all_gather x1, blocking collectives, per_device(): spots = lax.all_gather(spots, 'slab')  19.8 us
    all_to_all x1, blocking collectives, per_device(): split = lax.all_to_all(jnp.swapaxes(split, 0, 1), 'slab', 0, 0, tiled=True)  17.9 us
    pallas_call x1, Pallas kernels, per_device(): pl.pallas_call(functools.partial(order_kernel, planes, freq), grid=(tiles...  5.8 us
    all_to_all x1, starting transfers between devices, per_device(): sent = lax.all_to_all(lines, 'slab', 0, 0, tiled=True)  5.34 us
    all_to_all x1, starting transfers between devices, per_device(): split = lax.all_to_all(split, 'coil', 0, 0, tiled=True)  4.87 us
  transfers between devices with their start and end apart: 2, of which 1 were waited for; matrix products, arithmetic and copies ran while one was open for 4% of the time, Pallas kernels for 0%

profile of v3, /device:TPU:0, one launch (start us, length us, event | category | flops | bytes accessed | tf_op | source)
XLA Modules:
  0.0 174.3 jit_solution(13143523190089439388)
XLA Ops:
  0.0 0.0 copy-start.6
  0.0 0.0 copy-start.2
  0.0 0.0 copy-start.4
  0.0 0.1 multiply_bitcast_fusion.1
  0.1 0.1 sine_multiply_fusion.1
  0.4 0.1 copy.36
  0.6 0.1 copy.38
  0.7 0.1 mul.394
  0.8 0.1 mul.395
  1.0 0.1 pad_maximum_fusion.5
  1.1 0.7 gather_fusion
  1.9 0.1 copy.39
  2.0 0.7 copy.49
  2.7 0.0 copy-done.6
  2.7 0.0 copy-done.2
  2.7 0.0 copy-done.4
  2.8 0.2 fusion
  3.0 1.1 copy.34
  4.1 0.0 copy-start.5
  4.1 1.8 %reshape.406.pos_ref = bf16[4096,128]{1,0:T(8,128)(2,1)} reshape(bf16[8192,64]{1,0:T(8,128)(2,1)S(1)} %copy.34) | data formatting | bytes 2097152 | tf_op jit(solution)/shard_map/reshape | solution.py:302
  5.9 0.0 copy-done.5
  5.9 0.7 add_select_fusion.1
  6.5 5.8 %order_kz.1 = (f32[1,8192]{1,0:T(1,128)}, f32[4,2,2048]{2,1,0:T(2,128)}) custom-call(f32[1,8192]{1,0:T(1,128)} %bitcast.49, f32[1,8192]{1,0:T(1,128)} %bitcast.48), custom_call_target="tpu_custom_call" | custom-call | tf_op jit(solution)/shard_map/order_kz/pallas_call | solution.py:316
  12.3 0.7 broadcast_in_dim.16.x_ref
  13.1 41.7 %grid_x.1 = bf16[8,4,8,2048]{3,2,1,0:T(8,128)(2,1)} custom-call(bf16[4096,128]{1,0:T(8,128)(2,1)} %reshape.406.pos_ref, bf16[2,8192,128]{2,1,0:T(8,128)(2,1)} %val_ref.1, s32[1,8192]{1,0:T(1,128)} %bitcast.46, s32[64,512]{1,0:T(8,128)} %broadcast_in_dim.16.x_ref, bf16[128,512]{1,0:T(8,128)(2,1)} %bitcast.41, f32[1,8192]{1,0:T(1,128)} %get-tuple-element.8.spot_ref), custom_call_target="tpu_custom_call" | custom-call | tf_op jit(solution)/shard_map/grid_x/pallas_call | solution.py:331
  54.8 0.0 copy-start.3
  54.8 5.3 %all-to-all-start = ((bf16[8,4,8,2048]{3,2,1,0:T(8,128)(2,1)}), bf16[8,4,8,2048]{3,2,1,0:T(8,128)(2,1)S(1)}, u32[]{:S(2)}, u32[]{:S(2)}) async-start(bf16[8,4,8,2048]{3,2,1,0:T(8,128)(2,1)} %grid_x.1), calls=%async_computation | async-start | bytes 2097152 | tf_op jit(solution)/shard_map/all_to_all | solution.py:353
  60.1 0.0 copy-done.3
  60.1 19.8 %all-gather = f32[32,2,2048]{2,1,0:T(2,128)S(1)} all-gather(f32[4,2,2048]{2,1,0:T(2,128)S(1)} %copy-done.3), channel_id=2, replica_groups=mesh['slab'=8,'coil'=4] {'slab'}, dimensions={0}, use_global_device_ids=true | all-gather | bytes 589824 | tf_op jit(solution)/shard_map/all_gather | solution.py:354
  79.9 0.0 copy-start.1
  79.9 0.5 slice_reduce_fusion
  80.4 0.1 reduce_min.14
  80.5 0.1 reduce_min.18
  80.6 0.1 convert_element_type.120.lo_ref
  80.7 0.0 copy-start.7
  80.7 0.1 reduce_max.14
  80.7 0.1 reduce_max.18
  80.9 0.1 convert_element_type.122
  81.0 1.0 fusion.9
  81.9 1.1 negate_convert_fusion
  83.1 1.1 fusion.2
  84.1 0.6 fusion.30.more_ref
  84.7 0.0 all-to-all-done.vals_ref
  84.7 0.0 copy-start
  84.7 0.0 copy-done.1
  84.7 0.0 copy-done.7
  84.7 1.0 copy-done
  85.7 36.6 %add_yz.1 = bf16[4,256,512]{2,1,0:T(8,128)(2,1)} custom-call(s32[256]{0:T(256)} %copy-done.7, s32[256]{0:T(256)} %fusion.30.more_ref, bf16[8,4,8,2048]{3,2,1,0:T(8,128)(2,1)} %copy-done, f32[8,4,2,2048]{3,2,1,0:T(2,128)} %bitcast.40, bf16[512,512]{1,0:T(8,128)(2,1)} %get-tuple-element.14.ytab_ref, bf16[512,512]{1,0:T(8,128)(2,1)} %get-tuple-element.13.ztab_ref), custom_call_target="tpu_custom_call" | custom-call | tf_op jit(solution)/shard_map/add_yz/pallas_call | solution.py:364
  122.3 1.3 copy.48
  123.6 17.9 %all_to_all.15 = bf16[8,4,32,512]{3,2,1,0:T(8,128)(2,1)S(1)} all-to-all(bf16[8,4,32,512]{3,2,1,0:T(8,128)(2,1)S(1)} %bitcast.37), channel_id=1, replica_groups=mesh['slab'=8,'coil'=4] {'slab'}, dimensions={0} | all-to-all | bytes 2097152 | tf_op jit(solution)/shard_map/all_to_all | solution.py:389
  141.5 1.0 copy.41
  142.5 4.9 %all-to-all-start.2 = ((bf16[4,4,2,32,512]{4,3,2,1,0:T(8,128)(2,1)}), bf16[4,4,2,32,512]{4,3,2,1,0:T(8,128)(2,1)S(1)}, u32[]{:S(2)}, u32[]{:S(2)}) async-start(bf16[4,4,2,32,512]{4,3,2,1,0:T(8,128)(2,1)} %bitcast.17), calls=%async_computation.2 | async-start | bytes 2097152 | tf_op jit(solution)/shard_map/all_to_all | solution.py:394
  147.4 1.5 copy_convert_fusion
  148.9 23.6 %all-to-all-done.2 = bf16[4,4,2,32,512]{4,3,2,1,0:T(8,128)(2,1)S(1)} async-done(((bf16[4,4,2,32,512]{4,3,2,1,0:T(8,128)(2,1)}), bf16[4,4,2,32,512]{4,3,2,1,0:T(8,128)(2,1)S(1)}, u32[]{:S(2)}, u32[]{:S(2)}) %all-to-all-start.2) | async-done | bytes 1048608 | tf_op jit(solution)/shard_map/all_to_all | solution.py:394
  172.6 0.3 convert_bitcast_fusion
  172.8 0.3 copy.42
  173.1 0.3 add_reduce_fusion
  173.4 0.9 copy.43
  (16 shorter events, 0.3 us)
Async XLA Ops:
  0.0 2.7 %copy-start.6 = (s32[8192,1]{0,1:T(1,128)S(1)}, s32[8192,1]{0,1:T(1,128)}, u32[]{:S(2)}) copy-start(s32[8192,1]{0,1:T(1,128)} %param.10) | copy-start | bytes 98308
  0.0 2.7 %copy-start.2 = (bf16[8192,64]{0,1:T(8,128)(2,1)S(1)}, bf16[8192,64]{0,1:T(8,128)(2,1)}, u32[]{:S(2)}) copy-start(bf16[8192,64]{0,1:T(8,128)(2,1)} %param.7) | copy-start | bytes 3145732
  0.0 2.7 %copy-start.4 = (s32[8192]{0:T(1024)S(1)}, s32[8192]{0:T(1024)}, u32[]{:S(2)}) copy-start(s32[8192]{0:T(1024)} %param.8) | copy-start | bytes 98308
  4.1 1.8 %copy-start.5 = (s32[8192]{0:T(1024)S(1)}, s32[8192]{0:T(1024)}, u32[]{:S(2)}) copy-start(s32[8192]{0:T(1024)} %param.9) | copy-start | bytes 98308
  54.8 5.3 %copy-start.3 = (f32[4,2,2048]{2,1,0:T(2,128)S(1)}, f32[4,2,2048]{2,1,0:T(2,128)}, u32[]{:S(2)}) copy-start(f32[4,2,2048]{2,1,0:T(2,128)} %get-tuple-element.7) | copy-start | bytes 196612
  54.8 30.0 %all-to-all-start = ((bf16[8,4,8,2048]{3,2,1,0:T(8,128)(2,1)}), bf16[8,4,8,2048]{3,2,1,0:T(8,128)(2,1)S(1)}, u32[]{:S(2)}, u32[]{:S(2)}) async-start(bf16[8,4,8,2048]{3,2,1,0:T(8,128)(2,1)} %grid_x.1), calls=%async_computation | async-start | bytes 2097152 | tf_op jit(solution)/shard_map/all_to_all | solution.py:353
  79.9 4.9 %copy-start.1 = (f32[32,2,2048]{2,1,0:T(2,128)}, f32[32,2,2048]{2,1,0:T(2,128)S(1)}, u32[]{:S(2)}) copy-start(f32[32,2,2048]{2,1,0:T(2,128)S(1)} %all-gather) | copy-start | bytes 1572868
  80.7 4.1 %copy-start.7 = (s32[256]{0:T(256)}, s32[256]{0:T(256)S(1)}, u32[]{:S(2)}) copy-start(s32[256]{0:T(256)S(1)} %convert_element_type.120.lo_ref) | copy-start | bytes 3076
  84.7 1.0 copy-start
  142.5 30.0 %all-to-all-start.2 = ((bf16[4,4,2,32,512]{4,3,2,1,0:T(8,128)(2,1)}), bf16[4,4,2,32,512]{4,3,2,1,0:T(8,128)(2,1)S(1)}, u32[]{:S(2)}, u32[]{:S(2)}) async-start(bf16[4,4,2,32,512]{4,3,2,1,0:T(8,128)(2,1)} %bitcast.17), calls=%async_computation.2 | async-start | bytes 2097152 | tf_op jit(solution)/shard_map/all_to_all | solution.py:394

commit v4 on v3

--- a/solution.py
+++ b/solution.py
@@ -17,6 +17,7 @@
 STRETCH = HALF // RUNS
 SPAN = 40
 NT = (((1,), (1,)), ((), ()))
+MESH = pl.DeviceIdType.MESH
 
 
 def twiddle(first, second, length):
@@ -124,11 +125,75 @@
 
 
 def grid_kernel(
-    coils, unroll, pos_ref, val_ref, seg_ref, x_ref, tab_ref, spot_ref, out_ref,
-    cells, near, bump, placed,
+    coils, unroll, pos_ref, val_ref, seg_ref, x_ref, tab_ref, spot_ref, spots_ref, map_ref,
+    lines_ref, every_ref, maps_ref,
+    cells, near, bump, placed, ready, line_out, line_in, line_own,
+    spots_out, spots_in, spots_own, map_out, map_in, map_own,
 ):
-    slabs, _, each, tile = out_ref.shape
+    turn_at = pl.program_id(0)
+    tiles, slabs, each, tile = ready.shape
     rows = slabs * each
+    deals, shares = map_ref.shape[0], map_ref.shape[1]
+    slab, coil = lax.axis_index("slab"), lax.axis_index("coil")
+    barrier = pltpu.get_barrier_semaphore()
+    here = slab // shares == coil
+
+    def line_copy(at, hop):
+        peer = lax.rem(slab + hop, slabs)
+        return pltpu.make_async_remote_copy(
+            ready.at[at, peer], lines_ref.at[slab, at], line_out.at[at, hop], line_in.at[at, hop],
+            device_id={"slab": peer}, device_id_type=MESH,
+        )
+
+    def line_keep(at):
+        return pltpu.make_async_copy(
+            ready.at[at, slab], lines_ref.at[slab, at], line_own.at[at]
+        )
+
+    def spots_copy(hop):
+        peer = lax.rem(slab + hop, slabs)
+        return pltpu.make_async_remote_copy(
+            spots_ref, every_ref.at[slab], spots_out.at[hop], spots_in.at[hop],
+            device_id={"slab": peer}, device_id_type=MESH,
+        )
+
+    def spots_keep():
+        return pltpu.make_async_copy(spots_ref, every_ref.at[slab], spots_own)
+
+    def map_copy(deal, share):
+        return pltpu.make_async_remote_copy(
+            map_ref.at[deal, share], maps_ref.at[slab],
+            map_out.at[deal, share], map_in.at[slab],
+            device_id={"slab": coil * shares + share, "coil": deal}, device_id_type=MESH,
+        )
+
+    def map_take(source):
+        return pltpu.make_async_remote_copy(
+            map_ref.at[0, 0], maps_ref.at[source], map_out.at[0, 0], map_in.at[source],
+            device_id={"slab": slab, "coil": coil}, device_id_type=MESH,
+        )
+
+    def map_keep():
+        return pltpu.make_async_copy(
+            map_ref.at[coil, lax.rem(slab, shares)], maps_ref.at[slab], map_own
+        )
+
+    def is_me(deal, share):
+        return jnp.logical_and(coil * shares + share == slab, coil == deal)
+
+    @pl.when(turn_at == 0)
+    def _():
+        for hop in range(1, slabs):
+            pl.semaphore_signal(
+                barrier, 1, device_id={"slab": lax.rem(slab + hop, slabs)}, device_id_type=MESH
+            )
+        for source in range(slabs):
+            @pl.when(jnp.logical_not(jnp.logical_and(here, source == slab)))
+            def _():
+                pl.semaphore_signal(
+                    barrier, 1, device_id={"slab": source, "coil": slab // shares},
+                    device_id_type=MESH,
+                )
     length = tile // RUNS
     block = lax.broadcasted_iota(jnp.int32, (16, LANES), 0)
     upper = lax.broadcasted_iota(jnp.int32, (16, LANES), 1) >= CELLS
@@ -196,14 +261,58 @@
         turned = jnp.where(turn >= 2, -turned, turned).astype(jnp.bfloat16)
         placed[run] = permute(turned, spot_ref[:, cut]).astype(jnp.bfloat16)
     for at, out in regroup([placed.at[run] for run in range(RUNS)]):
-        for slab in range(slabs):
-            out_ref[slab, 0, :, at * LANES : (at + 1) * LANES] = out[
-                slab * each : (slab + 1) * each
+        for owner in range(slabs):
+            ready[turn_at, owner, :, at * LANES : (at + 1) * LANES] = out[
+                owner * each : (owner + 1) * each
             ]
 
+    @pl.when(turn_at == 0)
+    def _():
+        pl.semaphore_wait(barrier, slabs - 1 + deals * shares - here.astype(jnp.int32))
+        spots_keep().start()
+        for hop in range(1, slabs):
+            spots_copy(hop).start()
+        for deal in range(deals):
+            for share in range(shares):
+                @pl.when(jnp.logical_not(is_me(deal, share)))
+                def _():
+                    map_copy(deal, share).start()
+
+        @pl.when(here)
+        def _():
+            map_keep().start()
+
+    for hop in range(1, slabs):
+        line_copy(turn_at, hop).start()
+    line_keep(turn_at).start()
+
+    @pl.when(turn_at == tiles - 1)
+    def _():
+        spots_keep().wait()
+        for hop in range(1, slabs):
+            spots_copy(hop).wait()
+        for deal in range(deals):
+            for share in range(shares):
+                @pl.when(jnp.logical_not(is_me(deal, share)))
+                def _():
+                    map_copy(deal, share).wait_send()
+        for source in range(slabs):
+            @pl.when(jnp.logical_not(jnp.logical_and(here, source == slab)))
+            def _():
+                map_take(source).wait_recv()
+
+        @pl.when(here)
+        def _():
+            map_keep().wait()
+
+        for at in range(tiles):
+            line_keep(at).wait()
+            for hop in range(1, slabs):
+                line_copy(at, hop).wait()
+
 
 def add_kernel(
-    per, lo_ref, more_ref, vals_ref, spot_ref, ytab_ref, ztab_ref, out_ref, total
+    per, lo_ref, more_ref, vals_ref, spot_ref, out_ref, total
 ):
     step = pl.program_id(0)
     tiles, rows = vals_ref.shape[1], vals_ref.shape[2]
@@ -265,25 +374,91 @@
     @pl.when(step == pl.num_programs(0) - 1)
     def _():
         for pair in range(pairs):
-            both = jnp.concatenate(
-                [
-                    total[half, pl.ds(2 * pair + part, depth, stride=rows), :]
-                    for part in range(2)
-                    for half in range(freq // LANES)
-                ],
-                axis=1,
-            )
-            planes = jnp.dot(
-                both.astype(jnp.bfloat16), ytab_ref[...], preferred_element_type=jnp.float32
+            for part in range(2):
+                for half in range(freq // LANES):
+                    start = part * freq + half * LANES
+                    found = total[half, pl.ds(2 * pair + part, depth, stride=rows), :]
+                    out_ref[pair, :, start : start + LANES] = found.astype(jnp.bfloat16)
+
+
+def image_kernel(
+    rows_ref, map_ref, ytab_ref, ztab_ref, out_ref, ready, near, far,
+    near_out, near_in, far_out, far_in,
+):
+    wide, slabs, planes, _ = ready.shape
+    coils = rows_ref.shape[0] // wide
+    deals, shares = far.shape[0], far.shape[1]
+    depth, freq = rows_ref.shape[1], rows_ref.shape[2] // 2
+    slab, coil = lax.axis_index("slab"), lax.axis_index("coil")
+    barrier = pltpu.get_barrier_semaphore()
+    for hop in range(1, slabs):
+        peer = {"slab": lax.rem(slab + hop, slabs)}
+        pl.semaphore_signal(barrier, 1, device_id=peer, device_id_type=MESH)
+    for hop in range(1, deals):
+        peer = {"coil": lax.rem(coil + hop, deals)}
+        pl.semaphore_signal(barrier, 1, device_id=peer, device_id_type=MESH)
+
+    def near_copy(x, hop):
+        peer = lax.rem(slab + hop, slabs)
+        return pltpu.make_async_remote_copy(
+            ready.at[x, peer], near.at[x, slab], near_out.at[x, hop], near_in.at[x, hop],
+            device_id={"slab": peer}, device_id_type=MESH,
+        )
+
+    def far_copy(x, source, hop):
+        share = lax.rem(source, shares)
+        return pltpu.make_async_remote_copy(
+            near.at[x, source], far.at[hop, share, x],
+            far_out.at[hop, share, x], far_in.at[hop, share, x],
+            device_id={"coil": lax.rem(coil + hop, deals)}, device_id_type=MESH,
+        )
+
+    for x in range(wide):
+        real = imag = 0.0
+        for c in range(coils):
+            planar = jnp.dot(
+                rows_ref[c * wide + x], ytab_ref[...], preferred_element_type=jnp.float32
             ).astype(jnp.bfloat16)
-            planes = jnp.concatenate([planes[:, :freq], planes[:, freq:]], axis=0)
-            image = jnp.dot(ztab_ref[...], planes, preferred_element_type=jnp.float32)
-            out_ref[pair, :, :freq] = image[:depth].astype(jnp.bfloat16)
-            out_ref[pair, :, freq:] = image[depth:].astype(jnp.bfloat16)
-
-
-def whole(memory=pltpu.VMEM):
-    return pl.BlockSpec(memory_space=memory)
+            planar = jnp.concatenate([planar[:, :freq], planar[:, freq:]], axis=0)
+            image = jnp.dot(ztab_ref[...], planar, preferred_element_type=jnp.float32)
+            image = image.astype(jnp.bfloat16).astype(jnp.float32)
+            img_re, img_im = image[:depth], image[depth:]
+            maps = map_ref[:, c, x].reshape(depth, 2 * freq).astype(jnp.float32)
+            map_re, map_im = maps[:, :freq], maps[:, freq:]
+            real = real + (map_re * img_re + map_im * img_im)
+            imag = imag + (map_re * img_im - map_im * img_re)
+        both = jnp.concatenate([real, imag], axis=1).astype(jnp.bfloat16)
+        ready[x] = both.reshape(slabs, planes, 2 * freq)
+        near[x, pl.ds(slab, 1)] = ready[x, pl.ds(slab, 1)]
+        if x == 0:
+            pl.semaphore_wait(barrier, slabs - 1 + deals - 1)
+        for hop in range(1, slabs):
+            near_copy(x, hop).start()
+
+    for x in range(wide):
+        for hop in range(slabs):
+            source = lax.rem(slab + slabs - hop, slabs)
+            if hop > 0:
+                near_copy(x, hop).wait_recv()
+            leap = lax.rem(source // shares + deals - coil, deals)
+
+            @pl.when(leap > 0)
+            def _():
+                far_copy(x, source, leap).start()
+
+    for x in range(wide):
+        for share in range(shares):
+            value = near[x, coil * shares + share].astype(jnp.float32)
+            for hop in range(1, deals):
+                far_copy(x, share, hop).wait_recv()
+                value = value + far[hop, share, x].astype(jnp.float32)
+            out_ref[:, share * wide + x, :] = value
+    for x in range(wide):
+        for hop in range(1, slabs):
+            near_copy(x, hop).wait_send()
+        for share in range(shares):
+            for hop in range(1, deals):
+                far_copy(x, share, hop).wait_send()
 
 
 def per_device(samples, sample_pos, block_count, grid_block, block_slab, sensitivity):
@@ -328,7 +503,12 @@
     table = spread_table(across_table(coils, rows_out, x_here), 2 * coils)
     x_at = (ints(count) // (2 * coils * x_here)) * x_here + ints(count) // 2 % x_here
     x_at = jnp.broadcast_to((x_at + (KX - rows_out) // 2)[:, None], (count, tile // RUNS))
-    lines = pl.pallas_call(
+    x_own = sensitivity.shape[2]
+    maps = sensitivity.reshape(
+        coil_total, coils, planes, x_own // x_here, x_here, 2 * freq
+    ).transpose(0, 3, 1, 4, 2, 5)
+    anywhere = pl.BlockSpec(memory_space=pl.ANY)
+    sent, spots, maps = pl.pallas_call(
         functools.partial(grid_kernel, coils, unroll),
         grid=(tiles,),
         in_specs=[
@@ -338,20 +518,34 @@
             pl.BlockSpec(x_at.shape, lambda b: (0, 0)),
             pl.BlockSpec(table.shape, lambda b: (0, 0)),
             row,
+            pl.BlockSpec(spots.shape, lambda b: (0, 0, 0)),
+            anywhere,
         ],
-        out_specs=pl.BlockSpec((slab_total, 1, each, tile), lambda b: (0, b, 0, 0)),
-        out_shape=jax.ShapeDtypeStruct((slab_total, tiles, each, tile), jnp.bfloat16),
+        out_specs=[anywhere] * 3,
+        out_shape=[
+            jax.ShapeDtypeStruct((slab_total, tiles, each, tile), jnp.bfloat16),
+            jax.ShapeDtypeStruct((slab_total,) + spots.shape, jnp.float32),
+            jax.ShapeDtypeStruct((slab_total,) + maps.shape[2:], jnp.bfloat16),
+        ],
         scratch_shapes=[
             pltpu.VMEM((tile, 2 * coils * LANES), jnp.bfloat16),
             pltpu.VMEM((unroll, CLASSES, 8, LANES), jnp.float32),
             pltpu.VMEM((unroll, CLASSES, 8, LANES), jnp.float32),
             pltpu.VMEM((RUNS, count, tile // RUNS), jnp.bfloat16),
+            pltpu.VMEM((tiles, slab_total, each, tile), jnp.bfloat16),
+            pltpu.SemaphoreType.DMA((tiles, slab_total)),
+            pltpu.SemaphoreType.DMA((tiles, slab_total)),
+            pltpu.SemaphoreType.DMA((tiles,)),
+            pltpu.SemaphoreType.DMA((slab_total,)),
+            pltpu.SemaphoreType.DMA((slab_total,)),
+            pltpu.SemaphoreType.DMA,
+            pltpu.SemaphoreType.DMA(maps.shape[:2]),
+            pltpu.SemaphoreType.DMA((slab_total,)),
+            pltpu.SemaphoreType.DMA,
         ],
+        compiler_params=pltpu.CompilerParams(collective_id=0, has_side_effects=True),
         name="grid_x",
-    )(pos, samples, seg, x_at, table, spot)
-
-    sent = lax.all_to_all(lines, "slab", 0, 0, tiled=True)
-    spots = lax.all_gather(spots, "slab")
+    )(pos, samples, seg, x_at, table, spot, spots, maps)
 
     per = math.gcd(chunks, 4)
     steps = chunks // per
@@ -373,8 +567,6 @@
                 pl.BlockSpec(
                     (1, tiles, 2, per * LANES), lambda i, a, b: (i // steps, 0, 0, i % steps)
                 ),
-                pl.BlockSpec(ytab.shape, lambda i, a, b: (0, 0)),
-                pl.BlockSpec(ztab.shape, lambda i, a, b: (0, 0)),
             ],
             out_specs=pl.BlockSpec((pairs, depth, 2 * freq), lambda i, a, b: (0, 0, 0)),
             scratch_shapes=[
@@ -383,22 +575,27 @@
         ),
         out_shape=jax.ShapeDtypeStruct((pairs, depth, 2 * freq), jnp.bfloat16),
         name="add_yz",
-    )(low.reshape(-1), high.reshape(-1), sent, spots, ytab, ztab)
-
-    split = imaged.reshape(pairs, slab_total, planes, 2 * freq)
-    split = lax.all_to_all(jnp.swapaxes(split, 0, 1), "slab", 0, 0, tiled=True)
-    split = split.reshape(slab_total, coils, x_here, planes, 2 * freq)
-    split = jnp.transpose(split, (0, 2, 1, 3, 4)).reshape(
-        coil_total, rows_out // coil_total, coils, planes, 2 * freq
-    )
-    split = lax.all_to_all(split, "coil", 0, 0, tiled=True)
-    mine = jnp.transpose(split, (0, 2, 3, 1, 4)).reshape(sensitivity.shape).astype(jnp.float32)
-    maps = sensitivity.astype(jnp.float32)
-    map_re, map_im = maps[..., :freq], maps[..., freq:]
-    img_re, img_im = mine[..., :freq], mine[..., freq:]
-    real_part = jnp.sum(map_re * img_re + map_im * img_im, axis=0)
-    imag_part = jnp.sum(map_re * img_im - map_im * img_re, axis=0)
-    return jnp.concatenate([real_part, imag_part], axis=-1)
+    )(low.reshape(-1), high.reshape(-1), sent, spots)
+
+    shares = x_own // x_here
+    memory = pl.BlockSpec(memory_space=pltpu.VMEM)
+    return pl.pallas_call(
+        image_kernel,
+        in_specs=[memory] * 4,
+        out_specs=memory,
+        out_shape=jax.ShapeDtypeStruct((planes, x_own, 2 * freq), jnp.float32),
+        scratch_shapes=[
+            pltpu.VMEM((x_here, slab_total, planes, 2 * freq), jnp.bfloat16),
+            pltpu.VMEM((x_here, slab_total, planes, 2 * freq), jnp.bfloat16),
+            pltpu.VMEM((coil_total, shares, x_here, planes, 2 * freq), jnp.bfloat16),
+            pltpu.SemaphoreType.DMA((x_here, slab_total)),
+            pltpu.SemaphoreType.DMA((x_here, slab_total)),
+            pltpu.SemaphoreType.DMA((coil_total, shares, x_here)),
+            pltpu.SemaphoreType.DMA((coil_total, shares, x_here)),
+        ],
+        compiler_params=pltpu.CompilerParams(collective_id=1, has_side_effects=True),
+        name="image_sum",
+    )(imaged, maps, ytab, ztab)
 
 
 def solution(mesh):

time: 176 us -> 129 us (0.73)
  blocking collectives: 37.6 us -> 0 us
  Pallas kernels: 84.1 us -> 111 us
  waiting for transfers between devices: 23.6 us -> 0 us
  starting transfers between devices: 10.2 us -> 0 us
    all_to_all x2 -> x0, waiting for transfers between devices: 23.6 us -> none  [the longest x1 23.6 us: per_device(): split = lax.all_to_all(split, 'coil', 0, 0, tiled=True)]
    pallas_call x0 -> x1, Pallas kernels: none -> 22.8 us  [per_device(): pl.pallas_call(image_kernel, in_specs=[memory] * 4, out_specs=memory, out...]
    all_gather x1 -> x0, blocking collectives: 19.8 us -> none  [per_device(): spots = lax.all_gather(spots, 'slab')]
    all_to_all x1 -> x0, blocking collectives: 17.9 us -> none  [per_device(): split = lax.all_to_all(jnp.swapaxes(split, 0, 1), 'slab', 0, 0, tiled=True)]
    all_to_all x2 -> x0, starting transfers between devices: 10.2 us -> none  [the longest x1 5.34 us: per_device(): sent = lax.all_to_all(lines, 'slab', 0, 0, tiled=True)]
    pallas_call x1, Pallas kernels: 41.7 us -> 48.9 us  [per_device(): pl.pallas_call(functools.partial(grid_kernel, coils, unroll), grid=(tiles...]
    pallas_call x1, Pallas kernels: 36.6 us -> 33.3 us  [per_device(): pl.pallas_call(functools.partial(add_kernel, 2 * per), grid_spec=pltpu.Pr...]
  transfers between devices with their start and end apart: 2 -> 0, of which waited for: 1 -> 0; matrix products, arithmetic and copies ran while one was open for 4% -> 0% of each run, Pallas kernels for 0% -> 0%
where the time goes in v4:
time: 129 us; the launch traced here: 127 us
  Pallas kernels  111 us (86%)
  local copies, waits for them, and re-layouts  9 us (7%)
  other arithmetic  6.96 us (5%)
    pallas_call x1, Pallas kernels, per_device(): pl.pallas_call(functools.partial(grid_kernel, coils, unroll), grid=(tiles...  48.9 us
    pallas_call x1, Pallas kernels, per_device(): pl.pallas_call(functools.partial(add_kernel, 2 * per), grid_spec=pltpu.Pr...  33.3 us
    pallas_call x1, Pallas kernels, per_device(): pl.pallas_call(image_kernel, in_specs=[memory] * 4, out_specs=memory, out...  22.8 us
    pallas_call x1, Pallas kernels, per_device(): pl.pallas_call(functools.partial(order_kernel, planes, freq), grid=(tiles...  5.81 us
    unnamed x15, local copies, waits for them, and re-layouts  2.59 us

profile of v4, /device:TPU:0, one launch (start us, length us, event | category | flops | bytes accessed | tf_op | source)
XLA Modules:
  0.0 127.1 jit_solution(3319827960357065651)
XLA Ops:
  0.0 0.0 copy-start.4
  0.0 0.0 copy-start.3
  0.0 0.0 copy-start
  0.0 0.0 copy-start.2
  0.0 0.1 multiply_bitcast_fusion.1
  0.2 0.1 sine_multiply_fusion.1
  0.4 0.1 copy.24
  0.6 0.1 copy.26
  0.7 0.1 mul.379
  0.8 0.1 mul.380
  0.9 0.1 multiply_convert_fusion.2
  1.0 0.1 pad_maximum_fusion.4
  1.1 0.7 gather_fusion
  1.9 0.1 copy.27
  2.0 0.7 copy.34
  2.7 0.0 copy-done.4
  2.7 0.0 copy-done.3
  2.7 0.7 fusion.14
  3.4 5.8 %order_kz.1 = (f32[1,8192]{1,0:T(1,128)}, f32[4,2,2048]{2,1,0:T(2,128)}) custom-call(f32[1,8192]{1,0:T(1,128)} %bitcast.36, f32[1,8192]{1,0:T(1,128)} %bitcast.35), custom_call_target="tpu_custom_call" | custom-call | tf_op jit(solution)/shard_map/order_kz/pallas_call | solution.py:491
  9.2 0.0 copy-done
  9.2 0.0 copy-done.2
  9.2 0.2 fusion
  9.5 1.1 copy.22
  10.6 0.0 copy-start.1
  10.6 1.8 %reshape.397.pos_ref = bf16[4096,128]{1,0:T(8,128)(2,1)} reshape(bf16[8192,64]{1,0:T(8,128)(2,1)S(1)} %copy.22) | data formatting | bytes 2097152 | tf_op jit(solution)/shard_map/reshape | solution.py:477
  12.4 0.0 copy-done.1
  12.4 0.2 copy.28
  12.6 1.1 copy.33
  13.7 0.7 broadcast_in_dim.14.x_ref
  14.4 48.9 %grid_x.1 = (bf16[8,4,8,2048]{3,2,1,0:T(8,128)(2,1)}, f32[8,4,2,2048]{3,2,1,0:T(2,128)}, bf16[8,2,2,32,512]{4,3,2,1,0:T(8,128)(2,1)}) custom-call(bf16[4096,128]{1,0:T(8,128)(2,1)} %reshape.397.pos_ref, bf16[2,8192,128]{2,1,0:T(8,128)(2,1)} %val_ref.1, s32[1,8192]{1,0:T(1,128)} %bitcast.34, s32[64,512]{1,0:T(8,128)} %broadcast_in_dim.14.x_ref, ...), custom_call_target="tpu_custom_call" | custom-call | tf_op jit(solution)/shard_map/grid_x/pallas_call | solution.py:511
  63.4 1.5 %slice_reduce_fusion = (f32[8,2048]{1,0:T(8,128)S(1)}, f32[8,2048]{1,0:T(8,128)S(1)}) fusion(f32[8,4,2,2048]{3,2,1,0:T(2,128)} %get-tuple-element.12.spot_ref), kind=kLoop, calls=%fused_computation.23 | loop fusion | flops 98304 | bytes 393216 | tf_op jit(solution)/shard_map/reduce_max | solution.py:555
  64.9 0.1 reduce_min.14
  65.0 0.1 reduce_min.18
  65.1 0.1 convert_element_type.110.lo_ref
  65.2 0.0 copy-start.5
  65.2 0.1 reduce_max.14
  65.3 0.1 reduce_max.18
  65.4 0.1 convert_element_type.112
  65.5 0.6 fusion.30.more_ref
  66.1 0.0 copy-done.5
  66.1 33.3 %add_yz.1.rows_ref = bf16[4,256,512]{2,1,0:T(8,128)(2,1)} custom-call(s32[256]{0:T(256)} %copy-done.5, s32[256]{0:T(256)} %fusion.30.more_ref, bf16[8,4,8,2048]{3,2,1,0:T(8,128)(2,1)} %get-tuple-element.13.vals_ref, f32[8,4,2,2048]{3,2,1,0:T(2,128)} %get-tuple-element.12.spot_ref), custom_call_target="tpu_custom_call" | custom-call | tf_op jit(solution)/shard_map/add_yz/pallas_call | solution.py:558
  99.4 1.1 negate_convert_fusion
  100.5 1.0 fusion.9
  101.5 1.1 fusion.2
  102.6 22.8 %image_sum.1 = f32[32,4,512]{2,1,0:T(4,128)} custom-call(bf16[4,256,512]{2,1,0:T(8,128)(2,1)} %add_yz.1.rows_ref, bf16[8,2,2,32,512]{4,3,2,1,0:T(8,128)(2,1)} %get-tuple-element.14.map_ref, bf16[512,512]{1,0:T(8,128)(2,1)} %get-tuple-element.18.ytab_ref, bf16[512,512]{1,0:T(8,128)(2,1)} %get-tuple-element.17.ztab_ref), custom_call_target="tpu_custom_call" | custom-call | tf_op jit(solution)/shard_map/image_sum/pallas_call | solution.py:582
  125.4 1.7 %copy.36 = f32[32,4,512]{2,1,0:T(4,128)} copy(f32[32,4,512]{2,1,0:T(4,128)} %image_sum.1) | data formatting | bytes 524288
  (14 shorter events, 0.2 us)
Async XLA Ops:
  0.0 2.7 %copy-start.4 = (s32[8192,1]{0,1:T(1,128)S(1)}, s32[8192,1]{0,1:T(1,128)}, u32[]{:S(2)}) copy-start(s32[8192,1]{0,1:T(1,128)} %param.10) | copy-start | bytes 98308
  0.0 2.7 %copy-start.3 = (s32[8192]{0:T(1024)S(1)}, s32[8192]{0:T(1024)}, u32[]{:S(2)}) copy-start(s32[8192]{0:T(1024)} %param.9) | copy-start | bytes 98308
  0.0 9.2 %copy-start = (bf16[8192,64]{0,1:T(8,128)(2,1)S(1)}, bf16[8192,64]{0,1:T(8,128)(2,1)}, u32[]{:S(2)}) copy-start(bf16[8192,64]{0,1:T(8,128)(2,1)} %param.7) | copy-start | bytes 3145732
  0.0 9.2 %copy-start.2 = (s32[8192]{0:T(1024)S(1)}, s32[8192]{0:T(1024)}, u32[]{:S(2)}) copy-start(s32[8192]{0:T(1024)} %param.8) | copy-start | bytes 98308
  10.6 1.8 %copy-start.1 = (bf16[8,32,4,512]{3,2,1,0:T(4,128)(2,1)S(1)}, bf16[8,32,4,512]{3,2,1,0:T(4,128)(2,1)}, u32[]{:S(2)}) copy-start(bf16[8,32,4,512]{3,2,1,0:T(4,128)(2,1)} %param.11) | copy-start | bytes 3145732
  65.2 0.9 copy-start.5

commit v5 on v4

--- a/solution.py
+++ b/solution.py
@@ -3,6 +3,7 @@
 
 import jax
 import jax.numpy as jnp
+import numpy as np
 from jax import lax
 from jax.experimental import pallas as pl
 from jax.experimental.pallas import tpu as pltpu
@@ -16,53 +17,54 @@
 RUNS = 4
 STRETCH = HALF // RUNS
 SPAN = 40
+PER = 8
 NT = (((1,), (1,)), ((), ()))
 MESH = pl.DeviceIdType.MESH
 
 
-def twiddle(first, second, length):
-    phase = (first * second % length).astype(jnp.float32) * (2.0 * math.pi / length)
-    scale = 1.0 / math.sqrt(length)
-    return (jnp.cos(phase) * scale, jnp.sin(phase) * scale)
-
-
 def ints(count):
     return jnp.arange(count, dtype=jnp.int32)
 
 
+def twiddle(first, second, length):
+    phase = (first * second % length).astype(np.float32) * np.float32(2.0 * math.pi / length)
+    scale = np.float32(1.0 / math.sqrt(length))
+    return np.cos(phase) * scale, np.sin(phase) * scale
+
+
 def across_table(coils, rows_out, x_here):
     x0 = (KX - rows_out) // 2
-    cosine, sine = twiddle(x0 + ints(rows_out)[:, None], ints(CELLS)[None, :], KX)
-    upper = jnp.stack([cosine, -sine], axis=1)
-    lower = jnp.stack([sine, cosine], axis=1)
-    eye = jnp.eye(coils, dtype=jnp.float32)
+    cosine, sine = twiddle(x0 + np.arange(rows_out)[:, None], np.arange(CELLS)[None, :], KX)
+    upper = np.stack([cosine, -sine], axis=1)
+    lower = np.stack([sine, cosine], axis=1)
+    eye = np.eye(coils, dtype=np.float32)
     tables = []
-    for one in (jnp.stack([upper, lower], axis=1), jnp.stack([-lower, upper], axis=1)):
+    for one in (np.stack([upper, lower], axis=1), np.stack([-lower, upper], axis=1)):
         one = one.reshape(rows_out // x_here, 1, x_here, 2, 1, 2, CELLS)
         one = one * eye[None, :, None, None, :, None, None]
         tables.append(one.reshape(2 * coils * rows_out, 2 * coils * CELLS))
-    return jnp.concatenate(tables, axis=0).astype(jnp.bfloat16)
+    return np.concatenate(tables, axis=0)
 
 
 def right_table(length):
-    cosine, sine = twiddle(ints(length)[:, None], ints(length)[None, :], length)
-    upper = jnp.concatenate([cosine, sine], axis=1)
-    lower = jnp.concatenate([-sine, cosine], axis=1)
-    return jnp.concatenate([upper, lower], axis=0).astype(jnp.bfloat16)
+    cosine, sine = twiddle(np.arange(length)[:, None], np.arange(length)[None, :], length)
+    upper = np.concatenate([cosine, sine], axis=1)
+    lower = np.concatenate([-sine, cosine], axis=1)
+    return jnp.asarray(np.concatenate([upper, lower], axis=0).astype(jnp.bfloat16))
 
 
 def left_table(length):
-    cosine, sine = twiddle(ints(length)[:, None], ints(length)[None, :], length)
-    upper = jnp.concatenate([cosine, -sine], axis=1)
-    lower = jnp.concatenate([sine, cosine], axis=1)
-    return jnp.concatenate([upper, lower], axis=0).astype(jnp.bfloat16)
+    cosine, sine = twiddle(np.arange(length)[:, None], np.arange(length)[None, :], length)
+    upper = np.concatenate([cosine, -sine], axis=1)
+    lower = np.concatenate([sine, cosine], axis=1)
+    return jnp.asarray(np.concatenate([upper, lower], axis=0).astype(jnp.bfloat16))
 
 
 def spread_table(table, values):
-    at = ints(2 * CELLS) % CELLS
+    at = np.arange(2 * CELLS) % CELLS
     cell = CLASSES * (at % CLASSES) + at // CLASSES
     table = table.reshape(table.shape[0], values, CELLS)[:, :, cell]
-    return table.reshape(table.shape[0], values * 2 * CELLS)
+    return jnp.asarray(table.reshape(table.shape[0], values * 2 * CELLS).astype(jnp.bfloat16))
 
 
 def hot_rows(spots, depth):
@@ -315,6 +317,7 @@
     per, lo_ref, more_ref, vals_ref, spot_ref, out_ref, total
 ):
     step = pl.program_id(0)
+    chunks = vals_ref.shape[3] // HALF
     tiles, rows = vals_ref.shape[1], vals_ref.shape[2]
     pairs, depth, freq = out_ref.shape[0], out_ref.shape[1], out_ref.shape[2] // 2
     deep = 16 // rows
@@ -325,8 +328,9 @@
     def _():
         total[...] = jnp.zeros_like(total)
 
-    def pick(part, read):
-        cut = slice(part // 2 * LANES, part // 2 * LANES + LANES)
+    def pick(outer, part, read):
+        start = (outer * per + part // 2 * 2) * HALF
+        cut = pl.ds(pl.multiple_of(start, LANES), LANES)
         out = []
         for t in range(0, tiles, 2):
             first, second = read(t, cut), read(t + 1, cut)
@@ -338,10 +342,10 @@
             out.append(jnp.where(low, first, second))
         return jnp.concatenate(out, axis=1)
 
-    def add(part, start):
-        vals = pick(part, lambda t, cut: vals_ref[0, t, :, cut].astype(jnp.float32))
+    def add(outer, part, start):
+        vals = pick(outer, part, lambda t, cut: vals_ref[0, t, :, cut].astype(jnp.float32))
         vals = jnp.concatenate([vals] * deep, axis=0).astype(jnp.bfloat16)
-        both = pick(part, lambda t, cut: spot_ref[0, t, :, cut])
+        both = pick(outer, part, lambda t, cut: spot_ref[0, t, :, cut])
         base = jnp.full((16, width), start, jnp.int32).astype(jnp.float32)
         plane = jnp.broadcast_to(both[0:1], (16, width)) - base - inner
         plane = plane.astype(jnp.bfloat16)
@@ -359,17 +363,20 @@
         for half in range(freq // LANES):
             total[half, at, :] += moved[:, half * LANES : (half + 1) * LANES]
 
-    for part in range(per):
-        add(part, lo_ref[step * per + part])
-
-    for part in range(per):
-        first = lo_ref[step * per + part]
-
-        def again(at, carry):
-            add(part, first + at * SPAN)
-            return carry
-
-        lax.fori_loop(1, more_ref[step * per + part], again, 0)
+    @pl.loop(0, chunks // per)
+    def _(outer):
+        spot = step * chunks + outer * per
+        for part in range(per):
+            add(outer, part, lo_ref[spot + part])
+
+        for part in range(per):
+            first = lo_ref[spot + part]
+
+            def again(at, carry):
+                add(outer, part, first + at * SPAN)
+                return carry
+
+            lax.fori_loop(1, more_ref[spot + part], again, 0)
 
     @pl.when(step == pl.num_programs(0) - 1)
     def _():
@@ -547,8 +554,7 @@
         name="grid_x",
     )(pos, samples, seg, x_at, table, spot, spots, maps)
 
-    per = math.gcd(chunks, 4)
-    steps = chunks // per
+    per = math.gcd(2 * chunks, PER)
     by_chunk = spots[:, :, 0].reshape(slab_total, tiles, 2 * chunks, HALF)
     step_down = max(8 // each, 1)
     low = jnp.min(by_chunk, axis=(1, 3)).astype(jnp.int32) // step_down * step_down
@@ -556,17 +562,13 @@
     ytab, ztab = right_table(freq), left_table(depth)
     pairs = each // 2
     imaged = pl.pallas_call(
-        functools.partial(add_kernel, 2 * per),
+        functools.partial(add_kernel, per),
         grid_spec=pltpu.PrefetchScalarGridSpec(
             num_scalar_prefetch=2,
-            grid=(slab_total * steps,),
+            grid=(slab_total,),
             in_specs=[
-                pl.BlockSpec(
-                    (1, tiles, each, per * LANES), lambda i, a, b: (i // steps, 0, 0, i % steps)
-                ),
-                pl.BlockSpec(
-                    (1, tiles, 2, per * LANES), lambda i, a, b: (i // steps, 0, 0, i % steps)
-                ),
+                pl.BlockSpec((1, tiles, each, tile), lambda i, a, b: (i, 0, 0, 0)),
+                pl.BlockSpec((1, tiles, 2, tile), lambda i, a, b: (i, 0, 0, 0)),
             ],
             out_specs=pl.BlockSpec((pairs, depth, 2 * freq), lambda i, a, b: (0, 0, 0)),
             scratch_shapes=[

time: 129 us -> 125 us (0.969)
  local copies, waits for them, and re-layouts: 9 us -> 6.9 us
    another operation x4 -> x0, other arithmetic: 2.27 us -> none
    unnamed x15 -> x6, local copies, waits for them, and re-layouts: 2.59 us -> 1.92 us
where the time goes in v5:
time: 125 us; the launch traced here: 123 us
  Pallas kernels  110 us (88%)
  local copies, waits for them, and re-layouts  6.9 us (6%)
  other arithmetic  6.06 us (5%)
    pallas_call x1, Pallas kernels, per_device(): pl.pallas_call(functools.partial(grid_kernel, coils, unroll), grid=(tiles...  48.9 us
    pallas_call x1, Pallas kernels, per_device(): pl.pallas_call(functools.partial(add_kernel, per), grid_spec=pltpu.Prefet...  32.9 us
    pallas_call x1, Pallas kernels, per_device(): pl.pallas_call(image_kernel, in_specs=[memory] * 4, out_specs=memory, out...  22.8 us
    pallas_call x1, Pallas kernels, per_device(): pl.pallas_call(functools.partial(order_kernel, planes, freq), grid=(tiles...  5.8 us

profile of v5, /device:TPU:0, one launch (start us, length us, event | category | flops | bytes accessed | tf_op | source)
XLA Modules:
  0.0 123.5 jit_solution(15546290412759868560)
XLA Ops:
  0.0 0.8 broadcast_multiply_fusion
  0.8 1.4 %fusion.5 = (f32[8192]{0:T(1024)}, f32[8192]{0:T(1024)}, s32[8192]{0:T(1024)}) fusion(s32[8192]{0:T(1024)} %param.12, s32[8192]{0:T(1024)S(1)} %bitcast.13), kind=kLoop, calls=%fused_computation.20 | loop fusion | flops 352256 | bytes 163840 | tf_op jit(solution)/shard_map/convert_element_type | solution.py:488
  2.2 5.8 %order_kz.1 = (f32[1,8192]{1,0:T(1,128)}, f32[4,2,2048]{2,1,0:T(2,128)}) custom-call(f32[1,8192]{1,0:T(1,128)} %bitcast.12, f32[1,8192]{1,0:T(1,128)} %bitcast.11), custom_call_target="tpu_custom_call" | custom-call | tf_op jit(solution)/shard_map/order_kz/pallas_call | solution.py:498
  8.0 0.7 broadcast_in_dim.23.x_ref
  8.8 1.5 %fusion = bf16[8192,64]{0,1:T(8,128)(2,1)S(1)} fusion(bf16[8192,64]{0,1:T(8,128)(2,1)} %param.10, s32[8192]{0:T(1024)} %param.11), kind=kLoop, calls=%fused_computation.1 | loop fusion | flops 1048576 | bytes 2129920 | tf_op jit(solution)/shard_map/jit(_where)/select_n | solution.py:484
  10.2 1.1 copy.14
  11.3 0.0 copy-start
  11.3 1.8 %reshape.55.pos_ref = bf16[4096,128]{1,0:T(8,128)(2,1)} reshape(bf16[8192,64]{1,0:T(8,128)(2,1)S(1)} %copy.14) | data formatting | bytes 2097152 | tf_op jit(solution)/shard_map/reshape | solution.py:484
  13.1 0.0 copy-done
  13.1 0.2 copy.15
  13.4 1.1 copy.18
  14.4 48.9 %grid_x.1 = (bf16[8,4,8,2048]{3,2,1,0:T(8,128)(2,1)}, f32[8,4,2,2048]{3,2,1,0:T(2,128)}, bf16[8,2,2,32,512]{4,3,2,1,0:T(8,128)(2,1)}) custom-call(bf16[4096,128]{1,0:T(8,128)(2,1)} %reshape.55.pos_ref, bf16[2,8192,128]{2,1,0:T(8,128)(2,1)} %val_ref.1, s32[1,8192]{1,0:T(1,128)} %bitcast.10, s32[64,512]{1,0:T(8,128)} %broadcast_in_dim.23.x_ref, ...), custom_call_target="tpu_custom_call" | custom-call | tf_op jit(solution)/shard_map/grid_x/pallas_call | solution.py:518
  63.4 1.5 %slice_reduce_fusion = (f32[8,2048]{1,0:T(8,128)S(1)}, f32[8,2048]{1,0:T(8,128)S(1)}) fusion(f32[8,4,2,2048]{3,2,1,0:T(2,128)} %get-tuple-element.12.spot_ref), kind=kLoop, calls=%fused_computation.3 | loop fusion | flops 98304 | bytes 393216 | tf_op jit(solution)/shard_map/reduce_max | solution.py:561
  64.9 0.1 reduce_max.14
  65.0 0.1 reduce_max.18
  65.1 0.1 convert_element_type.28
  65.2 0.1 reduce_min.14
  65.3 0.1 reduce_min.18
  65.4 0.1 convert_element_type.26.lo_ref
  65.5 0.0 copy-start.1
  65.5 0.6 fusion.8.more_ref
  66.1 0.0 copy-done.1
  66.1 32.9 %add_yz.1.rows_ref = bf16[4,256,512]{2,1,0:T(8,128)(2,1)} custom-call(s32[256]{0:T(256)} %copy-done.1, s32[256]{0:T(256)} %fusion.8.more_ref, bf16[8,4,8,2048]{3,2,1,0:T(8,128)(2,1)} %get-tuple-element.13.vals_ref, f32[8,4,2,2048]{3,2,1,0:T(2,128)} %get-tuple-element.12.spot_ref), custom_call_target="tpu_custom_call" | custom-call | tf_op jit(solution)/shard_map/add_yz/pallas_call | solution.py:564
  99.0 22.8 %image_sum.1 = f32[32,4,512]{2,1,0:T(4,128)} custom-call(bf16[4,256,512]{2,1,0:T(8,128)(2,1)} %add_yz.1.rows_ref, bf16[8,2,2,32,512]{4,3,2,1,0:T(8,128)(2,1)} %get-tuple-element.14.map_ref, bf16[512,512]{1,0:T(8,128)(2,1)} %constant.124.clone.ytab_ref, bf16[512,512]{1,0:T(8,128)(2,1)} %constant.125.clone.ztab_ref), custom_call_target="tpu_custom_call" | custom-call | tf_op jit(solution)/shard_map/image_sum/pallas_call | solution.py:584
  121.8 1.7 %copy.20 = f32[32,4,512]{2,1,0:T(4,128)} copy(f32[32,4,512]{2,1,0:T(4,128)} %image_sum.1) | data formatting | bytes 524288
  (3 shorter events, 0.0 us)
Async XLA Ops:
  11.3 1.8 %copy-start = (bf16[8,32,4,512]{3,2,1,0:T(4,128)(2,1)S(1)}, bf16[8,32,4,512]{3,2,1,0:T(4,128)(2,1)}, u32[]{:S(2)}) copy-start(bf16[8,32,4,512]{3,2,1,0:T(4,128)(2,1)} %param.14) | copy-start | bytes 3145732
  65.5 0.6 copy-start.1

commit v6 on v5

--- a/solution.py
+++ b/solution.py
@@ -13,17 +13,13 @@
 CELLS = 64
 CLASSES = 8
 LANES = 128
-HALF = LANES // 2
 RUNS = 4
-STRETCH = HALF // RUNS
-SPAN = 40
+STRETCH = LANES // RUNS
+SPAN = 56
 PER = 8
+DEAD = 9984.0
 NT = (((1,), (1,)), ((), ()))
 MESH = pl.DeviceIdType.MESH
-
-
-def ints(count):
-    return jnp.arange(count, dtype=jnp.int32)
 
 
 def twiddle(first, second, length):
@@ -89,8 +85,8 @@
 
 def regroup(runs):
     rows, length = runs[0].shape
-    place = lax.broadcasted_iota(jnp.int32, (rows, LANES), 1) % HALF // STRETCH
-    for at in range(length // (2 * STRETCH)):
+    place = lax.broadcasted_iota(jnp.int32, (rows, LANES), 1) // STRETCH
+    for at in range(length // STRETCH):
         cut = slice(at // RUNS * LANES, at // RUNS * LANES + LANES)
         out = runs[0][:, cut]
         for run in range(1, RUNS):
@@ -98,39 +94,29 @@
         yield at, out
 
 
-def order_kernel(planes, freq, kz_ref, ky_ref, spot_ref, sorted_ref):
-    tile = kz_ref.shape[1]
-    length = tile // RUNS
+def order(kz, run):
+    length = kz.shape[1]
     pieces = length // LANES
-    runs = []
-    for run in range(RUNS):
-        cut = slice(run * length, (run + 1) * length)
-        kz, ky = kz_ref[:, cut], ky_ref[:, cut]
-        lane = lax.broadcasted_iota(jnp.int32, (1, length), 1).astype(jnp.float32)
-        key = kz * float(length) + lane
-        rank = jnp.zeros((1, length), jnp.float32)
-        for piece in range(pieces):
-            part = key[:, piece * LANES : (piece + 1) * LANES]
-            part = jnp.broadcast_to(part, (LANES, LANES)).T
-            part = jnp.concatenate([part] * pieces, axis=1)
-            rank = rank + jnp.sum(jnp.where(part < key, 1.0, 0.0), axis=0, keepdims=True)
-        rank = rank.astype(jnp.int32)
-        seat = rank // (2 * STRETCH)
-        spot = seat // RUNS * LANES + rank // STRETCH % 2 * HALF
-        spot = spot + (seat + run) % RUNS * STRETCH + rank % STRETCH
-        spot = spot.astype(jnp.float32)
-        spot_ref[:, cut] = spot
-        both = jnp.concatenate([kz, ky, jnp.zeros((14, length), jnp.float32)], axis=0)
-        runs.append(permute(both.astype(jnp.bfloat16), spot))
-    for at, out in regroup(runs):
-        sorted_ref[0, :, at * LANES : (at + 1) * LANES] = out[:2]
+    lane = lax.broadcasted_iota(jnp.int32, (1, length), 1).astype(jnp.float32)
+    key = kz * float(length) + lane
+    rank = jnp.zeros((1, length), jnp.float32)
+    for piece in range(pieces):
+        part = key[:, piece * LANES : (piece + 1) * LANES]
+        part = jnp.broadcast_to(part, (LANES, LANES)).T
+        part = jnp.concatenate([part] * pieces, axis=1)
+        rank = rank + jnp.sum(jnp.where(part < key, 1.0, 0.0), axis=0, keepdims=True)
+    rank = rank.astype(jnp.int32)
+    seat = rank // STRETCH
+    spot = seat // RUNS * LANES + (seat + run) % RUNS * STRETCH + rank % STRETCH
+    return spot.astype(jnp.float32)
 
 
 def grid_kernel(
-    coils, unroll, pos_ref, val_ref, seg_ref, x_ref, tab_ref, spot_ref, spots_ref, map_ref,
-    lines_ref, every_ref, maps_ref,
-    cells, near, bump, placed, ready, line_out, line_in, line_own,
-    spots_out, spots_in, spots_own, map_out, map_in, map_own,
+    coils, unroll, planes, freq, pos_ref, count_ref, block_ref, slab_ref, val_ref, tab_ref, map_ref,
+    lines_ref, every_ref, limits_ref, maps_ref,
+    flat, cells, near, bump, placed, ready, spots, least, most, limits,
+    line_out, line_in, line_own, spots_out, spots_in, spots_own,
+    limit_out, limit_in, limit_own, map_out, map_in, map_own,
 ):
     turn_at = pl.program_id(0)
     tiles, slabs, each, tile = ready.shape
@@ -152,15 +138,25 @@
             ready.at[at, slab], lines_ref.at[slab, at], line_own.at[at]
         )
 
-    def spots_copy(hop):
+    def spots_copy(at, hop):
         peer = lax.rem(slab + hop, slabs)
         return pltpu.make_async_remote_copy(
-            spots_ref, every_ref.at[slab], spots_out.at[hop], spots_in.at[hop],
+            spots.at[at], every_ref.at[slab, at], spots_out.at[at, hop], spots_in.at[at, hop],
             device_id={"slab": peer}, device_id_type=MESH,
         )
 
-    def spots_keep():
-        return pltpu.make_async_copy(spots_ref, every_ref.at[slab], spots_own)
+    def spots_keep(at):
+        return pltpu.make_async_copy(spots.at[at], every_ref.at[slab, at], spots_own.at[at])
+
+    def limit_copy(hop):
+        peer = lax.rem(slab + hop, slabs)
+        return pltpu.make_async_remote_copy(
+            limits, limits_ref.at[slab], limit_out.at[hop], limit_in.at[hop],
+            device_id={"slab": peer}, device_id_type=MESH,
+        )
+
+    def limit_keep():
+        return pltpu.make_async_copy(limits, limits_ref.at[slab], limit_own)
 
     def map_copy(deal, share):
         return pltpu.make_async_remote_copy(
@@ -197,11 +193,27 @@
                     device_id_type=MESH,
                 )
     length = tile // RUNS
+    chunks = tile // LANES
+
+    for piece in range(chunks):
+        cut = slice(piece * LANES, (piece + 1) * LANES)
+        live = lax.broadcasted_iota(jnp.int32, (CELLS, LANES), 0) < count_ref[:, cut]
+        place = jnp.where(live, pos_ref[:, cut].astype(jnp.float32), DEAD)
+        both = jnp.concatenate([place, pltpu.roll(place, LANES - 8, 1)], axis=0)
+        flat[cut, :] = both.T
+
+    segments = KX // CELLS
+    kz = slab_ref[...] * planes + block_ref[...] // (segments * freq)
+    ky = block_ref[...] // segments % freq
+    seg = block_ref[...] % segments
+    kz, ky = kz.astype(jnp.float32), ky.astype(jnp.float32)
+
     block = lax.broadcasted_iota(jnp.int32, (16, LANES), 0)
     upper = lax.broadcasted_iota(jnp.int32, (16, LANES), 1) >= CELLS
-    odd = block % 2 == 1
-    own = [block % 4 // 2 == half for half in range(2)]
-    mine = block // 4 % 2 == upper.astype(jnp.int32)
+    odd = block >= 8
+    own = [block % 2 == half for half in range(2)]
+    head = block % 8 < 4
+    mine = block % 4 // 2 == upper.astype(jnp.int32)
     level = lax.broadcasted_iota(jnp.int32, (CLASSES, LANES), 0).astype(jnp.float32)
 
     def step(g, slot):
@@ -216,7 +228,7 @@
                 )
                 halves = [jnp.where(own[half], placed_here, 0.0) for half in range(2)]
                 left.append(jnp.concatenate(halves, axis=1).astype(jnp.bfloat16))
-        place = pos_ref[pl.ds(pl.multiple_of(g * 8, 8), 8), :].astype(jnp.float32) * 0.125
+        place = flat[pl.ds(pl.multiple_of(g * 16, 16), 8), :] * 0.125
         for r in range(CLASSES):
             offset = place - ((r + 0.5) * 0.125 - 0.5)
             seat = jnp.floor(offset)
@@ -243,9 +255,9 @@
             preferred_element_type=jnp.float32,
         )
         for v in range(2 * coils):
-            first = done[16 * v : 16 * v + 8, :LANES]
-            second = done[16 * v + 8 : 16 * v + 16, LANES:]
-            both = jnp.where(mine, jnp.concatenate([first, second], axis=0), 0.0)
+            rows16 = slice(16 * v, 16 * v + 16)
+            both = jnp.where(head, done[rows16, :LANES], done[rows16, LANES:])
+            both = jnp.where(mine, both, 0.0)
             cells[at, LANES * v : LANES * (v + 1)] = both.astype(jnp.bfloat16)
 
     @pl.loop(0, tile // (16 * unroll))
@@ -253,27 +265,53 @@
         for slot in range(unroll):
             step(outer * unroll + slot, slot)
 
+    wide = 2 * coils
+    x_here = each // wide
+    line = lax.broadcasted_iota(jnp.int32, (rows, LANES), 0)
+    x_at = line // each * x_here + line // 2 % x_here + (KX - rows // wide) // 2
+    x_at = jnp.concatenate([x_at] * (length // LANES), axis=1)
+    pad = jnp.zeros((14, length), jnp.float32)
     for run in range(RUNS):
         cut = slice(run * length, (run + 1) * length)
         moved = lax.dot_general(
             tab_ref[...], cells[cut, :], NT, preferred_element_type=jnp.float32
         )
-        turn = (x_ref[...] * seg_ref[:, cut]) & 3
+        turn = (x_at * seg[:, cut]) & 3
         turned = jnp.where((turn & 1) == 0, moved[:rows], moved[rows:])
-        turned = jnp.where(turn >= 2, -turned, turned).astype(jnp.bfloat16)
-        placed[run] = permute(turned, spot_ref[:, cut]).astype(jnp.bfloat16)
+        turned = jnp.where(turn >= 2, -turned, turned)
+        turned = jnp.concatenate([turned, kz[:, cut], ky[:, cut], pad], axis=0)
+        spot = order(kz[:, cut], run)
+        placed[run] = permute(turned.astype(jnp.bfloat16), spot).astype(jnp.bfloat16)
+
+    @pl.when(turn_at == 0)
+    def _():
+        least[...] = jnp.full_like(least, 1.0e4)
+        most[...] = jnp.zeros_like(most)
+
     for at, out in regroup([placed.at[run] for run in range(RUNS)]):
         for owner in range(slabs):
             ready[turn_at, owner, :, at * LANES : (at + 1) * LANES] = out[
                 owner * each : (owner + 1) * each
             ]
+        found = out[rows : rows + 2].astype(jnp.float32)
+        spots[turn_at, :, at * LANES : (at + 1) * LANES] = found
+        least[at : at + 1] = jnp.minimum(least[at : at + 1], found[0:1])
+        most[at : at + 1] = jnp.maximum(most[at : at + 1], found[0:1])
+
+    @pl.when(turn_at == tiles - 1)
+    def _():
+        step_down = max(8 // each, 1)
+        low = jnp.min(least[...].T, axis=0, keepdims=True).astype(jnp.int32)
+        low = low // step_down * step_down
+        high = jnp.max(most[...].T, axis=0, keepdims=True).astype(jnp.int32)
+        high = (high - low) // SPAN + 1
+        limits[0:1] = low
+        limits[1:2] = high
+        limits[2:] = jnp.zeros((6, LANES), jnp.int32)
 
     @pl.when(turn_at == 0)
     def _():
         pl.semaphore_wait(barrier, slabs - 1 + deals * shares - here.astype(jnp.int32))
-        spots_keep().start()
-        for hop in range(1, slabs):
-            spots_copy(hop).start()
         for deal in range(deals):
             for share in range(shares):
                 @pl.when(jnp.logical_not(is_me(deal, share)))
@@ -286,13 +324,15 @@
 
     for hop in range(1, slabs):
         line_copy(turn_at, hop).start()
+        spots_copy(turn_at, hop).start()
     line_keep(turn_at).start()
+    spots_keep(turn_at).start()
 
     @pl.when(turn_at == tiles - 1)
     def _():
-        spots_keep().wait()
         for hop in range(1, slabs):
-            spots_copy(hop).wait()
+            limit_copy(hop).start()
+        limit_keep().start()
         for deal in range(deals):
             for share in range(shares):
                 @pl.when(jnp.logical_not(is_me(deal, share)))
@@ -309,19 +349,24 @@
 
         for at in range(tiles):
             line_keep(at).wait()
+            spots_keep(at).wait()
             for hop in range(1, slabs):
                 line_copy(at, hop).wait()
+                spots_copy(at, hop).wait()
+        limit_keep().wait()
+        for hop in range(1, slabs):
+            limit_copy(hop).wait()
 
 
 def add_kernel(
-    per, lo_ref, more_ref, vals_ref, spot_ref, out_ref, total
+    per, limit_ref, vals_ref, spot_ref, out_ref, total
 ):
     step = pl.program_id(0)
-    chunks = vals_ref.shape[3] // HALF
+    chunks = vals_ref.shape[3] // LANES
     tiles, rows = vals_ref.shape[1], vals_ref.shape[2]
     pairs, depth, freq = out_ref.shape[0], out_ref.shape[1], out_ref.shape[2] // 2
     deep = 16 // rows
-    width = tiles * HALF
+    width = tiles * LANES
     inner = (lax.broadcasted_iota(jnp.int32, (16, width), 0) // rows).astype(jnp.float32)
 
     @pl.when(step == 0)
@@ -329,22 +374,12 @@
         total[...] = jnp.zeros_like(total)
 
     def pick(outer, part, read):
-        start = (outer * per + part // 2 * 2) * HALF
-        cut = pl.ds(pl.multiple_of(start, LANES), LANES)
-        out = []
-        for t in range(0, tiles, 2):
-            first, second = read(t, cut), read(t + 1, cut)
-            low = lax.broadcasted_iota(jnp.int32, first.shape, 1) < HALF
-            if part % 2 == 0:
-                second = pltpu.roll(second, HALF, 1)
-            else:
-                first = pltpu.roll(first, HALF, 1)
-            out.append(jnp.where(low, first, second))
-        return jnp.concatenate(out, axis=1)
+        cut = pl.ds(pl.multiple_of((outer * per + part) * LANES, LANES), LANES)
+        return jnp.concatenate([read(t, cut) for t in range(tiles)], axis=1)
 
     def add(outer, part, start):
-        vals = pick(outer, part, lambda t, cut: vals_ref[0, t, :, cut].astype(jnp.float32))
-        vals = jnp.concatenate([vals] * deep, axis=0).astype(jnp.bfloat16)
+        vals = pick(outer, part, lambda t, cut: vals_ref[0, t, :, cut])
+        vals = jnp.concatenate([vals] * deep, axis=0)
         both = pick(outer, part, lambda t, cut: spot_ref[0, t, :, cut])
         base = jnp.full((16, width), start, jnp.int32).astype(jnp.float32)
         plane = jnp.broadcast_to(both[0:1], (16, width)) - base - inner
@@ -365,18 +400,17 @@
 
     @pl.loop(0, chunks // per)
     def _(outer):
-        spot = step * chunks + outer * per
         for part in range(per):
-            add(outer, part, lo_ref[spot + part])
+            add(outer, part, limit_ref[step, 0, outer * per + part])
 
         for part in range(per):
-            first = lo_ref[spot + part]
+            first = limit_ref[step, 0, outer * per + part]
 
             def again(at, carry):
                 add(outer, part, first + at * SPAN)
                 return carry
 
-            lax.fori_loop(1, more_ref[spot + part], again, 0)
+            lax.fori_loop(1, limit_ref[step, 1, outer * per + part], again, 0)
 
     @pl.when(step == pl.num_programs(0) - 1)
     def _():
@@ -478,15 +512,6 @@
     depth = planes * slab_total
     freq = sensitivity.shape[3] // 2
     x_here = rows_out // slab_total
-    segments = KX // CELLS
-
-    live = ints(CELLS)[None, :] < block_count[:, None]
-    pos = jnp.where(live, sample_pos, 9984.0).reshape(blocks // 2, 2 * CELLS)
-    seg = (grid_block % segments)[None, :]
-    kz = block_slab[:, 0] * planes + grid_block // (segments * freq)
-    ky = grid_block // segments % freq
-    kz, ky = kz.astype(jnp.float32)[None, :], ky.astype(jnp.float32)[None, :]
-
     tile = math.gcd(blocks, 2048)
     tiles = blocks // tile
     chunks = tile // LANES
@@ -495,51 +520,45 @@
     each = 2 * coils * x_here
 
     row = pl.BlockSpec((1, tile), lambda b: (0, b))
-    spot, spots = pl.pallas_call(
-        functools.partial(order_kernel, planes, freq),
-        grid=(tiles,),
-        in_specs=[row, row],
-        out_specs=[row, pl.BlockSpec((1, 2, tile), lambda b: (b, 0, 0))],
-        out_shape=[
-            jax.ShapeDtypeStruct((1, blocks), jnp.float32),
-            jax.ShapeDtypeStruct((tiles, 2, tile), jnp.float32),
-        ],
-        name="order_kz",
-    )(kz, ky)
-
     table = spread_table(across_table(coils, rows_out, x_here), 2 * coils)
-    x_at = (ints(count) // (2 * coils * x_here)) * x_here + ints(count) // 2 % x_here
-    x_at = jnp.broadcast_to((x_at + (KX - rows_out) // 2)[:, None], (count, tile // RUNS))
     x_own = sensitivity.shape[2]
     maps = sensitivity.reshape(
         coil_total, coils, planes, x_own // x_here, x_here, 2 * freq
     ).transpose(0, 3, 1, 4, 2, 5)
     anywhere = pl.BlockSpec(memory_space=pl.ANY)
-    sent, spots, maps = pl.pallas_call(
-        functools.partial(grid_kernel, coils, unroll),
+    sent, spots, limits, maps = pl.pallas_call(
+        functools.partial(grid_kernel, coils, unroll, planes, freq),
         grid=(tiles,),
         in_specs=[
-            pl.BlockSpec((tile // 2, LANES), lambda b: (b, 0)),
+            pl.BlockSpec((CELLS, tile), lambda b: (0, b)),
+            row,
+            row,
+            row,
             pl.BlockSpec((coils, tile, LANES), lambda b: (0, b, 0)),
-            row,
-            pl.BlockSpec(x_at.shape, lambda b: (0, 0)),
             pl.BlockSpec(table.shape, lambda b: (0, 0)),
-            row,
-            pl.BlockSpec(spots.shape, lambda b: (0, 0, 0)),
             anywhere,
         ],
-        out_specs=[anywhere] * 3,
+        out_specs=[anywhere] * 4,
         out_shape=[
             jax.ShapeDtypeStruct((slab_total, tiles, each, tile), jnp.bfloat16),
-            jax.ShapeDtypeStruct((slab_total,) + spots.shape, jnp.float32),
+            jax.ShapeDtypeStruct((slab_total, tiles, 2, tile), jnp.float32),
+            jax.ShapeDtypeStruct((slab_total, 8, LANES), jnp.int32),
             jax.ShapeDtypeStruct((slab_total,) + maps.shape[2:], jnp.bfloat16),
         ],
         scratch_shapes=[
+            pltpu.VMEM((tile, LANES), jnp.float32),
             pltpu.VMEM((tile, 2 * coils * LANES), jnp.bfloat16),
             pltpu.VMEM((unroll, CLASSES, 8, LANES), jnp.float32),
             pltpu.VMEM((unroll, CLASSES, 8, LANES), jnp.float32),
-            pltpu.VMEM((RUNS, count, tile // RUNS), jnp.bfloat16),
+            pltpu.VMEM((RUNS, count + 16, tile // RUNS), jnp.bfloat16),
             pltpu.VMEM((tiles, slab_total, each, tile), jnp.bfloat16),
+            pltpu.VMEM((tiles, 2, tile), jnp.float32),
+            pltpu.VMEM((LANES, LANES), jnp.float32),
+            pltpu.VMEM((LANES, LANES), jnp.float32),
+            pltpu.VMEM((8, LANES), jnp.int32),
+            pltpu.SemaphoreType.DMA((tiles, slab_total)),
+            pltpu.SemaphoreType.DMA((tiles, slab_total)),
+            pltpu.SemaphoreType.DMA((tiles,)),
             pltpu.SemaphoreType.DMA((tiles, slab_total)),
             pltpu.SemaphoreType.DMA((tiles, slab_total)),
             pltpu.SemaphoreType.DMA((tiles,)),
@@ -552,32 +571,36 @@
         ],
         compiler_params=pltpu.CompilerParams(collective_id=0, has_side_effects=True),
         name="grid_x",
-    )(pos, samples, seg, x_at, table, spot, spots, maps)
-
-    per = math.gcd(2 * chunks, PER)
-    by_chunk = spots[:, :, 0].reshape(slab_total, tiles, 2 * chunks, HALF)
-    step_down = max(8 // each, 1)
-    low = jnp.min(by_chunk, axis=(1, 3)).astype(jnp.int32) // step_down * step_down
-    high = (jnp.max(by_chunk, axis=(1, 3)).astype(jnp.int32) - low) // SPAN + 1
+    )(
+        sample_pos.T,
+        block_count[None, :],
+        grid_block[None, :],
+        block_slab.reshape(1, blocks),
+        samples,
+        table,
+        maps,
+    )
+
+    per = math.gcd(chunks, PER)
     ytab, ztab = right_table(freq), left_table(depth)
     pairs = each // 2
     imaged = pl.pallas_call(
         functools.partial(add_kernel, per),
         grid_spec=pltpu.PrefetchScalarGridSpec(
-            num_scalar_prefetch=2,
+            num_scalar_prefetch=1,
             grid=(slab_total,),
             in_specs=[
-                pl.BlockSpec((1, tiles, each, tile), lambda i, a, b: (i, 0, 0, 0)),
-                pl.BlockSpec((1, tiles, 2, tile), lambda i, a, b: (i, 0, 0, 0)),
+                pl.BlockSpec((1, tiles, each, tile), lambda i, a: (i, 0, 0, 0)),
+                pl.BlockSpec((1, tiles, 2, tile), lambda i, a: (i, 0, 0, 0)),
             ],
-            out_specs=pl.BlockSpec((pairs, depth, 2 * freq), lambda i, a, b: (0, 0, 0)),
+            out_specs=pl.BlockSpec((pairs, depth, 2 * freq), lambda i, a: (0, 0, 0)),
             scratch_shapes=[
                 pltpu.VMEM((freq // LANES, (depth + SPAN) * each, LANES), jnp.float32)
             ],
         ),
         out_shape=jax.ShapeDtypeStruct((pairs, depth, 2 * freq), jnp.bfloat16),
         name="add_yz",
-    )(low.reshape(-1), high.reshape(-1), sent, spots)
+    )(limits, sent, spots)
 
     shares = x_own // x_here
     memory = pl.BlockSpec(memory_space=pltpu.VMEM)

time: 125 us -> 109 us (0.87); the launches traced: 123 us -> 109 us
  other arithmetic: 6.06 us -> 0 us
  Pallas kernels: 110 us -> 105 us
  local copies, waits for them, and re-layouts: 6.9 us -> 4.2 us
    pallas_call x1, Pallas kernels: 32.9 us -> 28.2 us  [per_device(): pl.pallas_call(functools.partial(add_kernel, per), grid_spec=pltpu.Prefet...]
    reshape x1 -> x0, local copies, waits for them, and re-layouts: 1.8 us -> none  [per_device(): pos = jnp.where(live, sample_pos, 9984.0).reshape(blocks // 2, 2 * CELLS)]
    reduce_max x2 -> x0, other arithmetic: 1.65 us -> none  [per_device(): high = (jnp.max(by_chunk, axis=(1, 3)).astype(jnp.int32) - low) // SPAN + 1]
    select_n x1 -> x0, other arithmetic: 1.47 us -> none  [per_device(): pos = jnp.where(live, sample_pos, 9984.0).reshape(blocks // 2, 2 * CELLS)]
    convert_element_type x3 -> x0, other arithmetic: 1.45 us -> none  [the longest x1 1.44 us: per_device(): kz, ky = (kz.astype(jnp.float32)[None, :], ky.astype(jnp.float32)[None, :])]
    unnamed x6 -> x2, local copies, waits for them, and re-layouts: 1.92 us -> 3.13 us
    pallas_call x2 -> x1, Pallas kernels: 54.7 us -> 54.5 us  [per_device(): pl.pallas_call(functools.partial(grid_kernel, coils, unroll, planes, freq...]
where the time goes in v6:
time: 109 us
  Pallas kernels  105 us (96%)
  local copies, waits for them, and re-layouts  4.2 us (4%)
    pallas_call x1, Pallas kernels, per_device(): pl.pallas_call(functools.partial(grid_kernel, coils, unroll, planes, freq...  54.5 us
    pallas_call x1, Pallas kernels, per_device(): pl.pallas_call(functools.partial(add_kernel, per), grid_spec=pltpu.Prefet...  28.2 us
    pallas_call x1, Pallas kernels, per_device(): pl.pallas_call(image_kernel, in_specs=[memory] * 4, out_specs=memory, out...  22.2 us
    unnamed x2, local copies, waits for them, and re-layouts  3.13 us

profile of v6, /device:TPU:0, one launch (start us, length us, event | category | flops | bytes accessed | tf_op | source)
XLA Modules:
  0.0 109.2 jit_solution(18280240367018275658)
XLA Ops:
  0.0 1.5 %copy.10 = bf16[8,32,4,512]{3,1,2,0:T(8,128)(2,1)S(1)} copy(bf16[8,32,4,512]{3,2,1,0:T(4,128)(2,1)} %param.14) | data formatting | bytes 2097152 | tf_op args[5]
  1.5 1.1 copy.13
  2.5 54.5 %grid_x.1 = (bf16[8,4,8,2048]{3,2,1,0:T(8,128)(2,1)}, f32[8,4,2,2048]{3,2,1,0:T(2,128)}, s32[8,8,128]{2,1,0:T(8,128)}, bf16[8,2,2,32,512]{4,3,2,1,0:T(8,128)(2,1)}) custom-call(bf16[64,8192]{1,0:T(8,128)(2,1)} %bitcast.10, s32[1,8192]{1,0:T(1,128)} %bitcast.11, s32[1,8192]{1,0:T(1,128)} %bitcast.12, s32[1,8192]{1,0:T(1,128)} %bitcast.13, ...), custom_call_target="tpu_custom_call" | custom-call | tf_op jit(solution)/shard_map/grid_x/pallas_call | solution.py:529
  57.0 28.2 %add_yz.1.rows_ref = bf16[4,256,512]{2,1,0:T(8,128)(2,1)} custom-call(s32[8,8,128]{2,1,0:T(8,128)} %get-tuple-element.9.limit_ref, bf16[8,4,8,2048]{3,2,1,0:T(8,128)(2,1)} %get-tuple-element.10.vals_ref, f32[8,4,2,2048]{3,2,1,0:T(2,128)} %get-tuple-element.11.spot_ref), custom_call_target="tpu_custom_call" | custom-call | tf_op jit(solution)/shard_map/add_yz/pallas_call | solution.py:587
  85.3 22.2 %image_sum.1 = f32[32,4,512]{2,1,0:T(4,128)} custom-call(bf16[4,256,512]{2,1,0:T(8,128)(2,1)} %add_yz.1.rows_ref, bf16[8,2,2,32,512]{4,3,2,1,0:T(8,128)(2,1)} %get-tuple-element.12.map_ref, bf16[512,512]{1,0:T(8,128)(2,1)} %constant.7.clone.ytab_ref, bf16[512,512]{1,0:T(8,128)(2,1)} %constant.8.clone.ztab_ref), custom_call_target="tpu_custom_call" | custom-call | tf_op jit(solution)/shard_map/image_sum/pallas_call | solution.py:607
  107.5 1.7 %copy.15 = f32[32,4,512]{2,1,0:T(4,128)} copy(f32[32,4,512]{2,1,0:T(4,128)} %image_sum.1) | data formatting | bytes 524288

commit v7 on v6

--- a/solution.py
+++ b/solution.py
@@ -16,7 +16,7 @@
 RUNS = 4
 STRETCH = LANES // RUNS
 SPAN = 56
-PER = 8
+PER = 16
 DEAD = 9984.0
 NT = (((1,), (1,)), ((), ()))
 MESH = pl.DeviceIdType.MESH
@@ -121,7 +121,7 @@
     turn_at = pl.program_id(0)
     tiles, slabs, each, tile = ready.shape
     rows = slabs * each
-    deals, shares = map_ref.shape[0], map_ref.shape[1]
+    deals, shares = map_ref.shape[0], map_ref.shape[2]
     slab, coil = lax.axis_index("slab"), lax.axis_index("coil")
     barrier = pltpu.get_barrier_semaphore()
     here = slab // shares == coil
@@ -160,20 +160,20 @@
 
     def map_copy(deal, share):
         return pltpu.make_async_remote_copy(
-            map_ref.at[deal, share], maps_ref.at[slab],
+            map_ref.at[deal, :, share], maps_ref.at[slab],
             map_out.at[deal, share], map_in.at[slab],
             device_id={"slab": coil * shares + share, "coil": deal}, device_id_type=MESH,
         )
 
     def map_take(source):
         return pltpu.make_async_remote_copy(
-            map_ref.at[0, 0], maps_ref.at[source], map_out.at[0, 0], map_in.at[source],
+            map_ref.at[0, :, 0], maps_ref.at[source], map_out.at[0, 0], map_in.at[source],
             device_id={"slab": slab, "coil": coil}, device_id_type=MESH,
         )
 
     def map_keep():
         return pltpu.make_async_copy(
-            map_ref.at[coil, lax.rem(slab, shares)], maps_ref.at[slab], map_own
+            map_ref.at[coil, :, lax.rem(slab, shares)], maps_ref.at[slab], map_own
         )
 
     def is_me(deal, share):
@@ -265,6 +265,19 @@
         for slot in range(unroll):
             step(outer * unroll + slot, slot)
 
+        @pl.when(jnp.logical_and(turn_at == 0, outer == 0))
+        def _():
+            pl.semaphore_wait(barrier, slabs - 1 + deals * shares - here.astype(jnp.int32))
+            for deal in range(deals):
+                for share in range(shares):
+                    @pl.when(jnp.logical_not(is_me(deal, share)))
+                    def _():
+                        map_copy(deal, share).start()
+
+            @pl.when(here)
+            def _():
+                map_keep().start()
+
     wide = 2 * coils
     x_here = each // wide
     line = lax.broadcasted_iota(jnp.int32, (rows, LANES), 0)
@@ -293,8 +306,9 @@
             ready[turn_at, owner, :, at * LANES : (at + 1) * LANES] = out[
                 owner * each : (owner + 1) * each
             ]
-        found = out[rows : rows + 2].astype(jnp.float32)
+        found = out[rows : rows + 2]
         spots[turn_at, :, at * LANES : (at + 1) * LANES] = found
+        found = found.astype(jnp.float32)
         least[at : at + 1] = jnp.minimum(least[at : at + 1], found[0:1])
         most[at : at + 1] = jnp.maximum(most[at : at + 1], found[0:1])
 
@@ -308,19 +322,6 @@
         limits[0:1] = low
         limits[1:2] = high
         limits[2:] = jnp.zeros((6, LANES), jnp.int32)
-
-    @pl.when(turn_at == 0)
-    def _():
-        pl.semaphore_wait(barrier, slabs - 1 + deals * shares - here.astype(jnp.int32))
-        for deal in range(deals):
-            for share in range(shares):
-                @pl.when(jnp.logical_not(is_me(deal, share)))
-                def _():
-                    map_copy(deal, share).start()
-
-        @pl.when(here)
-        def _():
-            map_keep().start()
 
     for hop in range(1, slabs):
         line_copy(turn_at, hop).start()
@@ -380,7 +381,7 @@
     def add(outer, part, start):
         vals = pick(outer, part, lambda t, cut: vals_ref[0, t, :, cut])
         vals = jnp.concatenate([vals] * deep, axis=0)
-        both = pick(outer, part, lambda t, cut: spot_ref[0, t, :, cut])
+        both = pick(outer, part, lambda t, cut: spot_ref[0, t, :, cut].astype(jnp.float32))
         base = jnp.full((16, width), start, jnp.int32).astype(jnp.float32)
         plane = jnp.broadcast_to(both[0:1], (16, width)) - base - inner
         plane = plane.astype(jnp.bfloat16)
@@ -403,14 +404,16 @@
         for part in range(per):
             add(outer, part, limit_ref[step, 0, outer * per + part])
 
-        for part in range(per):
+        def extra(part, carry):
             first = limit_ref[step, 0, outer * per + part]
 
             def again(at, carry):
                 add(outer, part, first + at * SPAN)
                 return carry
 
-            lax.fori_loop(1, limit_ref[step, 1, outer * per + part], again, 0)
+            return lax.fori_loop(1, limit_ref[step, 1, outer * per + part], again, carry)
+
+        lax.fori_loop(0, per, extra, 0)
 
     @pl.when(step == pl.num_programs(0) - 1)
     def _():
@@ -524,7 +527,7 @@
     x_own = sensitivity.shape[2]
     maps = sensitivity.reshape(
         coil_total, coils, planes, x_own // x_here, x_here, 2 * freq
-    ).transpose(0, 3, 1, 4, 2, 5)
+    ).transpose(0, 1, 3, 4, 2, 5)
     anywhere = pl.BlockSpec(memory_space=pl.ANY)
     sent, spots, limits, maps = pl.pallas_call(
         functools.partial(grid_kernel, coils, unroll, planes, freq),
@@ -541,9 +544,9 @@
         out_specs=[anywhere] * 4,
         out_shape=[
             jax.ShapeDtypeStruct((slab_total, tiles, each, tile), jnp.bfloat16),
-            jax.ShapeDtypeStruct((slab_total, tiles, 2, tile), jnp.float32),
+            jax.ShapeDtypeStruct((slab_total, tiles, 2, tile), jnp.bfloat16),
             jax.ShapeDtypeStruct((slab_total, 8, LANES), jnp.int32),
-            jax.ShapeDtypeStruct((slab_total,) + maps.shape[2:], jnp.bfloat16),
+            jax.ShapeDtypeStruct((slab_total, coils) + maps.shape[3:], jnp.bfloat16),
         ],
         scratch_shapes=[
             pltpu.VMEM((tile, LANES), jnp.float32),
@@ -552,7 +555,7 @@
             pltpu.VMEM((unroll, CLASSES, 8, LANES), jnp.float32),
             pltpu.VMEM((RUNS, count + 16, tile // RUNS), jnp.bfloat16),
             pltpu.VMEM((tiles, slab_total, each, tile), jnp.bfloat16),
-            pltpu.VMEM((tiles, 2, tile), jnp.float32),
+            pltpu.VMEM((tiles, 2, tile), jnp.bfloat16),
             pltpu.VMEM((LANES, LANES), jnp.float32),
             pltpu.VMEM((LANES, LANES), jnp.float32),
             pltpu.VMEM((8, LANES), jnp.int32),
@@ -565,7 +568,7 @@
             pltpu.SemaphoreType.DMA((slab_total,)),
             pltpu.SemaphoreType.DMA((slab_total,)),
             pltpu.SemaphoreType.DMA,
-            pltpu.SemaphoreType.DMA(maps.shape[:2]),
+            pltpu.SemaphoreType.DMA((coil_total, x_own // x_here)),
             pltpu.SemaphoreType.DMA((slab_total,)),
             pltpu.SemaphoreType.DMA,
         ],

time: 109 us -> 109 us (level); the launches traced: 109 us -> 108 us
    pallas_call x1, Pallas kernels: 54.5 us -> 56.8 us  [per_device(): pl.pallas_call(functools.partial(grid_kernel, coils, unroll, planes, freq...]
    pallas_call x1, Pallas kernels: 22.2 us -> 20 us  [per_device(): pl.pallas_call(image_kernel, in_specs=[memory] * 4, out_specs=memory, out...]
    pallas_call x1, Pallas kernels: 28.2 us -> 26.7 us  [per_device(): pl.pallas_call(functools.partial(add_kernel, per), grid_spec=pltpu.Prefet...]
where the time goes in v7:
time: 109 us; the launch traced here: 108 us
  Pallas kernels  104 us (95%)
  local copies, waits for them, and re-layouts  4.14 us (4%)
    pallas_call x1, Pallas kernels, per_device(): pl.pallas_call(functools.partial(grid_kernel, coils, unroll, planes, freq...  56.8 us
    pallas_call x1, Pallas kernels, per_device(): pl.pallas_call(functools.partial(add_kernel, per), grid_spec=pltpu.Prefet...  26.7 us
    pallas_call x1, Pallas kernels, per_device(): pl.pallas_call(image_kernel, in_specs=[memory] * 4, out_specs=memory, out...  20 us
    unnamed x2, local copies, waits for them, and re-layouts  4.14 us

profile of v7, /device:TPU:0, one launch (start us, length us, event | category | flops | bytes accessed | tf_op | source)
XLA Modules:
  0.0 107.7 jit_solution(12238642079711181912)
XLA Ops:
  0.0 2.5 %copy.10 = bf16[8,32,4,512]{3,1,2,0:T(8,128)(2,1)} copy(bf16[8,32,4,512]{3,2,1,0:T(4,128)(2,1)} %param.14) | data formatting | bytes 2097152 | tf_op args[5]
  2.5 56.8 %grid_x.1 = (bf16[8,4,8,2048]{3,2,1,0:T(8,128)(2,1)}, bf16[8,4,2,2048]{3,2,1,0:T(2,128)(2,1)}, s32[8,8,128]{2,1,0:T(8,128)}, bf16[8,2,2,32,512]{4,3,2,1,0:T(8,128)(2,1)}) custom-call(bf16[64,8192]{1,0:T(8,128)(2,1)} %bitcast.8, s32[1,8192]{1,0:T(1,128)} %bitcast.9, s32[1,8192]{1,0:T(1,128)} %bitcast.10, s32[1,8192]{1,0:T(1,128)} %bitcast.11, ...), custom_call_target="tpu_custom_call" | custom-call | tf_op jit(solution)/shard_map/grid_x/pallas_call | solution.py:532
  59.3 26.7 %add_yz.1.rows_ref = bf16[4,256,512]{2,1,0:T(8,128)(2,1)} custom-call(s32[8,8,128]{2,1,0:T(8,128)} %get-tuple-element.9.limit_ref, bf16[8,4,8,2048]{3,2,1,0:T(8,128)(2,1)} %get-tuple-element.10.vals_ref, bf16[8,4,2,2048]{3,2,1,0:T(2,128)(2,1)} %get-tuple-element.11.spot_ref), custom_call_target="tpu_custom_call" | custom-call | tf_op jit(solution)/shard_map/add_yz/pallas_call | solution.py:590
  86.0 20.0 %image_sum.1 = f32[32,4,512]{2,1,0:T(4,128)} custom-call(bf16[4,256,512]{2,1,0:T(8,128)(2,1)} %add_yz.1.rows_ref, bf16[8,2,2,32,512]{4,3,2,1,0:T(8,128)(2,1)} %get-tuple-element.12.map_ref, bf16[512,512]{1,0:T(8,128)(2,1)} %constant.7.clone.ytab_ref, bf16[512,512]{1,0:T(8,128)(2,1)} %constant.8.clone.ztab_ref), custom_call_target="tpu_custom_call" | custom-call | tf_op jit(solution)/shard_map/image_sum/pallas_call | solution.py:610
  106.0 1.7 %copy.12 = f32[32,4,512]{2,1,0:T(4,128)} copy(f32[32,4,512]{2,1,0:T(4,128)} %image_sum.1) | data formatting | bytes 524288

commit v8 on v7

--- a/solution.py
+++ b/solution.py
@@ -77,9 +77,10 @@
 
 
 def permute(values, spots):
-    depth = spots.shape[1]
-    level = lax.broadcasted_iota(jnp.int32, (depth, depth), 0).astype(jnp.float32)
-    hot = jnp.where(level == spots, 1.0, 0.0).astype(jnp.bfloat16)
+    length = spots.shape[1]
+    deep = math.gcd(length, 256)
+    hot = [hot_rows(spots - float(at), deep) for at in range(0, length, deep)]
+    hot = jnp.concatenate(hot, axis=0)
     return lax.dot_general(values, hot, NT, preferred_element_type=jnp.float32)
 
 
@@ -518,7 +519,7 @@
     tile = math.gcd(blocks, 2048)
     tiles = blocks // tile
     chunks = tile // LANES
-    unroll = math.gcd(tile // 16, 16)
+    unroll = math.gcd(tile // 16, 64)
     count = 2 * coils * rows_out
     each = 2 * coils * x_here
 

time: 109 us -> 104 us (0.954); the launches traced: 108 us -> 105 us
  Pallas kernels: 104 us -> 101 us
    pallas_call x1, Pallas kernels: 56.8 us -> 51.5 us  [per_device(): pl.pallas_call(functools.partial(grid_kernel, coils, unroll, planes, freq...]
    pallas_call x1, Pallas kernels: 20 us -> 21.7 us  [per_device(): pl.pallas_call(image_kernel, in_specs=[memory] * 4, out_specs=memory, out...]
where the time goes in v8:
time: 104 us; the launch traced here: 105 us
  Pallas kernels  101 us (97%)
  local copies, waits for them, and re-layouts  4.14 us (4%)
    pallas_call x1, Pallas kernels, per_device(): pl.pallas_call(functools.partial(grid_kernel, coils, unroll, planes, freq...  51.5 us
    pallas_call x1, Pallas kernels, per_device(): pl.pallas_call(functools.partial(add_kernel, per), grid_spec=pltpu.Prefet...  27.5 us
    pallas_call x1, Pallas kernels, per_device(): pl.pallas_call(image_kernel, in_specs=[memory] * 4, out_specs=memory, out...  21.7 us
    unnamed x2, local copies, waits for them, and re-layouts  4.14 us

profile of v8, /device:TPU:0, one launch (start us, length us, event | category | flops | bytes accessed | tf_op | source)
XLA Modules:
  0.0 104.9 jit_solution(5110391994277848859)
XLA Ops:
  0.0 2.5 %copy.10 = bf16[8,32,4,512]{3,1,2,0:T(8,128)(2,1)} copy(bf16[8,32,4,512]{3,2,1,0:T(4,128)(2,1)} %param.14) | data formatting | bytes 2097152 | tf_op args[5]
  2.5 51.5 %grid_x.1 = (bf16[8,4,8,2048]{3,2,1,0:T(8,128)(2,1)}, bf16[8,4,2,2048]{3,2,1,0:T(2,128)(2,1)}, s32[8,8,128]{2,1,0:T(8,128)}, bf16[8,2,2,32,512]{4,3,2,1,0:T(8,128)(2,1)}) custom-call(bf16[64,8192]{1,0:T(8,128)(2,1)} %bitcast.8, s32[1,8192]{1,0:T(1,128)} %bitcast.9, s32[1,8192]{1,0:T(1,128)} %bitcast.10, s32[1,8192]{1,0:T(1,128)} %bitcast.11, ...), custom_call_target="tpu_custom_call" | custom-call | tf_op jit(solution)/shard_map/grid_x/pallas_call | solution.py:533
  54.0 27.5 %add_yz.1.rows_ref = bf16[4,256,512]{2,1,0:T(8,128)(2,1)} custom-call(s32[8,8,128]{2,1,0:T(8,128)} %get-tuple-element.9.limit_ref, bf16[8,4,8,2048]{3,2,1,0:T(8,128)(2,1)} %get-tuple-element.10.vals_ref, bf16[8,4,2,2048]{3,2,1,0:T(2,128)(2,1)} %get-tuple-element.11.spot_ref), custom_call_target="tpu_custom_call" | custom-call | tf_op jit(solution)/shard_map/add_yz/pallas_call | solution.py:591
  81.5 21.7 %image_sum.1 = f32[32,4,512]{2,1,0:T(4,128)} custom-call(bf16[4,256,512]{2,1,0:T(8,128)(2,1)} %add_yz.1.rows_ref, bf16[8,2,2,32,512]{4,3,2,1,0:T(8,128)(2,1)} %get-tuple-element.12.map_ref, bf16[512,512]{1,0:T(8,128)(2,1)} %constant.7.clone.ytab_ref, bf16[512,512]{1,0:T(8,128)(2,1)} %constant.8.clone.ztab_ref), custom_call_target="tpu_custom_call" | custom-call | tf_op jit(solution)/shard_map/image_sum/pallas_call | solution.py:611
  103.3 1.7 %copy.12 = f32[32,4,512]{2,1,0:T(4,128)} copy(f32[32,4,512]{2,1,0:T(4,128)} %image_sum.1) | data formatting | bytes 524288

commit v9 on v8

--- a/solution.py
+++ b/solution.py
@@ -201,7 +201,7 @@
         live = lax.broadcasted_iota(jnp.int32, (CELLS, LANES), 0) < count_ref[:, cut]
         place = jnp.where(live, pos_ref[:, cut].astype(jnp.float32), DEAD)
         both = jnp.concatenate([place, pltpu.roll(place, LANES - 8, 1)], axis=0)
-        flat[cut, :] = both.T
+        flat[cut, :] = both.astype(jnp.bfloat16).T
 
     segments = KX // CELLS
     kz = slab_ref[...] * planes + block_ref[...] // (segments * freq)
@@ -229,7 +229,7 @@
                 )
                 halves = [jnp.where(own[half], placed_here, 0.0) for half in range(2)]
                 left.append(jnp.concatenate(halves, axis=1).astype(jnp.bfloat16))
-        place = flat[pl.ds(pl.multiple_of(g * 16, 16), 8), :] * 0.125
+        place = flat[at, :].astype(jnp.float32)[:8] * 0.125
         for r in range(CLASSES):
             offset = place - ((r + 0.5) * 0.125 - 0.5)
             seat = jnp.floor(offset)
@@ -427,21 +427,23 @@
 
 
 def image_kernel(
-    rows_ref, map_ref, ytab_ref, ztab_ref, out_ref, ready, near, far,
+    rows_ref, map_ref, ytab_ref, ztab_ref, out_ref, ready, near, far, sums,
     near_out, near_in, far_out, far_in,
 ):
     wide, slabs, planes, _ = ready.shape
     coils = rows_ref.shape[0] // wide
-    deals, shares = far.shape[0], far.shape[1]
+    deals, shares = far.shape[1], far.shape[2]
     depth, freq = rows_ref.shape[1], rows_ref.shape[2] // 2
     slab, coil = lax.axis_index("slab"), lax.axis_index("coil")
     barrier = pltpu.get_barrier_semaphore()
     for hop in range(1, slabs):
         peer = {"slab": lax.rem(slab + hop, slabs)}
         pl.semaphore_signal(barrier, 1, device_id=peer, device_id_type=MESH)
-    for hop in range(1, deals):
-        peer = {"coil": lax.rem(coil + hop, deals)}
-        pl.semaphore_signal(barrier, 1, device_id=peer, device_id_type=MESH)
+    for way in range(2):
+        @pl.when(coil != (0 if way else deals - 1))
+        def _():
+            peer = {"coil": coil + 1 - 2 * way}
+            pl.semaphore_signal(barrier, 1, device_id=peer, device_id_type=MESH)
 
     def near_copy(x, hop):
         peer = lax.rem(slab + hop, slabs)
@@ -450,13 +452,43 @@
             device_id={"slab": peer}, device_id_type=MESH,
         )
 
-    def far_copy(x, source, hop):
-        share = lax.rem(source, shares)
+    def line_copy(way, deal, share, x):
+        spot = (way, deal, share, x)
         return pltpu.make_async_remote_copy(
-            near.at[x, source], far.at[hop, share, x],
-            far_out.at[hop, share, x], far_in.at[hop, share, x],
-            device_id={"coil": lax.rem(coil + hop, deals)}, device_id_type=MESH,
-        )
+            sums.at[spot], far.at[spot], far_out.at[spot], far_in.at[spot],
+            device_id={"coil": coil + 1 - 2 * way}, device_id_type=MESH,
+        )
+
+    def own_part(deal, share, x):
+        source = deal * shares + share
+        hop = lax.rem(slab + slabs - source, slabs)
+
+        @pl.when(hop > 0)
+        def _():
+            near_copy(x, hop).wait_recv()
+
+        return near[x, source].astype(jnp.float32)
+
+    def pass_on(way):
+        last = deals - 1 if way else 0
+        goals = range(deals - 1) if way else range(deals - 1, 0, -1)
+        for deal in goals:
+            ahead = coil > deal if way else coil < deal
+
+            @pl.when(ahead)
+            def _():
+                for x in range(wide):
+                    for share in range(shares):
+                        sums[way, deal, share, x] = own_part(deal, share, x).astype(jnp.bfloat16)
+
+                        @pl.when(coil != last)
+                        def _():
+                            line_copy(way, deal, share, x).wait_recv()
+                            both = near[x, deal * shares + share].astype(jnp.float32)
+                            both = both + far[way, deal, share, x].astype(jnp.float32)
+                            sums[way, deal, share, x] = both.astype(jnp.bfloat16)
+
+                        line_copy(way, deal, share, x).start()
 
     for x in range(wide):
         real = imag = 0.0
@@ -476,34 +508,44 @@
         ready[x] = both.reshape(slabs, planes, 2 * freq)
         near[x, pl.ds(slab, 1)] = ready[x, pl.ds(slab, 1)]
         if x == 0:
-            pl.semaphore_wait(barrier, slabs - 1 + deals - 1)
+            ends = (coil == 0).astype(jnp.int32) + (coil == deals - 1).astype(jnp.int32)
+            pl.semaphore_wait(barrier, slabs + 1 - ends)
         for hop in range(1, slabs):
             near_copy(x, hop).start()
 
-    for x in range(wide):
-        for hop in range(slabs):
-            source = lax.rem(slab + slabs - hop, slabs)
-            if hop > 0:
-                near_copy(x, hop).wait_recv()
-            leap = lax.rem(source // shares + deals - coil, deals)
-
-            @pl.when(leap > 0)
-            def _():
-                far_copy(x, source, leap).start()
-
-    for x in range(wide):
-        for share in range(shares):
-            value = near[x, coil * shares + share].astype(jnp.float32)
-            for hop in range(1, deals):
-                far_copy(x, share, hop).wait_recv()
-                value = value + far[hop, share, x].astype(jnp.float32)
-            out_ref[:, share * wide + x, :] = value
+    @pl.when(coil < deals // 2)
+    def _():
+        pass_on(0)
+        pass_on(1)
+
+    @pl.when(coil >= deals // 2)
+    def _():
+        pass_on(1)
+        pass_on(0)
+
+    for deal in range(deals):
+        @pl.when(coil == deal)
+        def _():
+            for x in range(wide):
+                for share in range(shares):
+                    value = own_part(deal, share, x)
+                    for way in range(2):
+                        if deal != (deals - 1 if way else 0):
+                            line_copy(way, deal, share, x).wait_recv()
+                            value = value + far[way, deal, share, x].astype(jnp.float32)
+                    out_ref[:, share * wide + x, :] = value
+
     for x in range(wide):
         for hop in range(1, slabs):
             near_copy(x, hop).wait_send()
         for share in range(shares):
-            for hop in range(1, deals):
-                far_copy(x, share, hop).wait_send()
+            for way in range(2):
+                for deal in range(deals):
+                    ahead = coil > deal if way else coil < deal
+
+                    @pl.when(ahead)
+                    def _():
+                        line_copy(way, deal, share, x).wait_send()
 
 
 def per_device(samples, sample_pos, block_count, grid_block, block_slab, sensitivity):
@@ -550,7 +592,7 @@
             jax.ShapeDtypeStruct((slab_total, coils) + maps.shape[3:], jnp.bfloat16),
         ],
         scratch_shapes=[
-            pltpu.VMEM((tile, LANES), jnp.float32),
+            pltpu.VMEM((tile, LANES), jnp.bfloat16),
             pltpu.VMEM((tile, 2 * coils * LANES), jnp.bfloat16),
             pltpu.VMEM((unroll, CLASSES, 8, LANES), jnp.float32),
             pltpu.VMEM((unroll, CLASSES, 8, LANES), jnp.float32),
@@ -616,11 +658,12 @@
         scratch_shapes=[
             pltpu.VMEM((x_here, slab_total, planes, 2 * freq), jnp.bfloat16),
             pltpu.VMEM((x_here, slab_total, planes, 2 * freq), jnp.bfloat16),
-            pltpu.VMEM((coil_total, shares, x_here, planes, 2 * freq), jnp.bfloat16),
+            pltpu.VMEM((2, coil_total, shares, x_here, planes, 2 * freq), jnp.bfloat16),
+            pltpu.VMEM((2, coil_total, shares, x_here, planes, 2 * freq), jnp.bfloat16),
             pltpu.SemaphoreType.DMA((x_here, slab_total)),
             pltpu.SemaphoreType.DMA((x_here, slab_total)),
-            pltpu.SemaphoreType.DMA((coil_total, shares, x_here)),
-            pltpu.SemaphoreType.DMA((coil_total, shares, x_here)),
+            pltpu.SemaphoreType.DMA((2, coil_total, shares, x_here)),
+            pltpu.SemaphoreType.DMA((2, coil_total, shares, x_here)),
         ],
         compiler_params=pltpu.CompilerParams(collective_id=1, has_side_effects=True),
         name="image_sum",

time: 104 us -> 105 us (level); the launches traced: 105 us -> 105 us
  no operation moved by 1% of the time
where the time goes in v9:
time: 105 us
  Pallas kernels  100 us (95%)
  local copies, waits for them, and re-layouts  4.14 us (4%)
    pallas_call x1, Pallas kernels, per_device(): pl.pallas_call(functools.partial(grid_kernel, coils, unroll, planes, freq...  51 us
    pallas_call x1, Pallas kernels, per_device(): pl.pallas_call(functools.partial(add_kernel, per), grid_spec=pltpu.Prefet...  26.7 us
    pallas_call x1, Pallas kernels, per_device(): pl.pallas_call(image_kernel, in_specs=[memory] * 4, out_specs=memory, out...  22.7 us
    unnamed x2, local copies, waits for them, and re-layouts  4.14 us

profile of v9, /device:TPU:0, one launch (start us, length us, event | category | flops | bytes accessed | tf_op | source)
XLA Modules:
  0.0 104.6 jit_solution(6703989533010681696)
XLA Ops:
  0.0 2.5 %copy.10 = bf16[8,32,4,512]{3,1,2,0:T(8,128)(2,1)} copy(bf16[8,32,4,512]{3,2,1,0:T(4,128)(2,1)} %param.14) | data formatting | bytes 2097152 | tf_op args[5]
  2.5 51.0 %grid_x.1 = (bf16[8,4,8,2048]{3,2,1,0:T(8,128)(2,1)}, bf16[8,4,2,2048]{3,2,1,0:T(2,128)(2,1)}, s32[8,8,128]{2,1,0:T(8,128)}, bf16[8,2,2,32,512]{4,3,2,1,0:T(8,128)(2,1)}) custom-call(bf16[64,8192]{1,0:T(8,128)(2,1)} %bitcast.8, s32[1,8192]{1,0:T(1,128)} %bitcast.9, s32[1,8192]{1,0:T(1,128)} %bitcast.10, s32[1,8192]{1,0:T(1,128)} %bitcast.11, ...), custom_call_target="tpu_custom_call" | custom-call | tf_op jit(solution)/shard_map/grid_x/pallas_call | solution.py:575
  53.5 26.7 %add_yz.1.rows_ref = bf16[4,256,512]{2,1,0:T(8,128)(2,1)} custom-call(s32[8,8,128]{2,1,0:T(8,128)} %get-tuple-element.9.limit_ref, bf16[8,4,8,2048]{3,2,1,0:T(8,128)(2,1)} %get-tuple-element.10.vals_ref, bf16[8,4,2,2048]{3,2,1,0:T(2,128)(2,1)} %get-tuple-element.11.spot_ref), custom_call_target="tpu_custom_call" | custom-call | tf_op jit(solution)/shard_map/add_yz/pallas_call | solution.py:633
  80.2 22.7 %image_sum.1 = f32[32,4,512]{2,1,0:T(4,128)} custom-call(bf16[4,256,512]{2,1,0:T(8,128)(2,1)} %add_yz.1.rows_ref, bf16[8,2,2,32,512]{4,3,2,1,0:T(8,128)(2,1)} %get-tuple-element.12.map_ref, bf16[512,512]{1,0:T(8,128)(2,1)} %constant.7.clone.ytab_ref, bf16[512,512]{1,0:T(8,128)(2,1)} %constant.8.clone.ztab_ref), custom_call_target="tpu_custom_call" | custom-call | tf_op jit(solution)/shard_map/image_sum/pallas_call | solution.py:653
  102.9 1.7 %copy.12 = f32[32,4,512]{2,1,0:T(4,128)} copy(f32[32,4,512]{2,1,0:T(4,128)} %image_sum.1) | data formatting | bytes 524288

commit v10 on v9

--- a/solution.py
+++ b/solution.py
@@ -469,7 +469,7 @@
 
         return near[x, source].astype(jnp.float32)
 
-    def pass_on(way):
+    def pass_on(way, x):
         last = deals - 1 if way else 0
         goals = range(deals - 1) if way else range(deals - 1, 0, -1)
         for deal in goals:
@@ -477,18 +477,17 @@
 
             @pl.when(ahead)
             def _():
-                for x in range(wide):
-                    for share in range(shares):
-                        sums[way, deal, share, x] = own_part(deal, share, x).astype(jnp.bfloat16)
-
-                        @pl.when(coil != last)
-                        def _():
-                            line_copy(way, deal, share, x).wait_recv()
-                            both = near[x, deal * shares + share].astype(jnp.float32)
-                            both = both + far[way, deal, share, x].astype(jnp.float32)
-                            sums[way, deal, share, x] = both.astype(jnp.bfloat16)
-
-                        line_copy(way, deal, share, x).start()
+                for share in range(shares):
+                    sums[way, deal, share, x] = own_part(deal, share, x).astype(jnp.bfloat16)
+
+                    @pl.when(coil != last)
+                    def _():
+                        line_copy(way, deal, share, x).wait_recv()
+                        both = near[x, deal * shares + share].astype(jnp.float32)
+                        both = both + far[way, deal, share, x].astype(jnp.float32)
+                        sums[way, deal, share, x] = both.astype(jnp.bfloat16)
+
+                    line_copy(way, deal, share, x).start()
 
     for x in range(wide):
         real = imag = 0.0
@@ -515,13 +514,15 @@
 
     @pl.when(coil < deals // 2)
     def _():
-        pass_on(0)
-        pass_on(1)
+        for x in range(wide):
+            pass_on(0, x)
+            pass_on(1, x)
 
     @pl.when(coil >= deals // 2)
     def _():
-        pass_on(1)
-        pass_on(0)
+        for x in range(wide):
+            pass_on(1, x)
+            pass_on(0, x)
 
     for deal in range(deals):
         @pl.when(coil == deal)

time: 105 us -> 107 us (1.019)
  no operation moved by 1% of the time
where the time goes in v10:
time: 107 us; the launch traced here: 106 us
  Pallas kernels  101 us (94%)
  local copies, waits for them, and re-layouts  4.14 us (4%)
    pallas_call x1, Pallas kernels, per_device(): pl.pallas_call(functools.partial(grid_kernel, coils, unroll, planes, freq...  51 us
    pallas_call x1, Pallas kernels, per_device(): pl.pallas_call(functools.partial(add_kernel, per), grid_spec=pltpu.Prefet...  27 us
    pallas_call x1, Pallas kernels, per_device(): pl.pallas_call(image_kernel, in_specs=[memory] * 4, out_specs=memory, out...  23.4 us
    unnamed x2, local copies, waits for them, and re-layouts  4.14 us

profile of v10, /device:TPU:0, one launch (start us, length us, event | category | flops | bytes accessed | tf_op | source)
XLA Modules:
  0.0 105.6 jit_solution(11743144949629503885)
XLA Ops:
  0.0 2.5 %copy.10 = bf16[8,32,4,512]{3,1,2,0:T(8,128)(2,1)} copy(bf16[8,32,4,512]{3,2,1,0:T(4,128)(2,1)} %param.14) | data formatting | bytes 2097152 | tf_op args[5]
  2.5 51.0 %grid_x.1 = (bf16[8,4,8,2048]{3,2,1,0:T(8,128)(2,1)}, bf16[8,4,2,2048]{3,2,1,0:T(2,128)(2,1)}, s32[8,8,128]{2,1,0:T(8,128)}, bf16[8,2,2,32,512]{4,3,2,1,0:T(8,128)(2,1)}) custom-call(bf16[64,8192]{1,0:T(8,128)(2,1)} %bitcast.8, s32[1,8192]{1,0:T(1,128)} %bitcast.9, s32[1,8192]{1,0:T(1,128)} %bitcast.10, s32[1,8192]{1,0:T(1,128)} %bitcast.11, ...), custom_call_target="tpu_custom_call" | custom-call | tf_op jit(solution)/shard_map/grid_x/pallas_call | solution.py:576
  53.5 27.0 %add_yz.1.rows_ref = bf16[4,256,512]{2,1,0:T(8,128)(2,1)} custom-call(s32[8,8,128]{2,1,0:T(8,128)} %get-tuple-element.9.limit_ref, bf16[8,4,8,2048]{3,2,1,0:T(8,128)(2,1)} %get-tuple-element.10.vals_ref, bf16[8,4,2,2048]{3,2,1,0:T(2,128)(2,1)} %get-tuple-element.11.spot_ref), custom_call_target="tpu_custom_call" | custom-call | tf_op jit(solution)/shard_map/add_yz/pallas_call | solution.py:634
  80.5 23.4 %image_sum.1 = f32[32,4,512]{2,1,0:T(4,128)} custom-call(bf16[4,256,512]{2,1,0:T(8,128)(2,1)} %add_yz.1.rows_ref, bf16[8,2,2,32,512]{4,3,2,1,0:T(8,128)(2,1)} %get-tuple-element.12.map_ref, bf16[512,512]{1,0:T(8,128)(2,1)} %constant.7.clone.ytab_ref, bf16[512,512]{1,0:T(8,128)(2,1)} %constant.8.clone.ztab_ref), custom_call_target="tpu_custom_call" | custom-call | tf_op jit(solution)/shard_map/image_sum/pallas_call | solution.py:654
  103.9 1.7 %copy.12 = f32[32,4,512]{2,1,0:T(4,128)} copy(f32[32,4,512]{2,1,0:T(4,128)} %image_sum.1) | data formatting | bytes 524288
